TPU v7x, 256 devices: a whole 4x4x8 slice. The times are simulated.
256 devices in a mesh: out: 32 (over x, z_hi, core), in: 8 (over z_lo, y).
Axes of the slice: x: 4, y: 4, z: 8 (z_hi: 4, z_lo: 2; z = z_hi * 2 + z_lo), core: 2. Of those that a mesh axis runs over, the one named last changes fastest.
Arguments:
- slopes: bfloat16 [256, 163840], P('out', 'in'), may hold values from -6 to 6
- cols_first: int32 [128, 64], P(None, 'in'), may hold values from 0 to 79
- count_first: int32 [128, 8], P('out', 'in'), may hold values from 1 to 8
- weight_first: bfloat16 [128, 64, 256, 256], P('out', 'in'), may hold values from -0.0625 to 0.0625
- bias_first: float32 [32768], P(('out', 'in')), may hold values from -3 to 3
- cols_second: int32 [128, 32], P('out', 'in'), may hold values from 0 to 15
- count_second: int32 [128, 8], P('out', 'in'), may hold values from 1 to 4
- weight_second: bfloat16 [128, 32, 256, 256], P('out', 'in'), may hold values from -0.09375 to 0.09375
- bias_second: float32 [32768], P(('out', 'in')), may hold values from -3 to 3
- cotangent: bfloat16 [256, 32768], P(None, ('out', 'in')), may hold values from -6 to 6
Outputs:
- estimate: bfloat16 [256, 32768], P(None, ('out', 'in'))
- grad_first: bfloat16 [128, 64, 256, 256], P('out', 'in')
- grad_second: bfloat16 [128, 32, 256, 256], P('out', 'in')
Inputs may be any that keep to these rules, and one draw needn't show every extreme that they name: `cols_first`: A local block index within the range of slopes of the slot's in index. `count_first`: slots of a block row at or after this count, within one in range, are not used. `cols_second`: A local block index within the range of reordered hidden units of the slot's in index. `count_second`: slots of a block row at or after this count, within one in range, are not used.
All inputs are finite; a program needn't handle non-finite values.
Results may differ from a plain program's by a relative error of at most 0.025.
Values may be sent and summed in bfloat16 or wider, within the bound.
No kernel may reach another device: no remote copies, remote signals or barrier semaphores. Data moves between devices by JAX's collectives and lax.ppermute only.
A program may use at most 128 MiB of HBM per device.

v0:
```python
import jax
import jax.numpy as jnp
from jax import lax
from jax.sharding import PartitionSpec as P

BLK = 256
KD1 = 8
KD2 = 4


def shards(
    slopes,
    cols_first,
    count_first,
    weight_first,
    bias_first,
    cols_second,
    count_second,
    weight_second,
    bias_second,
    cotangent,
):
    rows = weight_first.shape[0]
    live_first = jnp.arange(KD1, dtype=jnp.int32)[None, :] < count_first
    live_second = jnp.arange(KD2, dtype=jnp.int32)[None, :] < count_second
    masked_first = weight_first * live_first.astype(jnp.bfloat16)[:, :, None, None]
    masked_second = weight_second * live_second.astype(jnp.bfloat16)[:, :, None, None]
    gathered = lax.all_gather(slopes, "out", axis=0, tiled=True)
    frames = gathered.shape[0]
    slope_blocks = gathered.reshape(frames, -1, BLK)
    own_cols = lax.dynamic_slice_in_dim(cols_first, lax.axis_index("out") * rows, rows, 0)
    panels_first = jnp.take(slope_blocks, own_cols.reshape(-1), axis=1).reshape(
        frames, rows, KD1, BLK
    )
    partial_first = jnp.einsum(
        "frkb,rkbo->fro", panels_first, masked_first, preferred_element_type=jnp.float32
    ).reshape(frames, rows * BLK)
    summed_first = lax.psum_scatter(partial_first, "in", scatter_dimension=1, tiled=True)
    hidden_first = jnp.tanh(summed_first + bias_first[None, :]).astype(jnp.bfloat16)
    second_input = lax.all_gather(hidden_first, "out", axis=1, tiled=True)
    hidden_blocks = second_input.reshape(frames, -1, BLK)
    panels_second = jnp.take(hidden_blocks, cols_second.reshape(-1), axis=1).reshape(
        frames, rows, KD2, BLK
    )
    partial_second = jnp.einsum(
        "frkb,rkbo->fro", panels_second, masked_second, preferred_element_type=jnp.float32
    ).reshape(frames, rows * BLK)
    summed_second = lax.psum_scatter(partial_second, "in", scatter_dimension=1, tiled=True)
    estimate = jnp.tanh(summed_second + bias_second[None, :]).astype(jnp.bfloat16)
    est32 = estimate.astype(jnp.float32)
    delta_second = (cotangent.astype(jnp.float32) * (1.0 - est32 * est32)).astype(jnp.bfloat16)
    rows_second = lax.all_gather(delta_second, "in", axis=1, tiled=True).reshape(frames, rows, BLK)
    grad_second = jnp.einsum(
        "frkb,fro->rkbo", panels_second, rows_second, preferred_element_type=jnp.float32
    )
    grad_second = (grad_second * live_second.astype(jnp.float32)[:, :, None, None]).astype(
        jnp.bfloat16
    )
    adjoint = jnp.einsum(
        "fro,rkbo->frkb", rows_second, masked_second, preferred_element_type=jnp.float32
    ).reshape(frames, rows * KD2, BLK)
    selector = (
        cols_second.reshape(-1)[:, None]
        == jnp.arange(hidden_blocks.shape[1], dtype=jnp.int32)[None, :]
    ).astype(jnp.float32)
    spread = jnp.einsum("fjb,jc->fcb", adjoint, selector, precision=lax.Precision.HIGHEST).reshape(
        frames, -1
    )
    back_first = lax.psum_scatter(
        spread.astype(jnp.bfloat16), "out", scatter_dimension=1, tiled=True
    ).astype(jnp.float32)
    hid32 = hidden_first.astype(jnp.float32)
    delta_first = (back_first * (1.0 - hid32 * hid32)).astype(jnp.bfloat16)
    rows_first = lax.all_gather(delta_first, "in", axis=1, tiled=True).reshape(frames, rows, BLK)
    grad_first = jnp.einsum(
        "frkb,fro->rkbo", panels_first, rows_first, preferred_element_type=jnp.float32
    )
    grad_first = (grad_first * live_first.astype(jnp.float32)[:, :, None, None]).astype(
        jnp.bfloat16
    )
    return (estimate, grad_first, grad_second)


def solution(mesh):
    return jax.shard_map(
        shards,
        mesh=mesh,
        in_specs=(
            P("out", "in"),
            P(None, "in"),
            P("out", "in"),
            P("out", "in", None, None),
            P(("out", "in")),
            P("out", "in"),
            P("out", "in"),
            P("out", "in", None, None),
            P(("out", "in")),
            P(None, ("out", "in")),
        ),
        out_specs=(P(None, ("out", "in")), P("out", "in", None, None), P("out", "in", None, None)),
        check_vma=False,
    )
```

profile of v0, /device:TPU:1, one launch (start us, length us, event | category | flops | bytes accessed | tf_op | source)
XLA Modules:
  0.0 469.4 jit_solution(1294169107600888628)
XLA Ops:
  7.2 0.0 all-gather.3.cloned.1.call-start
  7.2 0.7 all-gather.3.cloned.1.call-update
  7.9 0.0 reduce-scatter.4.cloned.1.call-start
  7.9 0.8 compare_and_fusion
  8.7 0.1 copy.57
  8.8 0.1 copy.59
  8.9 0.1 reshape.203
  9.0 0.7 fusion.17
  9.7 94.5 %all-gather.3.cloned.1.call-done = bf16[256,20480]{1,0:T(8,128)(2,1)} async-done(((bf16[8,20480]{1,0:T(8,128)(2,1)}), bf16[256,20480]{1,0:T(8,128)(2,1)}) %all-gather.3.cloned.1.call-update) | async-done | bytes 10485776 | tf_op jit(solution)/shard_map/all_gather | solution.py:28
  104.2 13.8 %copy.58 = bf16[256,20480]{0,1:T(8,128)(2,1)} copy(bf16[256,20480]{1,0:T(8,128)(2,1)} %all-gather.3.cloned.1.call-done) | data formatting | bytes 20971520 | tf_op jit(solution)/shard_map/all_gather | solution.py:28
  118.0 14.4 %copy.60 = bf16[256,80,256]{2,0,1:T(8,128)(2,1)} copy(bf16[256,80,256]{0,2,1:T(8,128)(2,1)} %bitcast.50) | data formatting | bytes 20971520 | tf_op jit(solution)/shard_map/reshape | solution.py:30
  132.4 6.8 %gather_fusion = bf16[32,256,256]{2,1,0:T(8,128)(2,1)} fusion(bf16[256,80,256]{2,0,1:T(8,128)(2,1)} %copy.60, s32[1024]{0:T(1024)S(1)} %pad_clamp_fusion.1), kind=kCustom, calls=%fused_computation | custom fusion | bytes 8388736 | tf_op jit(solution)/shard_map/jit(_take)/gather | solution.py:32
  139.2 6.2 %copy.61 = bf16[256,4,8,256]{0,3,2,1:T(8,128)(2,1)} copy(bf16[256,4,8,256]{3,0,2,1:T(8,128)(2,1)} %bitcast.52) | data formatting | bytes 8388608 | tf_op jit(solution)/shard_map/jit(_take)/gather | solution.py:32
  145.4 6.2 %fusion = f32[4,256,256,1]{2,1,3,0:T(8,128)} fusion(bf16[4,8,256,256]{3,2,1,0:T(8,128)(2,1)} %param.13, bf16[256,4,8,256]{0,3,2,1:T(8,128)(2,1)} %copy.61, pred[4,8]{1,0:T(4,128)(4,1)S(1)} %copy.57, bf16[4,8]{1,0:T(4,128)(2,1)S(1)} %get-tuple-element.19), kind=kOutput, calls=%fused_computation.4 | convolution fusion | flops 1077936128 | bytes 9437280 | tf_op jit(solution)/shard_map/frkb,rkbo->fro/dot_general | solution.py:35
  151.7 0.0 reduce-scatter.4.cloned.1.call-update
  151.7 0.0 all-gather.5.cloned.1.call-start
  151.7 34.7 %reduce-scatter.4.cloned.1.call-done = f32[256,128]{0,1:T(8,128)} async-done(((f32[256,1024]{0,1:T(8,128)}), f32[256,128]{0,1:T(8,128)}) %reduce-scatter.4.cloned.1.call-update) | async-done | bytes 131088 | tf_op jit(solution)/shard_map/reduce_scatter | solution.py:38
  186.4 0.0 copy-done.4
  186.4 1.6 tanh_convert_fusion.1
  188.0 0.0 all-gather.5.cloned.1.call-update
  188.0 0.0 reduce-scatter.6.cloned.1.call-start
  188.1 0.0 copy-done.3
  188.1 0.1 reshape.206
  188.2 0.0 copy-done.6
  188.2 0.1 fusion.19
  188.3 60.0 %all-gather.5.cloned.1.call-done = bf16[256,4096]{0,1:T(8,128)(2,1)} async-done(((bf16[256,128]{0,1:T(8,128)(2,1)}), bf16[256,4096]{0,1:T(8,128)(2,1)}) %all-gather.5.cloned.1.call-update) | async-done | bytes 2097168 | tf_op jit(solution)/shard_map/all_gather | solution.py:40
  248.3 2.8 copy.64
  251.2 2.0 gather_fusion.1
  253.2 4.3 copy.65
  257.5 3.6 fusion.8
  261.1 0.0 reduce-scatter.6.cloned.1.call-update
  261.1 0.0 reduce-scatter.8.cloned.1.call-start
  261.2 0.1 reshape.208
  261.3 0.1 copy.68
  261.4 33.4 %reduce-scatter.6.cloned.1.call-done = f32[256,128]{0,1:T(8,128)} async-done(((f32[256,1024]{0,1:T(8,128)}), f32[256,128]{0,1:T(8,128)}) %reduce-scatter.6.cloned.1.call-update) | async-done | bytes 131088 | tf_op jit(solution)/shard_map/reduce_scatter | solution.py:48
  294.8 1.0 multiply_convert_fusion.3
  295.8 22.8 %all_gather.14 = bf16[256,1024]{0,1:T(8,128)(2,1)S(1)} all-gather(bf16[256,128]{0,1:T(8,128)(2,1)S(1)} %get-tuple-element.12), channel_id=1, replica_groups=mesh['out'=32,'in'=8] {'in'}, dimensions={1}, use_global_device_ids=true | all-gather | bytes 589824 | tf_op jit(solution)/shard_map/all_gather | solution.py:52
  318.5 2.8 fusion.6
  321.3 5.5 %copy.70 = f32[256,16,256]{2,1,0:T(8,128)} copy(f32[256,16,256]{0,2,1:T(8,128)} %bitcast.51) | data formatting | bytes 8388608 | tf_op jit(solution)/shard_map/reshape | solution.py:61
  326.8 4.3 convert_bitcast_fusion
  331.2 2.7 copy.86
  333.9 0.0 reduce-scatter.8.cloned.1.call-update
  333.9 0.7 copy.74
  334.7 3.7 multiply_convert_fusion.1
  338.3 95.1 %reduce-scatter.8.cloned.1.call-done = bf16[256,128]{0,1:T(8,128)(2,1)} async-done(((bf16[256,4096]{0,1:T(8,128)(2,1)}), bf16[256,128]{0,1:T(8,128)(2,1)}) %reduce-scatter.8.cloned.1.call-update) | async-done | bytes 65552 | tf_op jit(solution)/shard_map/reduce_scatter | solution.py:69
  433.4 0.9 multiply_convert_fusion.2
  434.4 23.0 %all_gather.15 = bf16[256,1024]{0,1:T(8,128)(2,1)S(1)} all-gather(bf16[256,128]{0,1:T(8,128)(2,1)S(1)} %multiply_convert_fusion.2), channel_id=1, replica_groups=mesh['out'=32,'in'=8] {'in'}, dimensions={1}, use_global_device_ids=true | all-gather | bytes 589824 | tf_op jit(solution)/shard_map/all_gather | solution.py:74
  457.4 5.5 %multiply_convert_fusion = bf16[4,8,256,256]{3,2,1,0:T(8,128)(2,1)} fusion(f32[4,8]{1,0:T(4,128)S(1)} %get-tuple-element.18, bf16[256,4,256,1]{0,2,3,1:T(8,128)(2,1)S(1)} %bitcast.60, bf16[256,4,8,256]{0,3,2,1:T(8,128)(2,1)} %copy.61, pred[4,8]{1,0:T(4,128)(4,1)S(1)} %copy.57), kind=kOutput, calls=%fused_computation.2 | convolution fusion | flops 1080033280 | bytes 8913056 | tf_op jit(solution)/shard_map/frkb,fro->rkbo/dot_general | solution.py:75
  (15 shorter events, 0.0 us)
Async XLA Ops:
  7.2 97.1 %all-gather.3.cloned.1.call-start = ((), (), s32[]{:S(2)}) async-start(), calls=%async_computation.3 | async-start | bytes 10813440 | tf_op jit(solution)/shard_map/all_gather | solution.py:28
  7.9 178.5 %reduce-scatter.4.cloned.1.call-start = ((), (), s32[]{:S(2)}) async-start(), calls=%async_computation.4 | async-start | bytes 1179648 | tf_op jit(solution)/shard_map/reduce_scatter | solution.py:38
  145.4 41.0 %copy-start.4 = (f32[128]{0:T(128)S(1)}, f32[128]{0:T(128)}, u32[]{:S(2)}) copy-start(f32[128]{0:T(128)} %param.14) | copy-start | bytes 1540
  145.4 42.7 %copy-start.3 = (s32[4,4]{1,0:T(4,128)S(1)}, s32[4,4]{1,0:T(4,128)}, u32[]{:S(2)}) copy-start(s32[4,4]{1,0:T(4,128)} %param.15) | copy-start | bytes 196
  145.4 42.8 %copy-start.6 = (s32[4,1]{0,1:T(1,128)S(1)}, s32[4,1]{0,1:T(1,128)}, u32[]{:S(2)}) copy-start(s32[4,1]{0,1:T(1,128)} %param.16) | copy-start | bytes 52
  151.7 96.6 %all-gather.5.cloned.1.call-start = ((), (), s32[]{:S(2)}) async-start(), calls=%async_computation.5 | async-start | bytes 2162688 | tf_op jit(solution)/shard_map/all_gather | solution.py:40
  188.0 106.7 %reduce-scatter.6.cloned.1.call-start = ((), (), s32[]{:S(2)}) async-start(), calls=%async_computation.6 | async-start | bytes 1179648 | tf_op jit(solution)/shard_map/reduce_scatter | solution.py:48
  253.2 4.3 copy-start
  257.5 3.8 copy-start.2
  257.5 37.2 %copy-start.5 = (f32[128]{0:T(128)S(1)}, f32[128]{0:T(128)}, u32[]{:S(2)}) copy-start(f32[128]{0:T(128)} %param.18) | copy-start | bytes 1540
  261.1 172.3 %reduce-scatter.8.cloned.1.call-start = ((), (), s32[]{:S(2)}) async-start(), calls=%async_computation.7 | async-start | bytes 2162688 | tf_op jit(solution)/shard_map/reduce_scatter | solution.py:69
  333.9 99.5 %copy-start.1 = (f32[256,128]{0,1:T(8,128)S(1)}, f32[256,128]{0,1:T(8,128)}, u32[]{:S(2)}) copy-start(f32[256,128]{0,1:T(8,128)} %reduce-scatter.4.cloned.1.call-done) | copy-start | bytes 393220
Sparse Core Ops, SparseCore 0:
  10.5 93.6 all-gather.2
  151.8 34.5 reduce-scatter.3
  189.5 58.7 all-gather.4
  261.3 33.4 reduce-scatter.5
  334.0 99.3 reduce-scatter.7
where the time goes:
time: 478 us; the launch traced here: 469 us
  waiting for transfers between devices  318 us (67%)
  local copies, waits for them, and re-layouts  59.9 us (13%)
  blocking collectives  45.8 us (10%)
  matrix products  26.1 us (5%)
  between operations  13.9 us (3%)
  other arithmetic  5.16 us (1%)
    reduce_scatter x1, waiting for transfers between devices, shards(): lax.psum_scatter(spread.astype(jnp.bfloat16), 'out', scatter_dimension=1,...  95.1 us
    all_gather x1, waiting for transfers between devices, shards(): gathered = lax.all_gather(slopes, 'out', axis=0, tiled=True)  94.5 us
    all_gather x1, waiting for transfers between devices, shards(): second_input = lax.all_gather(hidden_first, 'out', axis=1, tiled=True)  60 us
    reduce_scatter x1, waiting for transfers between devices, shards(): lax.psum_scatter(partial_first, 'in', scatter_dimension=1, tiled=True)  34.7 us
    reduce_scatter x1, waiting for transfers between devices, shards(): lax.psum_scatter(partial_second, 'in', scatter_dimension=1, tiled=True)  33.4 us
    all_gather x1, blocking collectives, shards(): lax.all_gather(delta_first, 'in', axis=1, tiled=True)  23 us
    all_gather x1, blocking collectives, shards(): lax.all_gather(delta_second, 'in', axis=1, tiled=True)  22.8 us
    reshape x1, local copies, waits for them, and re-layouts, shards(): slope_blocks = gathered.reshape(frames, -1, BLK)  14.4 us
  transfers between devices with their start and end apart: 5, of which 5 were waited for; matrix products, arithmetic and copies ran while one was open for 1% of the time, Pallas kernels for 0%

commit v1 on v0

v1 whole, which is shorter than its diff:
```python
import jax
import jax.numpy as jnp
from jax import lax
from jax.experimental import pallas as pl
from jax.experimental.pallas import tpu as pltpu
from jax.sharding import Mesh
from jax.sharding import PartitionSpec as P

BLK = 256
KD1 = 8
KD2 = 4
SUB = 128
OUT = ("x", "zh", "core")
IN = ("zl", "y")
F32 = jnp.float32
BF16 = jnp.bfloat16


def dot(a, b, dims):
    return lax.dot_general(a, b, (dims, ((), ())), preferred_element_type=F32)


def forward_first(gathered, weight, cols, count):
    frames = gathered.shape[0]
    rows = weight.shape[0]

    def body(cols_ref, count_ref, *refs):
        panels, w_ref, out_ref, acc = refs[:KD1], refs[KD1], refs[KD1 + 1], refs[KD1 + 2]
        r = pl.program_id(0)
        acc[...] = dot(panels[0][...], w_ref[0, 0], ((1,), (0,)))
        for k in range(1, KD1):

            @pl.when(k < count_ref[r])
            def _():
                acc[...] += dot(panels[k][...], w_ref[0, k], ((1,), (0,)))

        out_ref[0] = acc[:, :SUB].astype(BF16)
        out_ref[1] = acc[:, SUB:].astype(BF16)

    return pl.pallas_call(
        body,
        out_shape=jax.ShapeDtypeStruct((rows * BLK // SUB, frames, SUB), BF16),
        grid_spec=pltpu.PrefetchScalarGridSpec(
            num_scalar_prefetch=2,
            grid=(rows,),
            in_specs=[
                pl.BlockSpec((frames, BLK), lambda r, cols, count, k=k: (0, cols[r, k]))
                for k in range(KD1)
            ]
            + [pl.BlockSpec((1, KD1, BLK, BLK), lambda r, cols, count: (r, 0, 0, 0))],
            out_specs=pl.BlockSpec((BLK // SUB, frames, SUB), lambda r, cols, count: (r, 0, 0)),
            scratch_shapes=[pltpu.VMEM((frames, BLK), F32)],
        ),
        name="forward_first",
    )(cols, count, *([gathered] * KD1), weight)


def grad_first_blocks(gathered, delta, cols, count):
    frames = gathered.shape[0]
    rows = cols.shape[0]

    def body(cols_ref, count_ref, *refs):
        panels, d_ref, out_ref = refs[:KD1], refs[KD1], refs[KD1 + 1]
        r = pl.program_id(0)
        d = jnp.concatenate([d_ref[0], d_ref[1]], axis=1)
        for k in range(KD1):

            @pl.when(k < count_ref[r])
            def _():
                out_ref[0, k] = dot(panels[k][...], d, ((0,), (0,))).astype(BF16)

            @pl.when(k >= count_ref[r])
            def _():
                out_ref[0, k] = jnp.zeros((BLK, BLK), BF16)

    return pl.pallas_call(
        body,
        out_shape=jax.ShapeDtypeStruct((rows, KD1, BLK, BLK), BF16),
        grid_spec=pltpu.PrefetchScalarGridSpec(
            num_scalar_prefetch=2,
            grid=(rows,),
            in_specs=[
                pl.BlockSpec((frames, BLK), lambda r, cols, count, k=k: (0, cols[r, k]))
                for k in range(KD1)
            ]
            + [pl.BlockSpec((BLK // SUB, frames, SUB), lambda r, cols, count: (r, 0, 0))],
            out_specs=pl.BlockSpec((1, KD1, BLK, BLK), lambda r, cols, count: (r, 0, 0, 0)),
        ),
        name="grad_first",
    )(cols, count, *([gathered] * KD1), delta)


def forward_second(hidden, weight, cols, count):
    frames = hidden.shape[1]
    rows = weight.shape[0]
    per = BLK // SUB

    def body(cols_ref, count_ref, h_ref, w_ref, out_ref, acc):
        for r in range(rows):
            for k in range(KD2):

                def term(r=r, k=k):
                    c = cols_ref[r, k]
                    block = jnp.concatenate([h_ref[per * c], h_ref[per * c + 1]], axis=1)
                    return dot(block, w_ref[r, k], ((1,), (0,)))

                if k == 0:
                    acc[...] = term()
                else:

                    @pl.when(k < count_ref[r])
                    def _():
                        acc[...] += term()

            out_ref[per * r] = acc[:, :SUB].astype(BF16)
            out_ref[per * r + 1] = acc[:, SUB:].astype(BF16)

    return pl.pallas_call(
        body,
        out_shape=jax.ShapeDtypeStruct((rows * per, frames, SUB), BF16),
        in_specs=[
            pl.BlockSpec(memory_space=pltpu.SMEM),
            pl.BlockSpec(memory_space=pltpu.SMEM),
            pl.BlockSpec(memory_space=pltpu.VMEM),
            pl.BlockSpec(memory_space=pltpu.VMEM),
        ],
        out_specs=pl.BlockSpec(memory_space=pltpu.VMEM),
        scratch_shapes=[pltpu.VMEM((frames, BLK), F32)],
        name="forward_second",
    )(cols, count, hidden, weight)


def adjoint_second(delta, weight, cols, count, blocks):
    frames = delta.shape[1]
    rows = weight.shape[0]
    per = BLK // SUB

    def body(cols_ref, count_ref, d_ref, w_ref, out_ref, acc):
        acc[...] = jnp.zeros(acc.shape, F32)
        for r in range(rows):
            d = jnp.concatenate([d_ref[per * r], d_ref[per * r + 1]], axis=1)
            for k in range(KD2):

                @pl.when(k < count_ref[r])
                def _():
                    c = cols_ref[r, k]
                    acc[c] += dot(d, w_ref[r, k], ((1,), (1,)))

        for c in range(blocks):
            out_ref[per * c] = acc[c, :, :SUB].astype(BF16)
            out_ref[per * c + 1] = acc[c, :, SUB:].astype(BF16)

    return pl.pallas_call(
        body,
        out_shape=jax.ShapeDtypeStruct((blocks * per, frames, SUB), BF16),
        in_specs=[
            pl.BlockSpec(memory_space=pltpu.SMEM),
            pl.BlockSpec(memory_space=pltpu.SMEM),
            pl.BlockSpec(memory_space=pltpu.VMEM),
            pl.BlockSpec(memory_space=pltpu.VMEM),
        ],
        out_specs=pl.BlockSpec(memory_space=pltpu.VMEM),
        scratch_shapes=[pltpu.VMEM((blocks, frames, BLK), F32)],
        name="adjoint_second",
    )(cols, count, delta, weight)


def grad_second_blocks(hidden, delta, cols, count):
    frames = hidden.shape[1]
    rows = cols.shape[0]
    per = BLK // SUB

    def body(cols_ref, count_ref, h_ref, d_ref, out_ref):
        for r in range(rows):
            d = jnp.concatenate([d_ref[per * r], d_ref[per * r + 1]], axis=1)
            for k in range(KD2):

                @pl.when(k < count_ref[r])
                def _():
                    c = cols_ref[r, k]
                    block = jnp.concatenate([h_ref[per * c], h_ref[per * c + 1]], axis=1)
                    out_ref[r, k] = dot(block, d, ((0,), (0,))).astype(BF16)

                @pl.when(k >= count_ref[r])
                def _():
                    out_ref[r, k] = jnp.zeros((BLK, BLK), BF16)

    return pl.pallas_call(
        body,
        out_shape=jax.ShapeDtypeStruct((rows, KD2, BLK, BLK), BF16),
        in_specs=[
            pl.BlockSpec(memory_space=pltpu.SMEM),
            pl.BlockSpec(memory_space=pltpu.SMEM),
            pl.BlockSpec(memory_space=pltpu.VMEM),
            pl.BlockSpec(memory_space=pltpu.VMEM),
        ],
        out_specs=pl.BlockSpec(memory_space=pltpu.VMEM),
        name="grad_second",
    )(cols, count, hidden, delta)


def shards(
    slopes,
    cols_first,
    count_first,
    weight_first,
    bias_first,
    cols_second,
    count_second,
    weight_second,
    bias_second,
    cotangent,
):
    rows = weight_first.shape[0]
    out_at = lax.axis_index(OUT)
    own_cols = lax.dynamic_slice_in_dim(cols_first, out_at * rows, rows, 0)
    live_first = count_first[:, 0]
    live_second = count_second[:, 0]
    gathered = lax.all_gather(slopes, OUT, axis=0, tiled=True)

    partial_first = forward_first(gathered, weight_first, own_cols, live_first)
    parts_first = lax.all_to_all(partial_first, IN, 0, 0, tiled=True)
    summed_first = jnp.sum(parts_first.astype(F32), axis=0)
    hidden_first = jnp.tanh(summed_first + bias_first[None, :]).astype(BF16)
    hidden = lax.all_gather(hidden_first, OUT, axis=0)

    partial_second = forward_second(hidden, weight_second, cols_second, live_second)
    parts_second = lax.all_to_all(partial_second, IN, 0, 0, tiled=True)
    summed_second = jnp.sum(parts_second.astype(F32), axis=0)
    estimate = jnp.tanh(summed_second + bias_second[None, :]).astype(BF16)
    est32 = estimate.astype(F32)
    delta_second = (cotangent.astype(F32) * (1.0 - est32 * est32)).astype(BF16)
    rows_second = lax.all_gather(delta_second, IN, axis=0)

    back = adjoint_second(rows_second, weight_second, cols_second, live_second, hidden.shape[0] // 2)
    parts_back = lax.all_to_all(back, OUT, 0, 0, tiled=True)
    back_first = jnp.sum(parts_back.astype(F32), axis=0)
    hid32 = hidden_first.astype(F32)
    delta_first = (back_first * (1.0 - hid32 * hid32)).astype(BF16)
    rows_first = lax.all_gather(delta_first, IN, axis=0)
    grad_second = grad_second_blocks(hidden, rows_second, cols_second, live_second)
    grad_first = grad_first_blocks(gathered, rows_first, own_cols, live_first)
    return (estimate, grad_first, grad_second)


def solution(mesh):
    fine = Mesh(mesh.devices.reshape(4, 4, 2, 2, 4), OUT + IN)
    return jax.shard_map(
        shards,
        mesh=fine,
        in_specs=(
            P(OUT, IN),
            P(None, IN),
            P(OUT, IN),
            P(OUT, IN, None, None),
            P(OUT + IN),
            P(OUT, IN),
            P(OUT, IN),
            P(OUT, IN, None, None),
            P(OUT + IN),
            P(None, OUT + IN),
        ),
        out_specs=(P(None, OUT + IN), P(OUT, IN, None, None), P(OUT, IN, None, None)),
        check_vma=False,
    )
```

time: 478 us -> 341 us (0.71)
  waiting for transfers between devices: 318 us -> 195 us
  local copies, waits for them, and re-layouts: 59.9 us -> 0.77 us
  Pallas kernels: 0 us -> 33.7 us
  blocking collectives: 45.8 us -> 77.5 us
  matrix products: 26.1 us -> 0 us
  starting transfers between devices: 0.2 us -> 12.6 us
    reduce_scatter x3 -> x0, waiting for transfers between devices: 163 us -> none  [the longest x1 95.1 us: shards(): lax.psum_scatter(spread.astype(jnp.bfloat16), 'out', scatter_dimension=1,...]
    all_to_all x0 -> x1, waiting for transfers between devices: none -> 45.9 us  [shards(): parts_back = lax.all_to_all(back, OUT, 0, 0, tiled=True)]
    pallas_call x0 -> x5, Pallas kernels: none -> 33.7 us  [the longest x1 9.8 us: grad_first_blocks(): pl.pallas_call(body, out_shape=jax.ShapeDtypeStruct((rows, KD1, BLK, BLK)...]
    all_to_all x0 -> x2, blocking collectives: none -> 27.4 us  [the longest x1 14.9 us: shards(): parts_second = lax.all_to_all(partial_second, IN, 0, 0, tiled=True)]
    dot_general x6 -> x0, matrix products: 26.1 us -> none  [the longest x1 6.23 us: shards(): jnp.einsum('frkb,rkbo->fro', panels_first, masked_first, preferred_elemen...]
    reshape x6 -> x0, local copies, waits for them, and re-layouts: 23 us -> none  [the longest x1 14.4 us: shards(): slope_blocks = gathered.reshape(frames, -1, BLK)]
    gather x4 -> x0, local copies, waits for them, and re-layouts: 19.4 us -> none  [the longest x2 13 us: shards(): jnp.take(slope_blocks, own_cols.reshape(-1), axis=1)]
    all_gather x1 -> x0, local copies, waits for them, and re-layouts: 13.8 us -> none  [shards(): gathered = lax.all_gather(slopes, 'out', axis=0, tiled=True)]
  transfers between devices with their start and end apart: 5 -> 3, of which waited for: 5 -> 3; matrix products, arithmetic and copies ran while one was open for 1% -> 0% of each run, Pallas kernels for 0% -> 2%
where the time goes in v1:
time: 341 us; the launch traced here: 336 us
  waiting for transfers between devices  195 us (57%)
  blocking collectives  77.5 us (23%)
  Pallas kernels  33.7 us (10%)
  between operations  14.1 us (4%)
  starting transfers between devices  12.6 us (4%)
    all_gather x1, waiting for transfers between devices, shards(): gathered = lax.all_gather(slopes, OUT, axis=0, tiled=True)  95.5 us
    all_gather x1, waiting for transfers between devices, shards(): hidden = lax.all_gather(hidden_first, OUT, axis=0)  53.3 us
    all_to_all x1, waiting for transfers between devices, shards(): parts_back = lax.all_to_all(back, OUT, 0, 0, tiled=True)  45.9 us
    all_gather x1, blocking collectives, shards(): rows_first = lax.all_gather(delta_first, IN, axis=0)  25.2 us
    all_gather x1, blocking collectives, shards(): rows_second = lax.all_gather(delta_second, IN, axis=0)  24.8 us
    all_to_all x1, blocking collectives, shards(): parts_second = lax.all_to_all(partial_second, IN, 0, 0, tiled=True)  14.9 us
    all_to_all x1, blocking collectives, shards(): parts_first = lax.all_to_all(partial_first, IN, 0, 0, tiled=True)  12.5 us
    all_to_all x1, starting transfers between devices, shards(): parts_back = lax.all_to_all(back, OUT, 0, 0, tiled=True)  12.5 us
  transfers between devices with their start and end apart: 3, of which 3 were waited for; matrix products, arithmetic and copies ran while one was open for 0% of the time, Pallas kernels for 2%

profile of v1, /device:TPU:1, one launch (start us, length us, event | category | flops | bytes accessed | tf_op | source)
XLA Modules:
  0.0 335.9 jit_solution(5400231488787845820)
XLA Ops:
  7.2 0.0 copy-start
  7.2 0.0 all-gather.4.cloned.1.call-start
  7.2 0.7 all-gather.4.cloned.1.call-update
  7.9 0.0 all-gather.6.cloned.1.call-start
  8.0 0.0 copy-done
  8.0 0.1 constant_dynamic-slice_fusion
  8.1 0.7 copy.15.cols_ref
  8.7 95.5 %all-gather.4.cloned.1.call-done.refs_0_.refs_1_.refs_2_.refs_3_.refs_4_.refs_5_.refs_6_.refs_7_ = bf16[256,20480]{1,0:T(8,128)(2,1)} async-done(((bf16[8,20480]{1,0:T(8,128)(2,1)}), bf16[256,20480]{1,0:T(8,128)(2,1)}) %all-gather.4.cloned.1.call-update) | async-done | bytes 10485776 | tf_op jit(solution)/shard_map/all_gather | solution.py:219
  104.2 0.0 copy-start.2
  104.2 8.9 %forward_first.1 = bf16[8,256,128]{2,1,0:T(8,128)(2,1)} custom-call(s32[4,8]{1,0:T(4,128)} %copy.15.cols_ref, s32[4]{0:T(128)} %bitcast.20, bf16[256,20480]{1,0:T(8,128)(2,1)} %all-gather.4.cloned.1.call-done.refs_0_.refs_1_.refs_2_.refs_3_.refs_4_.refs_5_.refs_6_.refs_7_, ...), custom_call_target="tpu_custom_call" | custom-call | tf_op jit(solution)/shard_map/forward_first/pallas_call | solution.py:40
  113.1 12.5 %all_to_all.15 = bf16[8,256,128]{2,1,0:T(8,128)(2,1)S(1)} all-to-all(bf16[8,256,128]{2,1,0:T(8,128)(2,1)} %forward_first.1), channel_id=1, replica_groups=mesh['x'=4,'zh'=4,'core'=2,'zl'=2,'y'=4] {'zl','y'}, dimensions={0} | all-to-all | bytes 1048576 | tf_op jit(solution)/shard_map/all_to_all | solution.py:222
  125.7 0.1 convert_reduce_fusion.2
  125.7 0.0 copy-done.2
  125.7 0.7 fusion.2
  126.4 0.0 all-gather.6.cloned.1.call-update
  126.4 53.3 %all-gather.6.cloned.1.call-done.h_ref = bf16[32,256,128]{2,1,0:T(8,128)(2,1)} async-done(((bf16[1,256,128]{2,1,0:T(8,128)(2,1)}), bf16[32,256,128]{2,1,0:T(8,128)(2,1)}) %all-gather.6.cloned.1.call-update) | async-done | bytes 2097168 | tf_op jit(solution)/shard_map/all_gather | solution.py:225
  179.8 0.0 copy-start.1
  179.8 0.0 copy-start.3
  179.8 4.6 %forward_second.1 = bf16[8,256,128]{2,1,0:T(8,128)(2,1)} custom-call(s32[4,4]{1,0:T(4,128)} %cols_ref.5, s32[4]{0:T(128)} %bitcast.17, bf16[32,256,128]{2,1,0:T(8,128)(2,1)} %all-gather.6.cloned.1.call-done.h_ref, bf16[4,4,256,256]{3,2,1,0:T(8,128)(2,1)} %w_ref.3), custom_call_target="tpu_custom_call" | custom-call | tf_op jit(solution)/shard_map/forward_second/pallas_call | solution.py:118
  184.3 14.9 %all_to_all.16 = bf16[8,256,128]{2,1,0:T(8,128)(2,1)S(1)} all-to-all(bf16[8,256,128]{2,1,0:T(8,128)(2,1)} %forward_second.1), channel_id=1, replica_groups=mesh['x'=4,'zh'=4,'core'=2,'zl'=2,'y'=4] {'zl','y'}, dimensions={0} | all-to-all | bytes 1048576 | tf_op jit(solution)/shard_map/all_to_all | solution.py:228
  199.2 0.1 convert_reduce_fusion.1
  199.3 0.0 copy-done.1
  199.3 0.0 copy-done.3
  199.3 0.7 multiply_convert_fusion
  200.0 24.8 %all-gather = bf16[2048,128]{1,0:T(8,128)(2,1)} all-gather(bf16[256,128]{1,0:T(8,128)(2,1)S(1)} %get-tuple-element.3), channel_id=2, replica_groups=mesh['x'=4,'zh'=4,'core'=2,'zl'=2,'y'=4] {'zl','y'}, dimensions={0}, use_global_device_ids=true | all-gather | bytes 589824 | tf_op jit(solution)/shard_map/all_gather | solution.py:233
  224.8 5.4 %adjoint_second.1 = bf16[32,256,128]{2,1,0:T(8,128)(2,1)} custom-call(s32[4,4]{1,0:T(4,128)} %cols_ref.5, s32[4]{0:T(128)} %bitcast.18, bf16[8,256,128]{2,1,0:T(8,128)(2,1)} %bitcast.15, bf16[4,4,256,256]{3,2,1,0:T(8,128)(2,1)} %w_ref.3), custom_call_target="tpu_custom_call" | custom-call | tf_op jit(solution)/shard_map/adjoint_second/pallas_call | solution.py:153
  230.2 12.5 %all-to-all-start.2 = ((bf16[32,256,128]{2,1,0:T(8,128)(2,1)}), bf16[32,256,128]{2,1,0:T(8,128)(2,1)S(1)}, u32[]{:S(2)}, u32[]{:S(2)}) async-start(bf16[32,256,128]{2,1,0:T(8,128)(2,1)} %adjoint_second.1), calls=%async_computation.2 | async-start | bytes 4194304 | tf_op jit(solution)/shard_map/all_to_all | solution.py:236
  242.7 5.1 %grad_second.1 = bf16[4,4,256,256]{3,2,1,0:T(8,128)(2,1)} custom-call(s32[4,4]{1,0:T(4,128)} %cols_ref.5, s32[4]{0:T(128)} %bitcast.19, bf16[32,256,128]{2,1,0:T(8,128)(2,1)} %all-gather.6.cloned.1.call-done.h_ref, bf16[8,256,128]{2,1,0:T(8,128)(2,1)} %bitcast.16), custom_call_target="tpu_custom_call" | custom-call | tf_op jit(solution)/shard_map/grad_second/pallas_call | solution.py:188
  247.8 45.9 %all-to-all-done.2 = bf16[32,256,128]{2,1,0:T(8,128)(2,1)S(1)} async-done(((bf16[32,256,128]{2,1,0:T(8,128)(2,1)}), bf16[32,256,128]{2,1,0:T(8,128)(2,1)S(1)}, u32[]{:S(2)}, u32[]{:S(2)}) %all-to-all-start.2) | async-done | bytes 2097184 | tf_op jit(solution)/shard_map/all_to_all | solution.py:236
  293.7 0.3 convert_reduce_fusion
  294.0 25.2 %all_gather.21.refs_8_ = bf16[8,256,128]{2,1,0:T(8,128)(2,1)} all-gather(bf16[1,256,128]{2,1,0:T(8,128)(2,1)S(1)} %fusion), channel_id=1, replica_groups=mesh['x'=4,'zh'=4,'core'=2,'zl'=2,'y'=4] {'zl','y'}, dimensions={0}, use_global_device_ids=true | all-gather | bytes 589824 | tf_op jit(solution)/shard_map/all_gather | solution.py:240
  319.2 9.8 %grad_first.1 = bf16[4,8,256,256]{3,2,1,0:T(8,128)(2,1)} custom-call(s32[4,8]{1,0:T(4,128)} %copy.15.cols_ref, s32[4]{0:T(128)} %bitcast.21, bf16[256,20480]{1,0:T(8,128)(2,1)} %all-gather.4.cloned.1.call-done.refs_0_.refs_1_.refs_2_.refs_3_.refs_4_.refs_5_.refs_6_.refs_7_, ...), custom_call_target="tpu_custom_call" | custom-call | tf_op jit(solution)/shard_map/grad_first/pallas_call | solution.py:76
  (1 shorter events, 0.0 us)
Async XLA Ops:
  7.2 0.8 copy-start
  7.2 97.1 %all-gather.4.cloned.1.call-start = ((), (), s32[]{:S(2)}) async-start(), calls=%async_computation.3 | async-start | bytes 10813440 | tf_op jit(solution)/shard_map/all_gather | solution.py:219
  7.9 171.8 %all-gather.6.cloned.1.call-start = ((), (), s32[]{:S(2)}) async-start(), calls=%async_computation.4 | async-start | bytes 2162688 | tf_op jit(solution)/shard_map/all_gather | solution.py:225
  104.2 21.5 %copy-start.2 = (f32[128]{0:T(128)S(1)}, f32[128]{0:T(128)}, u32[]{:S(2)}) copy-start(f32[128]{0:T(128)} %param.14) | copy-start | bytes 1540
  179.8 19.5 %copy-start.1 = (bf16[256,128]{1,0:T(8,128)(2,1)S(1)}, bf16[256,128]{1,0:T(8,128)(2,1)}, u32[]{:S(2)}) copy-start(bf16[256,128]{1,0:T(8,128)(2,1)} %param.19) | copy-start | bytes 196612
  179.8 19.5 %copy-start.3 = (f32[128]{0:T(128)S(1)}, f32[128]{0:T(128)}, u32[]{:S(2)}) copy-start(f32[128]{0:T(128)} %param.18) | copy-start | bytes 1540
  230.2 63.5 %all-to-all-start.2 = ((bf16[32,256,128]{2,1,0:T(8,128)(2,1)}), bf16[32,256,128]{2,1,0:T(8,128)(2,1)S(1)}, u32[]{:S(2)}, u32[]{:S(2)}) async-start(bf16[32,256,128]{2,1,0:T(8,128)(2,1)} %adjoint_second.1), calls=%async_computation.2 | async-start | bytes 4194304 | tf_op jit(solution)/shard_map/all_to_all | solution.py:236
Sparse Core Ops, SparseCore 0:
  10.6 93.6 all-gather.3
  126.5 53.1 all-gather.5

commit v2 on v0

v2 whole, which is shorter than its diff:
```python
import jax
import jax.numpy as jnp
from jax import lax
from jax.experimental import pallas as pl
from jax.experimental.pallas import tpu as pltpu
from jax.sharding import Mesh
from jax.sharding import PartitionSpec as P

BLK = 256
KD1 = 8
KD2 = 4
SUB = 128
ROWS = 4
NX = 4
NZ = 4
OUT = ("x", "zh", "core")
IN = ("zl", "y")
F32 = jnp.float32
BF16 = jnp.bfloat16

HBM = pl.BlockSpec(memory_space=pltpu.HBM)
SMEM = pl.BlockSpec(memory_space=pltpu.SMEM)
VMEM = pl.BlockSpec(memory_space=pltpu.VMEM)


def dot(a, b, dims):
    return lax.dot_general(a, b, (dims, ((), ())), preferred_element_type=F32)


def halves(ref, row, *at):
    return jnp.concatenate([ref[(2 * row, *at)], ref[(2 * row + 1, *at)]], axis=1)


def limit(mib):
    return pltpu.CompilerParams(vmem_limit_bytes=mib * 2**20)


def on_chip(*values):
    return [pltpu.with_memory_space_constraint(v, pltpu.VMEM) for v in values]


def in_hbm(*values):
    return [pltpu.with_memory_space_constraint(v, pltpu.HBM) for v in values]


def forward_first(pos, cols, table, sib_table, pieces, weight, sibling):
    arrays = [a for a, _, _ in pieces]
    n = len(arrays)
    own_rows = arrays[0].shape[0]
    width = arrays[0].shape[1]
    frames = NX * NZ * own_rows
    n_copies = sum(len(o) for _, o, _ in pieces)

    def body(pos_ref, cols_ref, tab_ref, sib_tab_ref, *refs):
        srcs, (own_ref, sib_ref, out_ref, p_own, p_sib) = refs[:n], refs[n : n + 5]
        whole, weights, sems, wsems, psems = refs[n + 5 :]
        x, z, core, out_at = pos_ref[0], pos_ref[1], pos_ref[2], pos_ref[3]
        copies = []
        for src, (a, offsets, first) in zip(srcs, pieces):
            for m, (dx, dz) in enumerate(offsets):
                row = ((x + dx) % NX * NZ + (z + dz) % NZ) * own_rows
                copies.append(
                    pltpu.make_async_copy(
                        src.at[pl.ds(m * own_rows, own_rows), :],
                        whole.at[
                            pl.ds(pl.multiple_of(row, own_rows), own_rows),
                            pl.ds(first, a.shape[1]),
                        ],
                        sems.at[len(copies)],
                    )
                )
                copies[-1].start()

        def load(who, r):
            src = (own_ref, sib_ref)[who]
            return pltpu.make_async_copy(src.at[r], weights.at[who, r], wsems.at[who, r])

        for who in range(2):
            for r in range(ROWS):
                load(who, r).start()
        for c in copies:
            c.wait()
        for mine in (True, False):
            who, tab, to = (0, tab_ref, p_own) if mine else (1, sib_tab_ref, p_sib)
            base = (out_at if mine else out_at ^ 1) * ROWS
            side = core if mine else 1 - core
            sem = psems.at[who]

            def row(r, _, who=who, base=base, side=side, tab=tab, to=to, sem=sem):
                panels = []
                for k in range(KD1):
                    at = pl.ds(pl.multiple_of(cols_ref[base + r, k] * BLK, BLK), BLK)
                    pltpu.make_async_copy(whole.at[:, at], to.at[r, k], sem).start()
                    panels.append(whole[:, at] * (k < tab[r, 0]).astype(BF16))
                load(who, r).wait()
                weight = weights[who, r].reshape(KD1 * BLK, BLK)
                out = dot(jnp.concatenate(panels, axis=1), weight, ((1,), (0,)))
                out_ref[2 * r, side] = out[:, :SUB].astype(BF16)
                out_ref[2 * r + 1, side] = out[:, SUB:].astype(BF16)
                return 0

            lax.fori_loop(0, ROWS, row, 0)
        for mine in (True, False):
            to = p_own if mine else p_sib
            pltpu.make_async_copy(to, to, psems.at[0 if mine else 1]).wait()

    panels = pltpu.HBM((ROWS, KD1, frames, BLK), BF16)
    return pl.pallas_call(
        body,
        out_shape=(jax.ShapeDtypeStruct((2 * ROWS, 2, frames, SUB), BF16), panels, panels),
        in_specs=[SMEM] * 4 + [HBM] * (n + 2),
        out_specs=(VMEM, HBM, HBM),
        scratch_shapes=[
            pltpu.VMEM((frames, width), BF16),
            pltpu.VMEM((2, ROWS, KD1, BLK, BLK), BF16),
            pltpu.SemaphoreType.DMA((n_copies,)),
            pltpu.SemaphoreType.DMA((2, ROWS)),
            pltpu.SemaphoreType.DMA((2,)),
        ],
        compiler_params=limit(20),
        cost_estimate=pl.CostEstimate(flops=2**31, bytes_accessed=2**24, transcendentals=0),
        name="forward_first",
    )(pos, cols, table, sib_table, *in_hbm(*arrays, weight, sibling))


def relative(block, x, z):
    return (block // NZ - x) % NX * NZ + (block % NZ - z) % NZ


def forward_second(pos, table, sib_table, pieces, weight, sibling):
    frames = pieces[0].shape[2]

    def body(pos_ref, tab_ref, sib_tab_ref, *refs):
        srcs, (own_ref, sib_ref, out_ref, p_own, p_sib) = refs[:NX], refs[NX : NX + 5]
        blocks, panels, psems = refs[NX + 5 :]
        x, z, core = pos_ref[0], pos_ref[1], pos_ref[2]
        for k in range(NX):
            for zr in range(NZ):
                blocks[k * NZ + zr, :, :SUB] = srcs[k][zr, 0]
                blocks[k * NZ + zr, :, SUB:] = srcs[k][zr, 1]
        for mine in (True, False):
            w_ref, tab, to = (own_ref, tab_ref, p_own) if mine else (sib_ref, sib_tab_ref, p_sib)
            side = core if mine else 1 - core
            n = 0 if mine else 1

            def row(r, _):
                used = []
                for k in range(KD2):
                    panel = blocks[relative(tab[r, 2 + k], x, z)]
                    panels[n, r, k] = panel
                    used.append(panel * (k < tab[r, 1]).astype(BF16))
                pltpu.make_async_copy(panels.at[n, r], to.at[r], psems.at[n]).start()
                out = dot(jnp.concatenate(used, axis=1), w_ref[r].reshape(KD2 * BLK, BLK), ((1,), (0,)))
                out_ref[2 * r, side] = out[:, :SUB].astype(BF16)
                out_ref[2 * r + 1, side] = out[:, SUB:].astype(BF16)
                return 0

            lax.fori_loop(0, ROWS, row, 0)
        for n, to in enumerate((p_own, p_sib)):
            pltpu.make_async_copy(to, to, psems.at[n]).wait()

    panels = pltpu.HBM((ROWS, KD2, frames, BLK), BF16)
    return pl.pallas_call(
        body,
        out_shape=(jax.ShapeDtypeStruct((2 * ROWS, 2, frames, SUB), BF16), panels, panels),
        in_specs=[SMEM] * 3 + [VMEM] * (NX + 2),
        out_specs=(VMEM, HBM, HBM),
        scratch_shapes=[
            pltpu.VMEM((NX * NZ, frames, BLK), BF16),
            pltpu.VMEM((2, ROWS, KD2, frames, BLK), BF16),
            pltpu.SemaphoreType.DMA((2,)),
        ],
        compiler_params=limit(12),
        cost_estimate=pl.CostEstimate(flops=2**30, bytes_accessed=2**23, transcendentals=0),
        name="forward_second",
    )(pos, table, sib_table, *on_chip(*pieces, weight, sibling))


def adjoint_second(pos, table, sib_table, delta, weight, sibling):
    frames = delta.shape[2]

    def body(pos_ref, tab_ref, sib_tab_ref, d_ref, own_ref, sib_ref, *refs):
        outs, (acc,) = refs[:NX], refs[NX:]
        x, z, core = pos_ref[0], pos_ref[1], pos_ref[2]
        acc[...] = jnp.zeros(acc.shape, F32)
        for mine in (True, False):
            w_ref, tab = (own_ref, tab_ref) if mine else (sib_ref, sib_tab_ref)
            side = core if mine else 1 - core

            def row(r, _):
                d = halves(d_ref, r, side)
                terms = dot(d, w_ref[r].reshape(KD2 * BLK, BLK), ((1,), (1,)))
                for k in range(KD2):
                    term = terms[:, k * BLK : (k + 1) * BLK]
                    acc[relative(tab[r, 2 + k], x, z)] += term * (k < tab[r, 1]).astype(F32)
                return 0

            lax.fori_loop(0, ROWS, row, 0)
        for k in range(NX):
            for zr in range(NZ):
                outs[k][zr, 0] = acc[k * NZ + zr, :, :SUB].astype(BF16)
                outs[k][zr, 1] = acc[k * NZ + zr, :, SUB:].astype(BF16)

    return pl.pallas_call(
        body,
        out_shape=(jax.ShapeDtypeStruct((NZ, 2, frames, SUB), BF16),) * NX,
        in_specs=[SMEM] * 3 + [VMEM] * 3,
        out_specs=(VMEM,) * NX,
        scratch_shapes=[pltpu.VMEM((NX * NZ, frames, BLK), F32)],
        compiler_params=limit(12),
        cost_estimate=pl.CostEstimate(flops=2**30, bytes_accessed=2**23, transcendentals=0),
        name="adjoint_second",
    )(pos, table, sib_table, *on_chip(delta, weight, sibling))


def add_shares(parts):
    n = parts[0].shape[0]

    def body(*refs):
        ins, outs = refs[: len(parts)], refs[len(parts) :]
        for k in range(n):
            total = ins[0][k].astype(F32)
            for p in ins[1:]:
                total += p[k].astype(F32)
            outs[k][...] = total.astype(BF16)

    return pl.pallas_call(
        body,
        out_shape=(jax.ShapeDtypeStruct(parts[0].shape[1:], BF16),) * n,
        in_specs=[VMEM] * len(parts),
        out_specs=(VMEM,) * n,
        compiler_params=limit(8),
        name="add_shares",
    )(*on_chip(*parts))


def weight_grads(pos, table, field, panels, other_panels, deltas, name):
    arrays, rows_of = deltas
    slots, frames = panels.shape[1], panels.shape[2]

    def body(pos_ref, tab_ref, p_ref, po_ref, *refs):
        d_refs, (out_ref, grads, gsem) = refs[: len(arrays)], refs[len(arrays) :]
        core = pos_ref[2]

        def row(r, _):
            d = jnp.concatenate(rows_of(core, d_refs, r), axis=0)
            for k in range(slots):
                panel = jnp.concatenate([p_ref[r, k], po_ref[r, k]], axis=0)
                live = (k < tab_ref[r, field]).astype(F32)
                grads[r, k] = (dot(panel, d, ((0,), (0,))) * live).astype(BF16)
            pltpu.make_async_copy(grads.at[r], out_ref.at[r], gsem).start()
            return 0

        lax.fori_loop(0, ROWS, row, 0)
        pltpu.make_async_copy(out_ref, out_ref, gsem).wait()

    return pl.pallas_call(
        body,
        out_shape=jax.ShapeDtypeStruct((ROWS, slots, BLK, BLK), BF16),
        in_specs=[SMEM, SMEM] + [VMEM] * (2 + len(arrays)),
        out_specs=HBM,
        scratch_shapes=[
            pltpu.VMEM((ROWS, slots, BLK, BLK), BF16),
            pltpu.SemaphoreType.DMA,
        ],
        compiler_params=limit(12),
        cost_estimate=pl.CostEstimate(
            flops=slots * 2**27, bytes_accessed=slots * 2**20, transcendentals=0
        ),
        name=name,
    )(pos, table, *on_chip(panels, other_panels, *arrays))


def ring(value, axis, step, label="ring"):
    n = lax.axis_size(axis)
    with jax.named_scope("L_" + label):
        return lax.ppermute(value, axis, [(i, (i + step) % n) for i in range(n)])


def swap(value, label="swap"):
    with jax.named_scope("L_" + label):
        return lax.ppermute(value, "core", [(0, 1), (1, 0)])


def together(*values):
    return lax.optimization_barrier(values)


def gather_slopes(s):
    half = s.shape[1] // 2
    zp, zn = ring(s, "zh", 1, "zp"), ring(s, "zh", -1, "zn")
    xp, xn = ring(s, "x", 1, "xp"), ring(s, "x", -1, "xn")
    zp, zn, xp, xn = together(zp, zn, xp, xn)
    zps, zns = zp[:, :half], zn[:, half:]
    t = jnp.concatenate([zp, zn], axis=0)
    zps, zns, t = together(zps, zns, t)
    zl, zr = ring(zps, "zh", 1, "zl"), ring(zns, "zh", -1, "zr")
    tp, tn = ring(t, "x", 1, "tp"), ring(t, "x", -1, "tn")
    zl, zr = together(zl, zr)
    f = jnp.concatenate([zl, zr], axis=1)
    fp, fn = ring(f, "x", 1, "fp"), ring(f, "x", -1, "fn")
    tp, tn = together(tp, tn)
    ol = jnp.concatenate([xp[:, :half], tp[:, :half]], axis=0)
    oh = jnp.concatenate([xn[:, half:], tn[:, half:]], axis=0)
    ol, oh = ring(ol, "x", 1, "ol"), ring(oh, "x", -1, "oh")
    fp, fn = together(fp, fn)
    fl, fh = ring(fp[:, :half], "x", 1, "fl"), ring(fn[:, half:], "x", -1, "fh")
    pieces = [(s, [(0, 0)], 0), (xp, [(-1, 0)], 0), (xn, [(1, 0)], 0)]
    pieces += [(t, [(0, -1), (0, 1)], 0), (tp, [(-1, -1), (-1, 1)], 0), (tn, [(1, -1), (1, 1)], 0)]
    pieces += [(f, [(0, 2)], 0), (fp, [(-1, 2)], 0), (fn, [(1, 2)], 0)]
    pieces += [(a, [(2, 0), (2, -1), (2, 1)], first) for a, first in ((ol, 0), (oh, half))]
    pieces += [(fl, [(2, 2)], 0), (fh, [(2, 2)], half)]
    return pieces


def gather_axis(value, axis):
    n = lax.axis_size(axis)
    return lax.all_to_all(jnp.broadcast_to(value[None], (n, *value.shape)), axis, 0, 0, tiled=True)


def sum_axis(parts, axis):
    return jnp.sum(lax.all_to_all(parts, axis, 0, 0, tiled=True).astype(F32), axis=0)


def shards(
    slopes,
    cols_first,
    count_first,
    weight_first,
    bias_first,
    cols_second,
    count_second,
    weight_second,
    bias_second,
    cotangent,
):
    frames = cotangent.shape[0]
    chips = NX * NZ
    own = slopes.shape[0]
    core = lax.axis_index("core")
    pos = jnp.stack(
        [lax.axis_index("x"), lax.axis_index("zh"), core, lax.axis_index(OUT)]
    ).astype(jnp.int32)

    def canonical(mine, other):
        return jnp.where(core == 0, jnp.stack([mine, other]), jnp.stack([other, mine]))

    pieces = gather_slopes(slopes)
    sibling_first = swap(weight_first)
    sibling_second = swap(weight_second)
    table = jnp.concatenate([count_first, count_second, cols_second], axis=1)
    sib_table = swap(table)
    bias = jnp.stack([bias_first, bias_second])
    biases = canonical(bias, swap(bias))
    by_core = cotangent.reshape(chips, 2, own, SUB)
    mine = lax.dynamic_index_in_dim(by_core, core, 1, keepdims=False)
    theirs = lax.dynamic_index_in_dim(by_core, 1 - core, 1, keepdims=False)
    cot = canonical(mine, swap(theirs)).reshape(2, chips * own, SUB).astype(F32)

    partial_first, panels_first, lent_first = forward_first(
        pos, cols_first, table, sib_table, pieces, weight_first, sibling_first
    )
    summed_first = sum_axis(partial_first, IN)
    hidden_first = jnp.tanh(summed_first + biases[:, 0][:, None, :]).astype(BF16)
    along_z = jnp.stack([hidden_first] + [ring(hidden_first, "zh", -k) for k in range(1, NZ)])
    hidden = [along_z] + [ring(along_z, "x", -k) for k in range(1, NX)]

    partial_second, panels_second, lent_second = forward_second(
        pos, table, sib_table, hidden, weight_second, sibling_second
    )
    summed_second = sum_axis(partial_second, IN)
    estimate = jnp.tanh(summed_second + biases[:, 1][:, None, :]).astype(BF16)
    est32 = estimate.astype(F32)
    delta_second = (cot * (1.0 - est32 * est32)).astype(BF16)
    rows_second = gather_axis(delta_second, IN)

    back = adjoint_second(pos, table, sib_table, rows_second, weight_second, sibling_second)
    along_x = add_shares([back[0]] + [ring(back[k], "x", k) for k in range(1, NX)])
    shares = [along_x[0]] + [ring(along_x[k], "zh", k) for k in range(1, NZ)]
    back_first = sum(s.astype(F32) for s in shares)
    hid32 = hidden_first.astype(F32)
    delta_first = (back_first * (1.0 - hid32 * hid32)).astype(BF16)
    to_all = jnp.broadcast_to(delta_first[:, None], (2, lax.axis_size(IN), *delta_first.shape[1:]))
    rows_first = lax.all_to_all(
        to_all.reshape(-1, *delta_first.shape[1:]), ("core", *IN), 0, 0, tiled=True
    ).reshape(to_all.shape)
    lent_rows = swap(lax.dynamic_index_in_dim(rows_second, 1 - core, 1, keepdims=False))
    grad_second = weight_grads(
        pos,
        table,
        1,
        panels_second,
        swap(lent_second),
        (
            (rows_second, lent_rows),
            lambda core, refs, r: [halves(refs[0], r, core), halves(refs[1], r)],
        ),
        "grad_second",
    )
    est_own = lax.dynamic_index_in_dim(estimate, core, 0, keepdims=False)
    est_other = swap(lax.dynamic_index_in_dim(estimate, 1 - core, 0, keepdims=False))
    both = canonical(est_own, est_other).reshape(2, chips, own, SUB)
    estimate_out = both.transpose(1, 0, 2, 3).reshape(frames, SUB)
    rows_first, grad_second, estimate_out = together(rows_first, grad_second, estimate_out)
    grad_first = weight_grads(
        pos,
        table,
        0,
        panels_first,
        swap(lent_first),
        (
            (rows_first,),
            lambda core, refs, r: [halves(refs[0].at[core], r), halves(refs[0].at[1 - core], r)],
        ),
        "grad_first",
    )
    return (estimate_out, grad_first, grad_second)


def solution(mesh):
    fine = Mesh(mesh.devices.reshape(NX, NZ, 2, 2, 4), OUT + IN)
    return jax.shard_map(
        shards,
        mesh=fine,
        in_specs=(
            P(OUT, IN),
            P(None, IN),
            P(OUT, IN),
            P(OUT, IN, None, None),
            P(OUT + IN),
            P(OUT, IN),
            P(OUT, IN),
            P(OUT, IN, None, None),
            P(OUT + IN),
            P(None, OUT + IN),
        ),
        out_specs=(P(None, OUT + IN), P(OUT, IN, None, None), P(OUT, IN, None, None)),
        check_vma=False,
    )
```

time: 478 us -> 208 us (0.44); the launches traced: 469 us -> 206 us
  waiting for transfers between devices: 318 us -> 86.7 us
  starting transfers between devices: 0.2 us -> 78.9 us
  local copies, waits for them, and re-layouts: 59.9 us -> 8.31 us
  blocking collectives: 45.8 us -> 0 us
  Pallas kernels: 0 us -> 28.1 us
  matrix products: 26.1 us -> 0 us
  between operations: 13.9 us -> 1.21 us
    reduce_scatter x3 -> x0, waiting for transfers between devices: 163 us -> none  [the longest x1 95.1 us: shards(): lax.psum_scatter(spread.astype(jnp.bfloat16), 'out', scatter_dimension=1,...]
    all_gather x2 -> x0, waiting for transfers between devices: 155 us -> none  [the longest x1 94.5 us: shards(): gathered = lax.all_gather(slopes, 'out', axis=0, tiled=True)]
    ppermute x0 -> x35, waiting for transfers between devices: none -> 66.3 us  [the longest x26 64.4 us: ring(): return lax.ppermute(value, axis, [(i, (i + step) % n) for i in range(n)])]
    ppermute x0 -> x35, starting transfers between devices: none -> 56.3 us  [the longest x26 44.2 us: ring(): return lax.ppermute(value, axis, [(i, (i + step) % n) for i in range(n)])]
    all_gather x2 -> x0, blocking collectives: 45.8 us -> none  [the longest x1 23 us: shards(): lax.all_gather(delta_first, 'in', axis=1, tiled=True)]
    pallas_call x0 -> x6, Pallas kernels: none -> 28.1 us  [the longest x1 11.1 us: forward_first(): pl.pallas_call(body, out_shape=(jax.ShapeDtypeStruct((2 * ROWS, 2, frames...]
    dot_general x6 -> x0, matrix products: 26.1 us -> none  [the longest x1 6.23 us: shards(): jnp.einsum('frkb,rkbo->fro', panels_first, masked_first, preferred_elemen...]
    reshape x6 -> x0, local copies, waits for them, and re-layouts: 23 us -> none  [the longest x1 14.4 us: shards(): slope_blocks = gathered.reshape(frames, -1, BLK)]
  transfers between devices with their start and end apart: 5 -> 39, of which waited for: 5 -> 18; matrix products, arithmetic and copies ran while one was open for 1% -> 2% of each run, Pallas kernels for 0% -> 9%
where the time goes in v2:
time: 208 us; the launch traced here: 206 us
  waiting for transfers between devices  86.7 us (42%)
  starting transfers between devices  78.9 us (38%)
  Pallas kernels  28.1 us (14%)
  local copies, waits for them, and re-layouts  8.31 us (4%)
  other arithmetic  2.92 us (1%)
    ppermute x26, waiting for transfers between devices, ring(): return lax.ppermute(value, axis, [(i, (i + step) % n) for i in range(n)])  64.4 us
    ppermute x26, starting transfers between devices, ring(): return lax.ppermute(value, axis, [(i, (i + step) % n) for i in range(n)])  44.2 us
    all_to_all x2, waiting for transfers between devices, sum_axis(): lax.all_to_all(parts, axis, 0, 0, tiled=True).astype(F32)  12.9 us
    ppermute x9, starting transfers between devices, swap(): return lax.ppermute(value, 'core', [(0, 1), (1, 0)])  12.1 us
    pallas_call x1, Pallas kernels, forward_first(): pl.pallas_call(body, out_shape=(jax.ShapeDtypeStruct((2 * ROWS, 2, frames...  11.1 us
    all_to_all x2, starting transfers between devices, sum_axis(): lax.all_to_all(parts, axis, 0, 0, tiled=True).astype(F32)  9.25 us
    all_to_all x1, starting transfers between devices, shards(): lax.all_to_all(to_all.reshape(-1, *delta_first.shape[1:]), ('core', *IN),...  8.2 us
    pallas_call x2, Pallas kernels, weight_grads(): pl.pallas_call(body, out_shape=jax.ShapeDtypeStruct((ROWS, slots, BLK, BL...  7.32 us
  transfers between devices with their start and end apart: 39, of which 18 were waited for; matrix products, arithmetic and copies ran while one was open for 2% of the time, Pallas kernels for 9%

profile of v2, /device:TPU:1, one launch (start us, length us, event | category | flops | bytes accessed | tf_op | source)
XLA Modules:
  0.0 206.1 jit_solution(7151285001764745905)
XLA Ops:
  0.6 3.9 %collective-permute-start.2 = (bf16[8,20480]{1,0:T(8,128)(2,1)}, bf16[8,20480]{1,0:T(8,128)(2,1)S(1)}, u32[]{:S(2)}, u32[]{:S(2)}) collective-permute-start(bf16[8,20480]{1,0:T(8,128)(2,1)} %refs_0_.1), channel_id=1, source_target_pairs={{0,16},{16,32},{32,48},{48,0},{1,17},{17,33},{33,49},{49,1},{2,18}... | collective-permute-start | bytes 983048 | tf_op jit(solution)/shard_map/L_zp/ppermute | solution.py:277
  4.5 3.1 %collective-permute-start.3 = (bf16[8,20480]{1,0:T(8,128)(2,1)}, bf16[8,20480]{1,0:T(8,128)(2,1)S(1)}, u32[]{:S(2)}, u32[]{:S(2)}) collective-permute-start(bf16[8,20480]{1,0:T(8,128)(2,1)} %refs_0_.1), channel_id=1, source_target_pairs={{0,48},{16,0},{32,16},{48,32},{1,49},{17,1},{33,17},{49,33},{2,50}... | collective-permute-start | bytes 983048 | tf_op jit(solution)/shard_map/L_zn/ppermute | solution.py:277
  7.6 1.2 collective-permute-start.4
  8.9 1.5 collective-permute-start.5
  10.3 6.9 %collective-permute-done.2 = bf16[8,20480]{1,0:T(8,128)(2,1)S(1)} collective-permute-done((bf16[8,20480]{1,0:T(8,128)(2,1)}, bf16[8,20480]{1,0:T(8,128)(2,1)S(1)}, u32[]{:S(2)}, u32[]{:S(2)}) %collective-permute-start.2) | collective-permute-done | bytes 327712 | tf_op jit(solution)/shard_map/L_zp/ppermute | solution.py:277
  17.2 6.5 %collective-permute-done.3 = bf16[8,20480]{1,0:T(8,128)(2,1)S(1)} collective-permute-done((bf16[8,20480]{1,0:T(8,128)(2,1)}, bf16[8,20480]{1,0:T(8,128)(2,1)S(1)}, u32[]{:S(2)}, u32[]{:S(2)}) %collective-permute-start.3) | collective-permute-done | bytes 327712 | tf_op jit(solution)/shard_map/L_zn/ppermute | solution.py:277
  23.8 3.2 %collective-permute-start.8 = (bf16[8,10240]{1,0:T(8,128)(2,1)S(1)}, bf16[8,10240]{1,0:T(8,128)(2,1)S(1)}, u32[]{:S(2)}, u32[]{:S(2)}) collective-permute-start(bf16[8,10240]{1,0:T(8,128)(2,1)S(1)} %slice.30), channel_id=1, source_target_pairs={{0,16},{16,32},{32,48},{48,0},{1,17},{17,33},{33,49},{49,1},{2,18}... | collective-permute-start | bytes 491528 | tf_op jit(solution)/shard_map/L_zl/ppermute | solution.py:277
  27.5 1.5 collective-permute-start.16
  30.2 1.5 collective-permute-start.7
  31.7 2.8 %collective-permute-done.8 = bf16[8,10240]{1,0:T(8,128)(2,1)S(1)} collective-permute-done((bf16[8,10240]{1,0:T(8,128)(2,1)S(1)}, bf16[8,10240]{1,0:T(8,128)(2,1)S(1)}, u32[]{:S(2)}, u32[]{:S(2)}) %collective-permute-start.8) | collective-permute-done | bytes 163872 | tf_op jit(solution)/shard_map/L_zl/ppermute | solution.py:277
  34.6 1.3 collective-permute-start.10
  35.9 1.5 collective-permute-start.11
  37.4 9.2 %collective-permute-done.6.refs_4_ = bf16[16,20480]{1,0:T(8,128)(2,1)S(1)} collective-permute-done((bf16[16,20480]{1,0:T(8,128)(2,1)S(1)}, bf16[16,20480]{1,0:T(8,128)(2,1)S(1)}, u32[]{:S(2)}, u32[]{:S(2)}) %collective-permute-start.6) | collective-permute-done | bytes 655392 | tf_op jit(solution)/shard_map/L_tp/ppermute | solution.py:277
  49.2 2.6 %collective-permute-start.13 = (bf16[24,10240]{1,0:T(8,128)(2,1)}, bf16[24,10240]{1,0:T(8,128)(2,1)S(1)}, u32[]{:S(2)}, u32[]{:S(2)}) collective-permute-start(bf16[24,10240]{1,0:T(8,128)(2,1)} %pad_maximum_fusion.2), channel_id=1, source_target_pairs={{0,192},{64,0},{128,64},{192,128},{1,193},{65,1},{129,65},{193,129... | collective-permute-start | bytes 1474568 | tf_op jit(solution)/shard_map/L_oh/ppermute | solution.py:277
  51.9 1.7 collective-permute-done.10.refs_7_
  55.0 2.1 %collective-permute-start = (s32[4,6]{1,0:T(4,128)S(1)}, s32[4,6]{1,0:T(4,128)S(1)}, u32[]{:S(2)}, u32[]{:S(2)}) collective-permute-start(s32[4,6]{1,0:T(4,128)S(1)} %pad_add_fusion.tab_ref), channel_id=1, source_target_pairs={{0,8},{8,0},{1,9},{9,1},{2,10},{10,2},{3,11},{11,3},{4,12},{12,4},... | collective-permute-start | bytes 296 | tf_op jit(solution)/shard_map/L_swap/ppermute | solution.py:282
  58.0 1.7 collective-permute-start.15
  59.7 7.9 %collective-permute-done.14.refs_11_ = bf16[8,10240]{1,0:T(8,128)(2,1)S(1)} collective-permute-done((bf16[8,10240]{1,0:T(8,128)(2,1)S(1)}, bf16[8,10240]{1,0:T(8,128)(2,1)S(1)}, u32[]{:S(2)}, u32[]{:S(2)}) %collective-permute-start.14) | collective-permute-done | bytes 163872 | tf_op jit(solution)/shard_map/L_fl/ppermute | solution.py:277
  69.5 11.1 %forward_first.1 = (bf16[8,2,128,128]{3,2,1,0:T(8,128)(2,1)}, bf16[4,8,128,256]{3,2,1,0:T(8,128)(2,1)}, bf16[4,8,128,256]{3,2,1,0:T(8,128)(2,1)}) custom-call(s32[4]{0:T(128)S(1)} %pad_add_fusion.1.pos_ref, s32[128,8]{1,0:T(8,128)S(1)} %copy.16.cols_ref, s32[4,6]{1,0:T(4,128)S(1)} %pad_add_fusion.tab_ref, s32[4,6]{1,0:T(4,128)S(1)} %collective-permute-done.sib_tab_ref, ...), custom_call_target="tpu_custom_call" | custom-call | flops 2147483648 | bytes 16777216 | tf_op jit(solution)/shard_map/forward_first/pallas_call | solution.py:108
  80.6 4.2 %all-to-all-start = ((bf16[8,2,128,128]{3,2,1,0:T(8,128)(2,1)}), bf16[8,2,128,128]{3,2,1,0:T(8,128)(2,1)S(1)}, u32[]{:S(2)}, u32[]{:S(2)}) async-start(bf16[8,2,128,128]{3,2,1,0:T(8,128)(2,1)} %get-tuple-element.46), calls=%async_computation | async-start | bytes 1048576 | tf_op jit(solution)/shard_map/all_to_all | solution.py:322
  86.0 7.3 %all-to-all-done = bf16[8,2,128,128]{3,2,1,0:T(8,128)(2,1)S(1)} async-done(((bf16[8,2,128,128]{3,2,1,0:T(8,128)(2,1)}), bf16[8,2,128,128]{3,2,1,0:T(8,128)(2,1)S(1)}, u32[]{:S(2)}, u32[]{:S(2)}) %all-to-all-start) | async-done | bytes 524320 | tf_op jit(solution)/shard_map/all_to_all | solution.py:322
  93.4 1.3 collective-permute-start.18
  94.8 4.4 %collective-permute-start.19 = (bf16[2,128,128]{2,1,0:T(8,128)(2,1)S(1)}, bf16[2,128,128]{2,1,0:T(8,128)(2,1)S(1)}, u32[]{:S(2)}, u32[]{:S(2)}) collective-permute-start(bf16[2,128,128]{2,1,0:T(8,128)(2,1)S(1)} %tanh_convert_fusion.1), channel_id=1, source_target_pairs={{0,32},{16,48},{32,0},{48,16},{1,33},{17,49},{33,1},{49,17},{2,34}... | collective-permute-start | bytes 196616 | tf_op jit(solution)/shard_map/L_ring/ppermute | solution.py:277
  99.3 2.5 %collective-permute-done.19 = bf16[2,128,128]{2,1,0:T(8,128)(2,1)S(1)} collective-permute-done((bf16[2,128,128]{2,1,0:T(8,128)(2,1)S(1)}, bf16[2,128,128]{2,1,0:T(8,128)(2,1)S(1)}, u32[]{:S(2)}, u32[]{:S(2)}) %collective-permute-start.19) | collective-permute-done | bytes 65568 | tf_op jit(solution)/shard_map/L_ring/ppermute | solution.py:277
  101.8 4.3 %collective-permute-done.20 = bf16[2,128,128]{2,1,0:T(8,128)(2,1)S(1)} collective-permute-done((bf16[2,128,128]{2,1,0:T(8,128)(2,1)S(1)}, bf16[2,128,128]{2,1,0:T(8,128)(2,1)S(1)}, u32[]{:S(2)}, u32[]{:S(2)}) %collective-permute-start.20) | collective-permute-done | bytes 65568 | tf_op jit(solution)/shard_map/L_ring/ppermute | solution.py:277
  106.2 1.2 collective-permute-start.22
  108.2 3.7 %collective-permute-done.21.refs_1_ = bf16[4,2,128,128]{3,2,1,0:T(8,128)(2,1)S(1)} collective-permute-done((bf16[4,2,128,128]{3,2,1,0:T(8,128)(2,1)S(1)}, bf16[4,2,128,128]{3,2,1,0:T(8,128)(2,1)S(1)}, u32[]{:S(2)}, u32[]{:S(2)}) %collective-permute-start.21) | collective-permute-done | bytes 262176 | tf_op jit(solution)/shard_map/L_ring/ppermute | solution.py:277
  113.1 7.0 %collective-permute-done.23.refs_3_ = bf16[4,2,128,128]{3,2,1,0:T(8,128)(2,1)S(1)} collective-permute-done((bf16[4,2,128,128]{3,2,1,0:T(8,128)(2,1)S(1)}, bf16[4,2,128,128]{3,2,1,0:T(8,128)(2,1)S(1)}, u32[]{:S(2)}, u32[]{:S(2)}) %collective-permute-start.23) | collective-permute-done | bytes 262176 | tf_op jit(solution)/shard_map/L_ring/ppermute | solution.py:277
  120.1 5.1 %forward_second.1 = (bf16[8,2,128,128]{3,2,1,0:T(8,128)(2,1)}, bf16[4,4,128,256]{3,2,1,0:T(8,128)(2,1)}, bf16[4,4,128,256]{3,2,1,0:T(8,128)(2,1)}) custom-call(s32[4]{0:T(128)S(1)} %pad_add_fusion.1.pos_ref, s32[4,6]{1,0:T(4,128)S(1)} %pad_add_fusion.tab_ref, s32[4,6]{1,0:T(4,128)S(1)} %collective-permute-done.sib_tab_ref, ...), custom_call_target="tpu_custom_call" | custom-call | flops 1073741824 | bytes 8388608 | tf_op jit(solution)/shard_map/forward_second/pallas_call | solution.py:163
  125.2 5.1 %all-to-all-start.1 = ((bf16[8,2,128,128]{3,2,1,0:T(8,128)(2,1)}), bf16[8,2,128,128]{3,2,1,0:T(8,128)(2,1)S(1)}, u32[]{:S(2)}, u32[]{:S(2)}) async-start(bf16[8,2,128,128]{3,2,1,0:T(8,128)(2,1)} %get-tuple-element.47), calls=%async_computation.1 | async-start | bytes 1048576 | tf_op jit(solution)/shard_map/all_to_all | solution.py:322
  130.3 1.6 collective-permute-start.1
  131.9 5.6 %all-to-all-done.1 = bf16[8,2,128,128]{3,2,1,0:T(8,128)(2,1)S(1)} async-done(((bf16[8,2,128,128]{3,2,1,0:T(8,128)(2,1)}), bf16[8,2,128,128]{3,2,1,0:T(8,128)(2,1)S(1)}, u32[]{:S(2)}, u32[]{:S(2)}) %all-to-all-start.1) | async-done | bytes 524320 | tf_op jit(solution)/shard_map/all_to_all | solution.py:322
  138.6 5.2 %all-to-all-start.2 = ((bf16[8,2,128,128]{3,2,1,0:T(8,128)(2,1)}), bf16[8,2,128,128]{3,2,1,0:T(8,128)(2,1)S(1)}, u32[]{:S(2)}, u32[]{:S(2)}) async-start(bf16[8,2,128,128]{3,2,1,0:T(8,128)(2,1)} %broadcast_in_dim.4), calls=%async_computation.2 | async-start | bytes 1048576 | tf_op jit(solution)/shard_map/all_to_all | solution.py:318
  143.8 1.8 collective-permute-start.34
  145.5 5.5 %all-to-all-done.2.d_ref.refs_0_ = bf16[8,2,128,128]{3,2,1,0:T(8,128)(2,1)S(1)} async-done(((bf16[8,2,128,128]{3,2,1,0:T(8,128)(2,1)}), bf16[8,2,128,128]{3,2,1,0:T(8,128)(2,1)S(1)}, u32[]{:S(2)}, u32[]{:S(2)}) %all-to-all-start.2) | async-done | bytes 524320 | tf_op jit(solution)/shard_map/all_to_all | solution.py:318
  151.0 4.4 %adjoint_second.1 = (bf16[4,2,128,128]{3,2,1,0:T(8,128)(2,1)S(1)}, bf16[4,2,128,128]{3,2,1,0:T(8,128)(2,1)S(1)}, bf16[4,2,128,128]{3,2,1,0:T(8,128)(2,1)S(1)}, bf16[4,2,128,128]{3,2,1,0:T(8,128)(2,1)S(1)}) custom-call(s32[4]{0:T(128)S(1)} %pad_add_fusion.1.pos_ref, s32[4,6]{1,0:T(4,128)S(1)} %pad_add_fusion.tab_ref, ...), custom_call_target="tpu_custom_call" | custom-call | flops 1073741824 | bytes 8388608 | tf_op jit(solution)/shard_map/adjoint_second/pallas_call | solution.py:204
  155.8 2.3 %collective-permute-start.27 = (bf16[4,2,128,128]{3,2,1,0:T(8,128)(2,1)S(1)}, bf16[4,2,128,128]{3,2,1,0:T(8,128)(2,1)S(1)}, u32[]{:S(2)}, u32[]{:S(2)}) collective-permute-start(bf16[4,2,128,128]{3,2,1,0:T(8,128)(2,1)S(1)} %get-tuple-element.51), channel_id=1, source_target_pairs={{0,192},{64,0},{128,64},{192,128},{1,193},{65,1},{129,65},{193,129... | collective-permute-start | bytes 786440 | tf_op jit(solution)/shard_map/L_ring/ppermute | solution.py:277
  158.2 10.7 %collective-permute-done.25.refs_1_ = bf16[4,2,128,128]{3,2,1,0:T(8,128)(2,1)S(1)} collective-permute-done((bf16[4,2,128,128]{3,2,1,0:T(8,128)(2,1)S(1)}, bf16[4,2,128,128]{3,2,1,0:T(8,128)(2,1)S(1)}, u32[]{:S(2)}, u32[]{:S(2)}) %collective-permute-start.25) | collective-permute-done | bytes 262176 | tf_op jit(solution)/shard_map/L_ring/ppermute | solution.py:277
  169.0 4.4 %collective-permute-start.28 = (bf16[2,128,128]{2,1,0:T(8,128)(2,1)S(1)}, bf16[2,128,128]{2,1,0:T(8,128)(2,1)S(1)}, u32[]{:S(2)}, u32[]{:S(2)}) collective-permute-start(bf16[2,128,128]{2,1,0:T(8,128)(2,1)S(1)} %get-tuple-element.53), channel_id=1, source_target_pairs={{0,16},{16,32},{32,48},{48,0},{1,17},{17,33},{33,49},{49,1},{2,18}... | collective-permute-start | bytes 196616 | tf_op jit(solution)/shard_map/L_ring/ppermute | solution.py:277
  173.4 1.5 collective-permute-start.29
  174.9 3.5 %collective-permute-start.30 = (bf16[2,128,128]{2,1,0:T(8,128)(2,1)S(1)}, bf16[2,128,128]{2,1,0:T(8,128)(2,1)S(1)}, u32[]{:S(2)}, u32[]{:S(2)}) collective-permute-start(bf16[2,128,128]{2,1,0:T(8,128)(2,1)S(1)} %get-tuple-element.55), channel_id=1, source_target_pairs={{0,48},{16,0},{32,16},{48,32},{1,49},{17,1},{33,17},{49,33},{2,50}... | collective-permute-start | bytes 196616 | tf_op jit(solution)/shard_map/L_ring/ppermute | solution.py:277
  178.4 3.3 %collective-permute-start.31 = (bf16[4,4,128,256]{3,2,1,0:T(8,128)(2,1)}, bf16[4,4,128,256]{3,2,1,0:T(8,128)(2,1)S(1)}, u32[]{:S(2)}, u32[]{:S(2)}) collective-permute-start(bf16[4,4,128,256]{3,2,1,0:T(8,128)(2,1)} %get-tuple-element.57), channel_id=1, source_target_pairs={{0,8},{8,0},{1,9},{9,1},{2,10},{10,2},{3,11},{11,3},{4,12},{12,4},... | collective-permute-start | bytes 3145736 | tf_op jit(solution)/shard_map/L_swap/ppermute | solution.py:282
  182.6 8.2 %all-to-all-start.3 = ((bf16[16,128,128]{2,1,0:T(8,128)(2,1)}), bf16[16,128,128]{2,1,0:T(8,128)(2,1)S(1)}, u32[]{:S(2)}, u32[]{:S(2)}) async-start(bf16[16,128,128]{2,1,0:T(8,128)(2,1)} %bitcast.18), calls=%async_computation.3 | async-start | bytes 1048576 | tf_op jit(solution)/shard_map/all_to_all | solution.py:384
  194.2 1.2 copy-done.2
  195.4 1.2 copy-done.4
  196.6 2.8 %grad_second.1 = bf16[4,4,256,256]{3,2,1,0:T(8,128)(2,1)} custom-call(s32[4]{0:T(128)S(1)} %pad_add_fusion.1.pos_ref, s32[4,6]{1,0:T(4,128)S(1)} %pad_add_fusion.tab_ref, bf16[4,4,128,256]{3,2,1,0:T(8,128)(2,1)S(1)} %copy-done.2, bf16[4,4,128,256]{3,2,1,0:T(8,128)(2,1)S(1)} %copy-done.4, bf16[8,2,128,128]{3,2,1,0:T(8,128)(2,1)S(1)} %all-to-all-done.2.d_ref.refs_0_, ...), custom_call_target="tpu_custom_call" | custom-call | flops 536870912 | bytes 4194304 | tf_op jit(solution)/shard_map/grad_second/pallas_call | solution.py:257
  199.4 2.0 all-to-all-done.3
  201.4 4.5 %grad_first.1 = bf16[4,8,256,256]{3,2,1,0:T(8,128)(2,1)} custom-call(s32[4]{0:T(128)S(1)} %pad_add_fusion.1.pos_ref, s32[4,6]{1,0:T(4,128)S(1)} %pad_add_fusion.tab_ref, bf16[4,8,128,256]{3,2,1,0:T(8,128)(2,1)S(1)} %copy-done.1, bf16[4,8,128,256]{3,2,1,0:T(8,128)(2,1)} %collective-permute-done.34.po_ref, bf16[2,8,128,128]{3,2,1,0:T(8,128)(2,1)S(1)} %bitcast.40), custom_call_target="tpu_custom_call" | custom-call | flops 1073741824 | bytes 8388608 | tf_op jit(solution)/shard_map/grad_first/pallas_call | solution.py:257
  (112 shorter events, 18.0 us)
Async XLA Ops:
  0.6 16.6 %collective-permute-start.2 = (bf16[8,20480]{1,0:T(8,128)(2,1)}, bf16[8,20480]{1,0:T(8,128)(2,1)S(1)}, u32[]{:S(2)}, u32[]{:S(2)}) collective-permute-start(bf16[8,20480]{1,0:T(8,128)(2,1)} %refs_0_.1), channel_id=1, source_target_pairs={{0,16},{16,32},{32,48},{48,0},{1,17},{17,33},{33,49},{49,1},{2,18}... | collective-permute-start | bytes 983048 | tf_op jit(solution)/shard_map/L_zp/ppermute | solution.py:277
  4.5 19.2 %collective-permute-start.3 = (bf16[8,20480]{1,0:T(8,128)(2,1)}, bf16[8,20480]{1,0:T(8,128)(2,1)S(1)}, u32[]{:S(2)}, u32[]{:S(2)}) collective-permute-start(bf16[8,20480]{1,0:T(8,128)(2,1)} %refs_0_.1), channel_id=1, source_target_pairs={{0,48},{16,0},{32,16},{48,32},{1,49},{17,1},{33,17},{49,33},{2,50}... | collective-permute-start | bytes 983048 | tf_op jit(solution)/shard_map/L_zn/ppermute | solution.py:277
  7.6 16.0 %collective-permute-start.4 = (bf16[8,20480]{1,0:T(8,128)(2,1)}, bf16[8,20480]{1,0:T(8,128)(2,1)S(1)}, u32[]{:S(2)}, u32[]{:S(2)}) collective-permute-start(bf16[8,20480]{1,0:T(8,128)(2,1)} %refs_0_.1), channel_id=1, source_target_pairs={{0,64},{64,128},{128,192},{192,0},{1,65},{65,129},{129,193},{193,1... | collective-permute-start | bytes 983048 | tf_op jit(solution)/shard_map/L_xp/ppermute | solution.py:277
  8.9 14.8 %collective-permute-start.5 = (bf16[8,20480]{1,0:T(8,128)(2,1)}, bf16[8,20480]{1,0:T(8,128)(2,1)S(1)}, u32[]{:S(2)}, u32[]{:S(2)}) collective-permute-start(bf16[8,20480]{1,0:T(8,128)(2,1)} %refs_0_.1), channel_id=1, source_target_pairs={{0,192},{64,0},{128,64},{192,128},{1,193},{65,1},{129,65},{193,129... | collective-permute-start | bytes 983048 | tf_op jit(solution)/shard_map/L_xn/ppermute | solution.py:277
  23.7 24.6 %copy-start.8 = (bf16[8,20480]{1,0:T(8,128)(2,1)}, bf16[8,20480]{1,0:T(8,128)(2,1)S(1)}, u32[]{:S(2)}) copy-start(bf16[8,20480]{1,0:T(8,128)(2,1)S(1)} %collective-permute-done.4.refs_1_) | copy-start | bytes 983044
  23.7 24.6 %copy-start.9 = (bf16[8,20480]{1,0:T(8,128)(2,1)}, bf16[8,20480]{1,0:T(8,128)(2,1)S(1)}, u32[]{:S(2)}) copy-start(bf16[8,20480]{1,0:T(8,128)(2,1)S(1)} %collective-permute-done.5.refs_2_) | copy-start | bytes 983044
  23.8 25.4 %copy-start.5 = (bf16[16,20480]{1,0:T(8,128)(2,1)}, bf16[16,20480]{1,0:T(8,128)(2,1)S(1)}, u32[]{:S(2)}) copy-start(bf16[16,20480]{1,0:T(8,128)(2,1)S(1)} %pad_maximum_fusion.refs_3_) | copy-start | bytes 1966084
  23.8 10.7 %collective-permute-start.8 = (bf16[8,10240]{1,0:T(8,128)(2,1)S(1)}, bf16[8,10240]{1,0:T(8,128)(2,1)S(1)}, u32[]{:S(2)}, u32[]{:S(2)}) collective-permute-start(bf16[8,10240]{1,0:T(8,128)(2,1)S(1)} %slice.30), channel_id=1, source_target_pairs={{0,16},{16,32},{32,48},{48,0},{1,17},{17,33},{33,49},{49,1},{2,18}... | collective-permute-start | bytes 491528 | tf_op jit(solution)/shard_map/L_zl/ppermute | solution.py:277
  27.0 7.5 %collective-permute-start.9 = (bf16[8,10240]{1,0:T(8,128)(2,1)S(1)}, bf16[8,10240]{1,0:T(8,128)(2,1)S(1)}, u32[]{:S(2)}, u32[]{:S(2)}) collective-permute-start(bf16[8,10240]{1,0:T(8,128)(2,1)S(1)} %slice.31), channel_id=1, source_target_pairs={{0,48},{16,0},{32,16},{48,32},{1,49},{17,1},{33,17},{49,33},{2,50}... | collective-permute-start | bytes 491528 | tf_op jit(solution)/shard_map/L_zr/ppermute | solution.py:277
  27.5 41.2 %collective-permute-start.16 = (bf16[4,8,256,256]{3,2,1,0:T(8,128)(2,1)}, bf16[4,8,256,256]{3,2,1,0:T(8,128)(2,1)}, u32[]{:S(2)}, u32[]{:S(2)}) collective-permute-start(bf16[4,8,256,256]{3,2,1,0:T(8,128)(2,1)} %refs_13_.1), channel_id=1, source_target_pairs={{0,8},{8,0},{1,9},{9,1},{2,10},{10,2},{3,11},{11,3},{4,12},{12,4},... | collective-permute-start | bytes 12582920 | tf_op jit(solution)/shard_map/L_swap/ppermute | solution.py:282
  29.0 17.6 %collective-permute-start.6 = (bf16[16,20480]{1,0:T(8,128)(2,1)S(1)}, bf16[16,20480]{1,0:T(8,128)(2,1)S(1)}, u32[]{:S(2)}, u32[]{:S(2)}) collective-permute-start(bf16[16,20480]{1,0:T(8,128)(2,1)S(1)} %pad_maximum_fusion.refs_3_), channel_id=1, source_target_pairs={{0,64},{64,128},{128,192},{192,0},{1,65},{65,129},{129,193},{193,1... | collective-permute-start | bytes 1966088 | tf_op jit(solution)/shard_map/L_tp/ppermute | solution.py:277
  30.2 16.4 %collective-permute-start.7 = (bf16[16,20480]{1,0:T(8,128)(2,1)S(1)}, bf16[16,20480]{1,0:T(8,128)(2,1)S(1)}, u32[]{:S(2)}, u32[]{:S(2)}) collective-permute-start(bf16[16,20480]{1,0:T(8,128)(2,1)S(1)} %pad_maximum_fusion.refs_3_), channel_id=1, source_target_pairs={{0,192},{64,0},{128,64},{192,128},{1,193},{65,1},{129,65},{193,129... | collective-permute-start | bytes 1966088 | tf_op jit(solution)/shard_map/L_tn/ppermute | solution.py:277
  31.7 23.0 %copy-start.17 = (s32[4,1]{0,1:T(1,128)S(1)}, s32[4,1]{0,1:T(1,128)}, u32[]{:S(2)}) copy-start(s32[4,1]{0,1:T(1,128)} %param.12) | copy-start | bytes 52
  31.7 23.1 %copy-start.18 = (s32[4,1]{0,1:T(1,128)S(1)}, s32[4,1]{0,1:T(1,128)}, u32[]{:S(2)}) copy-start(s32[4,1]{0,1:T(1,128)} %param.16) | copy-start | bytes 52
  31.7 23.1 %copy-start.16 = (s32[4,4]{1,0:T(4,128)S(1)}, s32[4,4]{1,0:T(4,128)}, u32[]{:S(2)}) copy-start(s32[4,4]{1,0:T(4,128)} %param.15) | copy-start | bytes 196
  34.5 33.1 %copy-start = (bf16[4,4,256,256]{3,2,1,0:T(8,128)(2,1)S(1)}, bf16[4,4,256,256]{3,2,1,0:T(8,128)(2,1)}, u32[]{:S(2)}) copy-start(bf16[4,4,256,256]{3,2,1,0:T(8,128)(2,1)} %own_ref.1) | copy-start | bytes 6291460
  34.6 34.0 %copy-start.15 = (s32[128,8]{0,1:T(8,128)S(1)}, s32[128,8]{0,1:T(8,128)}, u32[]{:S(2)}) copy-start(s32[128,8]{0,1:T(8,128)} %param.11) | copy-start | bytes 12292
  34.6 19.0 %collective-permute-start.10 = (bf16[8,20480]{1,0:T(8,128)(2,1)S(1)}, bf16[8,20480]{1,0:T(8,128)(2,1)S(1)}, u32[]{:S(2)}, u32[]{:S(2)}) collective-permute-start(bf16[8,20480]{1,0:T(8,128)(2,1)S(1)} %constant_dynamic-update-slice_fusion.refs_6_), channel_id=1, source_target_pairs={{0,64},{64,128},{128,192},{192,0},{1,65},{65,129},{129,193},{193,1... | collective-permute-start | bytes 983048 | tf_op jit(solution)/shard_map/L_fp/ppermute | solution.py:277
  35.9 17.7 %collective-permute-start.11 = (bf16[8,20480]{1,0:T(8,128)(2,1)S(1)}, bf16[8,20480]{1,0:T(8,128)(2,1)}, u32[]{:S(2)}, u32[]{:S(2)}) collective-permute-start(bf16[8,20480]{1,0:T(8,128)(2,1)S(1)} %constant_dynamic-update-slice_fusion.refs_6_), channel_id=1, source_target_pairs={{0,192},{64,0},{128,64},{192,128},{1,193},{65,1},{129,65},{193,129... | collective-permute-start | bytes 983048 | tf_op jit(solution)/shard_map/L_fn/ppermute | solution.py:277
  48.3 20.3 %collective-permute-start.12 = (bf16[24,10240]{1,0:T(8,128)(2,1)}, bf16[24,10240]{1,0:T(8,128)(2,1)}, u32[]{:S(2)}, u32[]{:S(2)}) collective-permute-start(bf16[24,10240]{1,0:T(8,128)(2,1)} %pad_maximum_fusion.1), channel_id=1, source_target_pairs={{0,64},{64,128},{128,192},{192,0},{1,65},{65,129},{129,193},{193,1... | collective-permute-start | bytes 1474568 | tf_op jit(solution)/shard_map/L_ol/ppermute | solution.py:277
  49.2 19.4 %collective-permute-start.13 = (bf16[24,10240]{1,0:T(8,128)(2,1)}, bf16[24,10240]{1,0:T(8,128)(2,1)S(1)}, u32[]{:S(2)}, u32[]{:S(2)}) collective-permute-start(bf16[24,10240]{1,0:T(8,128)(2,1)} %pad_maximum_fusion.2), channel_id=1, source_target_pairs={{0,192},{64,0},{128,64},{192,128},{1,193},{65,1},{129,65},{193,129... | collective-permute-start | bytes 1474568 | tf_op jit(solution)/shard_map/L_oh/ppermute | solution.py:277
  53.6 14.0 %collective-permute-start.14 = (bf16[8,10240]{1,0:T(8,128)(2,1)S(1)}, bf16[8,10240]{1,0:T(8,128)(2,1)S(1)}, u32[]{:S(2)}, u32[]{:S(2)}) collective-permute-start(bf16[8,10240]{1,0:T(8,128)(2,1)S(1)} %slice.36), channel_id=1, source_target_pairs={{0,64},{64,128},{128,192},{192,0},{1,65},{65,129},{129,193},{193,1... | collective-permute-start | bytes 491528 | tf_op jit(solution)/shard_map/L_fl/ppermute | solution.py:277
  55.0 3.0 %collective-permute-start = (s32[4,6]{1,0:T(4,128)S(1)}, s32[4,6]{1,0:T(4,128)S(1)}, u32[]{:S(2)}, u32[]{:S(2)}) collective-permute-start(s32[4,6]{1,0:T(4,128)S(1)} %pad_add_fusion.tab_ref), channel_id=1, source_target_pairs={{0,8},{8,0},{1,9},{9,1},{2,10},{10,2},{3,11},{11,3},{4,12},{12,4},... | collective-permute-start | bytes 296 | tf_op jit(solution)/shard_map/L_swap/ppermute | solution.py:282
  58.0 10.6 %collective-permute-start.15 = (bf16[8,10240]{1,0:T(8,128)(2,1)S(1)}, bf16[8,10240]{1,0:T(8,128)(2,1)}, u32[]{:S(2)}, u32[]{:S(2)}) collective-permute-start(bf16[8,10240]{1,0:T(8,128)(2,1)S(1)} %slice.37), channel_id=1, source_target_pairs={{0,192},{64,0},{128,64},{192,128},{1,193},{65,1},{129,65},{193,129... | collective-permute-start | bytes 491528 | tf_op jit(solution)/shard_map/L_fh/ppermute | solution.py:277
  67.6 40.6 %collective-permute-start.24 = (bf16[4,4,256,256]{3,2,1,0:T(8,128)(2,1)S(1)}, bf16[4,4,256,256]{3,2,1,0:T(8,128)(2,1)}, u32[]{:S(2)}, u32[]{:S(2)}) collective-permute-start(bf16[4,4,256,256]{3,2,1,0:T(8,128)(2,1)S(1)} %copy-done), channel_id=1, source_target_pairs={{0,8},{8,0},{1,9},{9,1},{2,10},{10,2},{3,11},{11,3},{4,12},{12,4},... | collective-permute-start | bytes 6291464 | tf_op jit(solution)/shard_map/L_swap/ppermute | solution.py:282
  80.6 12.8 %all-to-all-start = ((bf16[8,2,128,128]{3,2,1,0:T(8,128)(2,1)}), bf16[8,2,128,128]{3,2,1,0:T(8,128)(2,1)S(1)}, u32[]{:S(2)}, u32[]{:S(2)}) async-start(bf16[8,2,128,128]{3,2,1,0:T(8,128)(2,1)} %get-tuple-element.46), calls=%async_computation | async-start | bytes 1048576 | tf_op jit(solution)/shard_map/all_to_all | solution.py:322
  84.8 1.2 collective-permute-start.17
  93.4 5.8 %collective-permute-start.18 = (bf16[2,128,128]{2,1,0:T(8,128)(2,1)S(1)}, bf16[2,128,128]{2,1,0:T(8,128)(2,1)S(1)}, u32[]{:S(2)}, u32[]{:S(2)}) collective-permute-start(bf16[2,128,128]{2,1,0:T(8,128)(2,1)S(1)} %tanh_convert_fusion.1), channel_id=1, source_target_pairs={{0,48},{16,0},{32,16},{48,32},{1,49},{17,1},{33,17},{49,33},{2,50}... | collective-permute-start | bytes 196616 | tf_op jit(solution)/shard_map/L_ring/ppermute | solution.py:277
  94.8 7.0 %collective-permute-start.19 = (bf16[2,128,128]{2,1,0:T(8,128)(2,1)S(1)}, bf16[2,128,128]{2,1,0:T(8,128)(2,1)S(1)}, u32[]{:S(2)}, u32[]{:S(2)}) collective-permute-start(bf16[2,128,128]{2,1,0:T(8,128)(2,1)S(1)} %tanh_convert_fusion.1), channel_id=1, source_target_pairs={{0,32},{16,48},{32,0},{48,16},{1,33},{17,49},{33,1},{49,17},{2,34}... | collective-permute-start | bytes 196616 | tf_op jit(solution)/shard_map/L_ring/ppermute | solution.py:277
  99.1 6.9 %collective-permute-start.20 = (bf16[2,128,128]{2,1,0:T(8,128)(2,1)S(1)}, bf16[2,128,128]{2,1,0:T(8,128)(2,1)S(1)}, u32[]{:S(2)}, u32[]{:S(2)}) collective-permute-start(bf16[2,128,128]{2,1,0:T(8,128)(2,1)S(1)} %tanh_convert_fusion.1), channel_id=1, source_target_pairs={{0,16},{16,32},{32,48},{48,0},{1,17},{17,33},{33,49},{49,1},{2,18}... | collective-permute-start | bytes 196616 | tf_op jit(solution)/shard_map/L_ring/ppermute | solution.py:277
  106.1 24.2 %copy-start.14 = (bf16[256,128]{1,0:T(8,128)(2,1)S(1)}, bf16[256,128]{1,0:T(8,128)(2,1)}, u32[]{:S(2)}) copy-start(bf16[256,128]{1,0:T(8,128)(2,1)} %param.19) | copy-start | bytes 196612
  106.1 5.8 %collective-permute-start.21 = (bf16[4,2,128,128]{3,2,1,0:T(8,128)(2,1)S(1)}, bf16[4,2,128,128]{3,2,1,0:T(8,128)(2,1)S(1)}, u32[]{:S(2)}, u32[]{:S(2)}) collective-permute-start(bf16[4,2,128,128]{3,2,1,0:T(8,128)(2,1)S(1)} %pad_maximum_fusion.3.refs_0_), channel_id=1, source_target_pairs={{0,192},{64,0},{128,64},{192,128},{1,193},{65,1},{129,65},{193,129... | collective-permute-start | bytes 786440 | tf_op jit(solution)/shard_map/L_ring/ppermute | solution.py:277
  106.2 6.9 %collective-permute-start.22 = (bf16[4,2,128,128]{3,2,1,0:T(8,128)(2,1)S(1)}, bf16[4,2,128,128]{3,2,1,0:T(8,128)(2,1)S(1)}, u32[]{:S(2)}, u32[]{:S(2)}) collective-permute-start(bf16[4,2,128,128]{3,2,1,0:T(8,128)(2,1)S(1)} %pad_maximum_fusion.3.refs_0_), channel_id=1, source_target_pairs={{0,128},{64,192},{128,0},{192,64},{1,129},{65,193},{129,1},{193,65... | collective-permute-start | bytes 786440 | tf_op jit(solution)/shard_map/L_ring/ppermute | solution.py:277
  107.5 12.6 %collective-permute-start.23 = (bf16[4,2,128,128]{3,2,1,0:T(8,128)(2,1)S(1)}, bf16[4,2,128,128]{3,2,1,0:T(8,128)(2,1)S(1)}, u32[]{:S(2)}, u32[]{:S(2)}) collective-permute-start(bf16[4,2,128,128]{3,2,1,0:T(8,128)(2,1)S(1)} %pad_maximum_fusion.3.refs_0_), channel_id=1, source_target_pairs={{0,64},{64,128},{128,192},{192,0},{1,65},{65,129},{129,193},{193,1... | collective-permute-start | bytes 786440 | tf_op jit(solution)/shard_map/L_ring/ppermute | solution.py:277
  125.2 12.3 %all-to-all-start.1 = ((bf16[8,2,128,128]{3,2,1,0:T(8,128)(2,1)}), bf16[8,2,128,128]{3,2,1,0:T(8,128)(2,1)S(1)}, u32[]{:S(2)}, u32[]{:S(2)}) async-start(bf16[8,2,128,128]{3,2,1,0:T(8,128)(2,1)} %get-tuple-element.47), calls=%async_computation.1 | async-start | bytes 1048576 | tf_op jit(solution)/shard_map/all_to_all | solution.py:322
  130.3 7.3 %collective-permute-start.1 = (bf16[16,8,128]{2,1,0:T(8,128)(2,1)S(1)}, bf16[16,8,128]{2,1,0:T(8,128)(2,1)S(1)}, u32[]{:S(2)}, u32[]{:S(2)}) collective-permute-start(bf16[16,8,128]{2,1,0:T(8,128)(2,1)S(1)} %get-tuple-element.68), channel_id=1, source_target_pairs={{0,8},{8,0},{1,9},{9,1},{2,10},{10,2},{3,11},{11,3},{4,12},{12,4},... | collective-permute-start | bytes 98312 | tf_op jit(solution)/shard_map/L_swap/ppermute | solution.py:282
  138.6 12.4 %all-to-all-start.2 = ((bf16[8,2,128,128]{3,2,1,0:T(8,128)(2,1)}), bf16[8,2,128,128]{3,2,1,0:T(8,128)(2,1)S(1)}, u32[]{:S(2)}, u32[]{:S(2)}) async-start(bf16[8,2,128,128]{3,2,1,0:T(8,128)(2,1)} %broadcast_in_dim.4), calls=%async_computation.2 | async-start | bytes 1048576 | tf_op jit(solution)/shard_map/all_to_all | solution.py:318
  143.8 57.6 %collective-permute-start.34 = (bf16[4,8,128,256]{3,2,1,0:T(8,128)(2,1)}, bf16[4,8,128,256]{3,2,1,0:T(8,128)(2,1)}, u32[]{:S(2)}, u32[]{:S(2)}) collective-permute-start(bf16[4,8,128,256]{3,2,1,0:T(8,128)(2,1)} %get-tuple-element.60), channel_id=1, source_target_pairs={{0,8},{8,0},{1,9},{9,1},{2,10},{10,2},{3,11},{11,3},{4,12},{12,4},... | collective-permute-start | bytes 6291464 | tf_op jit(solution)/shard_map/L_swap/ppermute | solution.py:282
  155.4 13.4 %collective-permute-start.25 = (bf16[4,2,128,128]{3,2,1,0:T(8,128)(2,1)S(1)}, bf16[4,2,128,128]{3,2,1,0:T(8,128)(2,1)S(1)}, u32[]{:S(2)}, u32[]{:S(2)}) collective-permute-start(bf16[4,2,128,128]{3,2,1,0:T(8,128)(2,1)S(1)} %get-tuple-element.49), channel_id=1, source_target_pairs={{0,64},{64,128},{128,192},{192,0},{1,65},{65,129},{129,193},{193,1... | collective-permute-start | bytes 786440 | tf_op jit(solution)/shard_map/L_ring/ppermute | solution.py:277
  155.5 13.3 %collective-permute-start.26 = (bf16[4,2,128,128]{3,2,1,0:T(8,128)(2,1)S(1)}, bf16[4,2,128,128]{3,2,1,0:T(8,128)(2,1)S(1)}, u32[]{:S(2)}, u32[]{:S(2)}) collective-permute-start(bf16[4,2,128,128]{3,2,1,0:T(8,128)(2,1)S(1)} %get-tuple-element.50), channel_id=1, source_target_pairs={{0,128},{64,192},{128,0},{192,64},{1,129},{65,193},{129,1},{193,65... | collective-permute-start | bytes 786440 | tf_op jit(solution)/shard_map/L_ring/ppermute | solution.py:277
  155.8 13.0 %collective-permute-start.27 = (bf16[4,2,128,128]{3,2,1,0:T(8,128)(2,1)S(1)}, bf16[4,2,128,128]{3,2,1,0:T(8,128)(2,1)S(1)}, u32[]{:S(2)}, u32[]{:S(2)}) collective-permute-start(bf16[4,2,128,128]{3,2,1,0:T(8,128)(2,1)S(1)} %get-tuple-element.51), channel_id=1, source_target_pairs={{0,192},{64,0},{128,64},{192,128},{1,193},{65,1},{129,65},{193,129... | collective-permute-start | bytes 786440 | tf_op jit(solution)/shard_map/L_ring/ppermute | solution.py:277
  169.0 12.7 %collective-permute-start.28 = (bf16[2,128,128]{2,1,0:T(8,128)(2,1)S(1)}, bf16[2,128,128]{2,1,0:T(8,128)(2,1)S(1)}, u32[]{:S(2)}, u32[]{:S(2)}) collective-permute-start(bf16[2,128,128]{2,1,0:T(8,128)(2,1)S(1)} %get-tuple-element.53), channel_id=1, source_target_pairs={{0,16},{16,32},{32,48},{48,0},{1,17},{17,33},{33,49},{49,1},{2,18}... | collective-permute-start | bytes 196616 | tf_op jit(solution)/shard_map/L_ring/ppermute | solution.py:277
  173.4 8.3 %collective-permute-start.29 = (bf16[2,128,128]{2,1,0:T(8,128)(2,1)S(1)}, bf16[2,128,128]{2,1,0:T(8,128)(2,1)S(1)}, u32[]{:S(2)}, u32[]{:S(2)}) collective-permute-start(bf16[2,128,128]{2,1,0:T(8,128)(2,1)S(1)} %get-tuple-element.54), channel_id=1, source_target_pairs={{0,32},{16,48},{32,0},{48,16},{1,33},{17,49},{33,1},{49,17},{2,34}... | collective-permute-start | bytes 196616 | tf_op jit(solution)/shard_map/L_ring/ppermute | solution.py:277
  174.9 6.8 %collective-permute-start.30 = (bf16[2,128,128]{2,1,0:T(8,128)(2,1)S(1)}, bf16[2,128,128]{2,1,0:T(8,128)(2,1)S(1)}, u32[]{:S(2)}, u32[]{:S(2)}) collective-permute-start(bf16[2,128,128]{2,1,0:T(8,128)(2,1)S(1)} %get-tuple-element.55), channel_id=1, source_target_pairs={{0,48},{16,0},{32,16},{48,32},{1,49},{17,1},{33,17},{49,33},{2,50}... | collective-permute-start | bytes 196616 | tf_op jit(solution)/shard_map/L_ring/ppermute | solution.py:277
  178.4 14.8 %collective-permute-start.31 = (bf16[4,4,128,256]{3,2,1,0:T(8,128)(2,1)}, bf16[4,4,128,256]{3,2,1,0:T(8,128)(2,1)S(1)}, u32[]{:S(2)}, u32[]{:S(2)}) collective-permute-start(bf16[4,4,128,256]{3,2,1,0:T(8,128)(2,1)} %get-tuple-element.57), channel_id=1, source_target_pairs={{0,8},{8,0},{1,9},{9,1},{2,10},{10,2},{3,11},{11,3},{4,12},{12,4},... | collective-permute-start | bytes 3145736 | tf_op jit(solution)/shard_map/L_swap/ppermute | solution.py:282
  182.6 18.8 %all-to-all-start.3 = ((bf16[16,128,128]{2,1,0:T(8,128)(2,1)}), bf16[16,128,128]{2,1,0:T(8,128)(2,1)S(1)}, u32[]{:S(2)}, u32[]{:S(2)}) async-start(bf16[16,128,128]{2,1,0:T(8,128)(2,1)} %bitcast.18), calls=%async_computation.3 | async-start | bytes 1048576 | tf_op jit(solution)/shard_map/all_to_all | solution.py:384
  190.9 3.3 %collective-permute-start.32 = (bf16[8,128,128]{2,1,0:T(8,128)(2,1)S(1)}, bf16[8,128,128]{2,1,0:T(8,128)(2,1)S(1)}, u32[]{:S(2)}, u32[]{:S(2)}) collective-permute-start(bf16[8,128,128]{2,1,0:T(8,128)(2,1)S(1)} %dynamic-slice_bitcast_fusion), channel_id=1, source_target_pairs={{0,8},{8,0},{1,9},{9,1},{2,10},{10,2},{3,11},{11,3},{4,12},{12,4},... | collective-permute-start | bytes 786440 | tf_op jit(solution)/shard_map/L_swap/ppermute | solution.py:282
  191.1 1.5 collective-permute-start.33
  (12 other events, 81.8 us)

commit v3 on v2

--- a/solution.py
+++ b/solution.py
@@ -286,31 +286,32 @@
     return lax.optimization_barrier(values)
 
 
-def gather_slopes(s):
+def gather_slopes(s, early):
     half = s.shape[1] // 2
     zp, zn = ring(s, "zh", 1, "zp"), ring(s, "zh", -1, "zn")
     xp, xn = ring(s, "x", 1, "xp"), ring(s, "x", -1, "xn")
-    zp, zn, xp, xn = together(zp, zn, xp, xn)
+    xp, xn = together(xp, xn)
+    xl, xh = ring(xp[:, :half], "x", 1, "xl"), ring(xn[:, half:], "x", -1, "xh")
+    zp, zn, xl, xh, early = together(zp, zn, xl, xh, early)
     zps, zns = zp[:, :half], zn[:, half:]
     t = jnp.concatenate([zp, zn], axis=0)
     zps, zns, t = together(zps, zns, t)
     zl, zr = ring(zps, "zh", 1, "zl"), ring(zns, "zh", -1, "zr")
     tp, tn = ring(t, "x", 1, "tp"), ring(t, "x", -1, "tn")
-    zl, zr = together(zl, zr)
+    w = jnp.concatenate([xl, xh], axis=1)
+    zl, zr, w = together(zl, zr, w)
+    wp, wn = ring(w, "zh", 1, "wp"), ring(w, "zh", -1, "wn")
     f = jnp.concatenate([zl, zr], axis=1)
+    f, tp, tn = together(f, tp, tn)
     fp, fn = ring(f, "x", 1, "fp"), ring(f, "x", -1, "fn")
-    tp, tn = together(tp, tn)
-    ol = jnp.concatenate([xp[:, :half], tp[:, :half]], axis=0)
-    oh = jnp.concatenate([xn[:, half:], tn[:, half:]], axis=0)
-    ol, oh = ring(ol, "x", 1, "ol"), ring(oh, "x", -1, "oh")
-    fp, fn = together(fp, fn)
+    fp, fn, wp, wn = together(fp, fn, wp, wn)
     fl, fh = ring(fp[:, :half], "x", 1, "fl"), ring(fn[:, half:], "x", -1, "fh")
-    pieces = [(s, [(0, 0)], 0), (xp, [(-1, 0)], 0), (xn, [(1, 0)], 0)]
+    pieces = [(s, [(0, 0)], 0), (xp, [(-1, 0)], 0), (xn, [(1, 0)], 0), (w, [(2, 0)], 0)]
     pieces += [(t, [(0, -1), (0, 1)], 0), (tp, [(-1, -1), (-1, 1)], 0), (tn, [(1, -1), (1, 1)], 0)]
+    pieces += [(wp, [(2, -1)], 0), (wn, [(2, 1)], 0)]
     pieces += [(f, [(0, 2)], 0), (fp, [(-1, 2)], 0), (fn, [(1, 2)], 0)]
-    pieces += [(a, [(2, 0), (2, -1), (2, 1)], first) for a, first in ((ol, 0), (oh, half))]
     pieces += [(fl, [(2, 2)], 0), (fh, [(2, 2)], half)]
-    return pieces
+    return pieces, early
 
 
 def gather_axis(value, axis):
@@ -345,8 +346,7 @@
     def canonical(mine, other):
         return jnp.where(core == 0, jnp.stack([mine, other]), jnp.stack([other, mine]))
 
-    pieces = gather_slopes(slopes)
-    sibling_first = swap(weight_first)
+    pieces, sibling_first = gather_slopes(slopes, swap(weight_first, "w1"))
     sibling_second = swap(weight_second)
     table = jnp.concatenate([count_first, count_second, cols_second], axis=1)
     sib_table = swap(table)

time: 208 us -> 200 us (0.962)
  waiting for transfers between devices: 86.7 us -> 60.4 us
  starting transfers between devices: 78.9 us -> 98 us
  local copies, waits for them, and re-layouts: 8.31 us -> 10.7 us
    ppermute x9, starting transfers between devices: 12.1 us -> 33.1 us  [swap(): return lax.ppermute(value, 'core', [(0, 1), (1, 0)])]
    ppermute x26 -> x28, waiting for transfers between devices: 64.4 us -> 49.6 us  [ring(): return lax.ppermute(value, axis, [(i, (i + step) % n) for i in range(n)])]
    all_to_all x2, waiting for transfers between devices: 12.9 us -> 4.05 us  [sum_axis(): lax.all_to_all(parts, axis, 0, 0, tiled=True).astype(F32)]
    all_to_all x1, waiting for transfers between devices: 5.46 us -> 1.56 us  [gather_axis(): lax.all_to_all(jnp.broadcast_to(value[None], (n, *value.shape)), axis, 0,...]
    unnamed x46 -> x43, local copies, waits for them, and re-layouts: 5.41 us -> 6.87 us
    ppermute x26 -> x28, starting transfers between devices: 44.2 us -> 43.6 us  [ring(): return lax.ppermute(value, axis, [(i, (i + step) % n) for i in range(n)])]
  transfers between devices with their start and end apart: 39 -> 41, of which waited for: 18 -> 20; matrix products, arithmetic and copies ran while one was open for 2% -> 2% of each run, Pallas kernels for 9% -> 9%
where the time goes in v3:
time: 200 us
  starting transfers between devices  98 us (49%)
  waiting for transfers between devices  60.4 us (30%)
  Pallas kernels  28.1 us (14%)
  local copies, waits for them, and re-layouts  10.7 us (5%)
    ppermute x28, waiting for transfers between devices, ring(): return lax.ppermute(value, axis, [(i, (i + step) % n) for i in range(n)])  49.6 us
    ppermute x28, starting transfers between devices, ring(): return lax.ppermute(value, axis, [(i, (i + step) % n) for i in range(n)])  43.6 us
    ppermute x9, starting transfers between devices, swap(): return lax.ppermute(value, 'core', [(0, 1), (1, 0)])  33.1 us
    pallas_call x1, Pallas kernels, forward_first(): pl.pallas_call(body, out_shape=(jax.ShapeDtypeStruct((2 * ROWS, 2, frames...  11.1 us
    all_to_all x2, starting transfers between devices, sum_axis(): lax.all_to_all(parts, axis, 0, 0, tiled=True).astype(F32)  8.89 us
    pallas_call x2, Pallas kernels, weight_grads(): pl.pallas_call(body, out_shape=jax.ShapeDtypeStruct((ROWS, slots, BLK, BL...  7.31 us
    all_to_all x1, starting transfers between devices, shards(): lax.all_to_all(to_all.reshape(-1, *delta_first.shape[1:]), ('core', *IN),...  7.02 us
    unnamed x43, local copies, waits for them, and re-layouts  6.87 us
  transfers between devices with their start and end apart: 41, of which 20 were waited for; matrix products, arithmetic and copies ran while one was open for 2% of the time, Pallas kernels for 9%

profile of v3, /device:TPU:1, one launch (start us, length us, event | category | flops | bytes accessed | tf_op | source)
XLA Modules:
  0.0 199.5 jit_solution(12675164879459042529)
XLA Ops:
  0.7 3.3 %collective-permute-start.8 = (bf16[4,8,256,256]{3,2,1,0:T(8,128)(2,1)}, bf16[4,8,256,256]{3,2,1,0:T(8,128)(2,1)}, u32[]{:S(2)}, u32[]{:S(2)}) collective-permute-start(bf16[4,8,256,256]{3,2,1,0:T(8,128)(2,1)} %refs_14_.1), channel_id=1, source_target_pairs={{0,8},{8,0},{1,9},{9,1},{2,10},{10,2},{3,11},{11,3},{4,12},{12,4},... | collective-permute-start | bytes 12582920 | tf_op jit(solution)/shard_map/L_w1/ppermute | solution.py:282
  4.0 2.7 %collective-permute-start.3 = (bf16[8,20480]{1,0:T(8,128)(2,1)}, bf16[8,20480]{1,0:T(8,128)(2,1)S(1)}, u32[]{:S(2)}, u32[]{:S(2)}) collective-permute-start(bf16[8,20480]{1,0:T(8,128)(2,1)} %refs_0_.1), channel_id=1, source_target_pairs={{0,192},{64,0},{128,64},{192,128},{1,193},{65,1},{129,65},{193,129... | collective-permute-start | bytes 983048 | tf_op jit(solution)/shard_map/L_xn/ppermute | solution.py:277
  6.7 1.3 collective-permute-start.4
  7.9 3.0 %collective-permute-start.5 = (bf16[8,20480]{1,0:T(8,128)(2,1)}, bf16[8,20480]{1,0:T(8,128)(2,1)S(1)}, u32[]{:S(2)}, u32[]{:S(2)}) collective-permute-start(bf16[8,20480]{1,0:T(8,128)(2,1)} %refs_0_.1), channel_id=1, source_target_pairs={{0,48},{16,0},{32,16},{48,32},{1,49},{17,1},{33,17},{49,33},{2,50}... | collective-permute-start | bytes 983048 | tf_op jit(solution)/shard_map/L_zn/ppermute | solution.py:277
  11.0 3.7 %collective-permute-done.2.refs_1_ = bf16[8,20480]{1,0:T(8,128)(2,1)S(1)} collective-permute-done((bf16[8,20480]{1,0:T(8,128)(2,1)}, bf16[8,20480]{1,0:T(8,128)(2,1)S(1)}, u32[]{:S(2)}, u32[]{:S(2)}) %collective-permute-start.2) | collective-permute-done | bytes 327712 | tf_op jit(solution)/shard_map/L_xp/ppermute | solution.py:277
  14.8 2.7 %collective-permute-start.7 = (bf16[8,10240]{1,0:T(8,128)(2,1)S(1)}, bf16[8,10240]{1,0:T(8,128)(2,1)S(1)}, u32[]{:S(2)}, u32[]{:S(2)}) collective-permute-start(bf16[8,10240]{1,0:T(8,128)(2,1)S(1)} %slice.25), channel_id=1, source_target_pairs={{0,192},{64,0},{128,64},{192,128},{1,193},{65,1},{129,65},{193,129... | collective-permute-start | bytes 491528 | tf_op jit(solution)/shard_map/L_xh/ppermute | solution.py:277
  17.6 3.1 %collective-permute-done.4 = bf16[8,20480]{1,0:T(8,128)(2,1)S(1)} collective-permute-done((bf16[8,20480]{1,0:T(8,128)(2,1)}, bf16[8,20480]{1,0:T(8,128)(2,1)S(1)}, u32[]{:S(2)}, u32[]{:S(2)}) %collective-permute-start.4) | collective-permute-done | bytes 327712 | tf_op jit(solution)/shard_map/L_zp/ppermute | solution.py:277
  20.7 6.4 %collective-permute-done.5 = bf16[8,20480]{1,0:T(8,128)(2,1)S(1)} collective-permute-done((bf16[8,20480]{1,0:T(8,128)(2,1)}, bf16[8,20480]{1,0:T(8,128)(2,1)S(1)}, u32[]{:S(2)}, u32[]{:S(2)}) %collective-permute-start.5) | collective-permute-done | bytes 327712 | tf_op jit(solution)/shard_map/L_zn/ppermute | solution.py:277
  28.0 1.9 collective-permute-start.12
  30.0 2.4 %collective-permute-start.10 = (bf16[8,10240]{1,0:T(8,128)(2,1)S(1)}, bf16[8,10240]{1,0:T(8,128)(2,1)S(1)}, u32[]{:S(2)}, u32[]{:S(2)}) collective-permute-start(bf16[8,10240]{1,0:T(8,128)(2,1)S(1)} %slice.27), channel_id=1, source_target_pairs={{0,48},{16,0},{32,16},{48,32},{1,49},{17,1},{33,17},{49,33},{2,50}... | collective-permute-start | bytes 491528 | tf_op jit(solution)/shard_map/L_zr/ppermute | solution.py:277
  33.1 3.4 %collective-permute-done.10 = bf16[8,10240]{1,0:T(8,128)(2,1)S(1)} collective-permute-done((bf16[8,10240]{1,0:T(8,128)(2,1)S(1)}, bf16[8,10240]{1,0:T(8,128)(2,1)S(1)}, u32[]{:S(2)}, u32[]{:S(2)}) %collective-permute-start.10) | collective-permute-done | bytes 163872 | tf_op jit(solution)/shard_map/L_zr/ppermute | solution.py:277
  36.4 2.3 %collective-permute-done.9 = bf16[8,10240]{1,0:T(8,128)(2,1)S(1)} collective-permute-done((bf16[8,10240]{1,0:T(8,128)(2,1)S(1)}, bf16[8,10240]{1,0:T(8,128)(2,1)S(1)}, u32[]{:S(2)}, u32[]{:S(2)}) %collective-permute-start.9) | collective-permute-done | bytes 163872 | tf_op jit(solution)/shard_map/L_zl/ppermute | solution.py:277
  38.7 2.5 %collective-permute-start.15 = (bf16[8,20480]{1,0:T(8,128)(2,1)S(1)}, bf16[8,20480]{1,0:T(8,128)(2,1)}, u32[]{:S(2)}, u32[]{:S(2)}) collective-permute-start(bf16[8,20480]{1,0:T(8,128)(2,1)S(1)} %pad_maximum_fusion.1.refs_3_), channel_id=1, source_target_pairs={{0,16},{16,32},{32,48},{48,0},{1,17},{17,33},{33,49},{49,1},{2,18}... | collective-permute-start | bytes 983048 | tf_op jit(solution)/shard_map/L_wp/ppermute | solution.py:277
  42.3 1.4 collective-permute-done.11.refs_5_
  45.5 1.8 collective-permute-start.14
  47.5 9.3 %collective-permute-done.15.refs_7_ = bf16[8,20480]{1,0:T(8,128)(2,1)} collective-permute-done((bf16[8,20480]{1,0:T(8,128)(2,1)S(1)}, bf16[8,20480]{1,0:T(8,128)(2,1)}, u32[]{:S(2)}, u32[]{:S(2)}) %collective-permute-start.15) | collective-permute-done | bytes 327712 | tf_op jit(solution)/shard_map/L_wp/ppermute | solution.py:277
  59.0 2.7 %collective-permute-start.18 = (bf16[8,10240]{1,0:T(8,128)(2,1)S(1)}, bf16[8,10240]{1,0:T(8,128)(2,1)S(1)}, u32[]{:S(2)}, u32[]{:S(2)}) collective-permute-start(bf16[8,10240]{1,0:T(8,128)(2,1)S(1)} %slice.29), channel_id=1, source_target_pairs={{0,192},{64,0},{128,64},{192,128},{1,193},{65,1},{129,65},{193,129... | collective-permute-start | bytes 491528 | tf_op jit(solution)/shard_map/L_fh/ppermute | solution.py:277
  61.8 3.6 %collective-permute-start = (s32[4,6]{1,0:T(4,128)S(1)}, s32[4,6]{1,0:T(4,128)S(1)}, u32[]{:S(2)}, u32[]{:S(2)}) collective-permute-start(s32[4,6]{1,0:T(4,128)S(1)} %pad_add_fusion.tab_ref), channel_id=1, source_target_pairs={{0,8},{8,0},{1,9},{9,1},{2,10},{10,2},{3,11},{11,3},{4,12},{12,4},... | collective-permute-start | bytes 296 | tf_op jit(solution)/shard_map/L_swap/ppermute | solution.py:282
  66.9 11.1 %forward_first.1 = (bf16[8,2,128,128]{3,2,1,0:T(8,128)(2,1)}, bf16[4,8,128,256]{3,2,1,0:T(8,128)(2,1)}, bf16[4,8,128,256]{3,2,1,0:T(8,128)(2,1)}) custom-call(s32[4]{0:T(128)S(1)} %pad_add_fusion.1.pos_ref, s32[128,8]{1,0:T(8,128)S(1)} %copy.16.cols_ref, s32[4,6]{1,0:T(4,128)S(1)} %pad_add_fusion.tab_ref, s32[4,6]{1,0:T(4,128)S(1)} %collective-permute-done.sib_tab_ref, ...), custom_call_target="tpu_custom_call" | custom-call | flops 2147483648 | bytes 16777216 | tf_op jit(solution)/shard_map/forward_first/pallas_call | solution.py:108
  78.0 4.2 %all-to-all-start = ((bf16[8,2,128,128]{3,2,1,0:T(8,128)(2,1)}), bf16[8,2,128,128]{3,2,1,0:T(8,128)(2,1)S(1)}, u32[]{:S(2)}, u32[]{:S(2)}) async-start(bf16[8,2,128,128]{3,2,1,0:T(8,128)(2,1)} %get-tuple-element.60), calls=%async_computation | async-start | bytes 1048576 | tf_op jit(solution)/shard_map/all_to_all | solution.py:323
  82.3 2.3 %collective-permute-start.19 = (f32[2,128]{1,0:T(2,128)S(1)}, f32[2,128]{1,0:T(2,128)S(1)}, u32[]{:S(2)}, u32[]{:S(2)}) collective-permute-start(f32[2,128]{1,0:T(2,128)S(1)} %get-tuple-element.86), channel_id=1, source_target_pairs={{0,8},{8,0},{1,9},{9,1},{2,10},{10,2},{3,11},{11,3},{4,12},{12,4},... | collective-permute-start | bytes 3080 | tf_op jit(solution)/shard_map/L_swap/ppermute | solution.py:282
  85.3 4.1 %all-to-all-done = bf16[8,2,128,128]{3,2,1,0:T(8,128)(2,1)S(1)} async-done(((bf16[8,2,128,128]{3,2,1,0:T(8,128)(2,1)}), bf16[8,2,128,128]{3,2,1,0:T(8,128)(2,1)S(1)}, u32[]{:S(2)}, u32[]{:S(2)}) %all-to-all-start) | async-done | bytes 524320 | tf_op jit(solution)/shard_map/all_to_all | solution.py:323
  89.5 1.6 collective-permute-start.20
  91.1 5.2 %collective-permute-start.21 = (bf16[2,128,128]{2,1,0:T(8,128)(2,1)S(1)}, bf16[2,128,128]{2,1,0:T(8,128)(2,1)S(1)}, u32[]{:S(2)}, u32[]{:S(2)}) collective-permute-start(bf16[2,128,128]{2,1,0:T(8,128)(2,1)S(1)} %tanh_convert_fusion.1), channel_id=1, source_target_pairs={{0,32},{16,48},{32,0},{48,16},{1,33},{17,49},{33,1},{49,17},{2,34}... | collective-permute-start | bytes 196616 | tf_op jit(solution)/shard_map/L_ring/ppermute | solution.py:277
  96.3 1.9 collective-permute-start.22
  98.3 4.4 %collective-permute-done.22 = bf16[2,128,128]{2,1,0:T(8,128)(2,1)S(1)} collective-permute-done((bf16[2,128,128]{2,1,0:T(8,128)(2,1)S(1)}, bf16[2,128,128]{2,1,0:T(8,128)(2,1)S(1)}, u32[]{:S(2)}, u32[]{:S(2)}) %collective-permute-start.22) | collective-permute-done | bytes 65568 | tf_op jit(solution)/shard_map/L_ring/ppermute | solution.py:277
  104.3 3.7 %collective-permute-done.23.refs_1_ = bf16[4,2,128,128]{3,2,1,0:T(8,128)(2,1)S(1)} collective-permute-done((bf16[4,2,128,128]{3,2,1,0:T(8,128)(2,1)S(1)}, bf16[4,2,128,128]{3,2,1,0:T(8,128)(2,1)S(1)}, u32[]{:S(2)}, u32[]{:S(2)}) %collective-permute-start.23) | collective-permute-done | bytes 262176 | tf_op jit(solution)/shard_map/L_ring/ppermute | solution.py:277
  108.1 1.9 collective-permute-done.24.refs_2_
  109.9 2.7 %collective-permute-done.25.refs_3_ = bf16[4,2,128,128]{3,2,1,0:T(8,128)(2,1)S(1)} collective-permute-done((bf16[4,2,128,128]{3,2,1,0:T(8,128)(2,1)S(1)}, bf16[4,2,128,128]{3,2,1,0:T(8,128)(2,1)S(1)}, u32[]{:S(2)}, u32[]{:S(2)}) %collective-permute-start.25) | collective-permute-done | bytes 262176 | tf_op jit(solution)/shard_map/L_ring/ppermute | solution.py:277
  112.6 5.1 %forward_second.1 = (bf16[8,2,128,128]{3,2,1,0:T(8,128)(2,1)}, bf16[4,4,128,256]{3,2,1,0:T(8,128)(2,1)}, bf16[4,4,128,256]{3,2,1,0:T(8,128)(2,1)}) custom-call(s32[4]{0:T(128)S(1)} %pad_add_fusion.1.pos_ref, s32[4,6]{1,0:T(4,128)S(1)} %pad_add_fusion.tab_ref, s32[4,6]{1,0:T(4,128)S(1)} %collective-permute-done.sib_tab_ref, ...), custom_call_target="tpu_custom_call" | custom-call | flops 1073741824 | bytes 8388608 | tf_op jit(solution)/shard_map/forward_second/pallas_call | solution.py:163
  117.8 4.7 %all-to-all-start.1 = ((bf16[8,2,128,128]{3,2,1,0:T(8,128)(2,1)}), bf16[8,2,128,128]{3,2,1,0:T(8,128)(2,1)S(1)}, u32[]{:S(2)}, u32[]{:S(2)}) async-start(bf16[8,2,128,128]{3,2,1,0:T(8,128)(2,1)} %get-tuple-element.61), calls=%async_computation.1 | async-start | bytes 1048576 | tf_op jit(solution)/shard_map/all_to_all | solution.py:323
  122.5 8.8 %collective-permute-start.1 = (bf16[16,8,128]{2,1,0:T(8,128)(2,1)S(1)}, bf16[16,8,128]{2,1,0:T(8,128)(2,1)S(1)}, u32[]{:S(2)}, u32[]{:S(2)}) collective-permute-start(bf16[16,8,128]{2,1,0:T(8,128)(2,1)S(1)} %get-tuple-element.82), channel_id=1, source_target_pairs={{0,8},{8,0},{1,9},{9,1},{2,10},{10,2},{3,11},{11,3},{4,12},{12,4},... | collective-permute-start | bytes 98312 | tf_op jit(solution)/shard_map/L_swap/ppermute | solution.py:282
  133.1 5.3 %all-to-all-start.2 = ((bf16[8,2,128,128]{3,2,1,0:T(8,128)(2,1)}), bf16[8,2,128,128]{3,2,1,0:T(8,128)(2,1)S(1)}, u32[]{:S(2)}, u32[]{:S(2)}) async-start(bf16[8,2,128,128]{3,2,1,0:T(8,128)(2,1)} %broadcast_in_dim.4), calls=%async_computation.2 | async-start | bytes 1048576 | tf_op jit(solution)/shard_map/all_to_all | solution.py:319
  138.4 5.6 %collective-permute-start.36 = (bf16[4,8,128,256]{3,2,1,0:T(8,128)(2,1)}, bf16[4,8,128,256]{3,2,1,0:T(8,128)(2,1)}, u32[]{:S(2)}, u32[]{:S(2)}) collective-permute-start(bf16[4,8,128,256]{3,2,1,0:T(8,128)(2,1)} %get-tuple-element.74), channel_id=1, source_target_pairs={{0,8},{8,0},{1,9},{9,1},{2,10},{10,2},{3,11},{11,3},{4,12},{12,4},... | collective-permute-start | bytes 6291464 | tf_op jit(solution)/shard_map/L_swap/ppermute | solution.py:282
  144.0 1.6 all-to-all-done.2.d_ref.refs_0_
  145.6 4.4 %adjoint_second.1 = (bf16[4,2,128,128]{3,2,1,0:T(8,128)(2,1)S(1)}, bf16[4,2,128,128]{3,2,1,0:T(8,128)(2,1)S(1)}, bf16[4,2,128,128]{3,2,1,0:T(8,128)(2,1)S(1)}, bf16[4,2,128,128]{3,2,1,0:T(8,128)(2,1)S(1)}) custom-call(s32[4]{0:T(128)S(1)} %pad_add_fusion.1.pos_ref, s32[4,6]{1,0:T(4,128)S(1)} %pad_add_fusion.tab_ref, ...), custom_call_target="tpu_custom_call" | custom-call | flops 1073741824 | bytes 8388608 | tf_op jit(solution)/shard_map/adjoint_second/pallas_call | solution.py:204
  150.1 1.5 collective-permute-start.28
  152.7 6.6 %collective-permute-done.27.refs_1_ = bf16[4,2,128,128]{3,2,1,0:T(8,128)(2,1)S(1)} collective-permute-done((bf16[4,2,128,128]{3,2,1,0:T(8,128)(2,1)S(1)}, bf16[4,2,128,128]{3,2,1,0:T(8,128)(2,1)S(1)}, u32[]{:S(2)}, u32[]{:S(2)}) %collective-permute-start.27) | collective-permute-done | bytes 262176 | tf_op jit(solution)/shard_map/L_ring/ppermute | solution.py:277
  160.1 1.4 collective-permute-start.30
  161.5 3.7 %collective-permute-start.31 = (bf16[2,128,128]{2,1,0:T(8,128)(2,1)S(1)}, bf16[2,128,128]{2,1,0:T(8,128)(2,1)S(1)}, u32[]{:S(2)}, u32[]{:S(2)}) collective-permute-start(bf16[2,128,128]{2,1,0:T(8,128)(2,1)S(1)} %get-tuple-element.68), channel_id=1, source_target_pairs={{0,32},{16,48},{32,0},{48,16},{1,33},{17,49},{33,1},{49,17},{2,34}... | collective-permute-start | bytes 196616 | tf_op jit(solution)/shard_map/L_ring/ppermute | solution.py:277
  165.2 2.2 %collective-permute-start.32 = (bf16[2,128,128]{2,1,0:T(8,128)(2,1)S(1)}, bf16[2,128,128]{2,1,0:T(8,128)(2,1)S(1)}, u32[]{:S(2)}, u32[]{:S(2)}) collective-permute-start(bf16[2,128,128]{2,1,0:T(8,128)(2,1)S(1)} %get-tuple-element.69), channel_id=1, source_target_pairs={{0,48},{16,0},{32,16},{48,32},{1,49},{17,1},{33,17},{49,33},{2,50}... | collective-permute-start | bytes 196616 | tf_op jit(solution)/shard_map/L_ring/ppermute | solution.py:277
  167.4 8.8 %collective-permute-start.33 = (bf16[4,4,128,256]{3,2,1,0:T(8,128)(2,1)}, bf16[4,4,128,256]{3,2,1,0:T(8,128)(2,1)S(1)}, u32[]{:S(2)}, u32[]{:S(2)}) collective-permute-start(bf16[4,4,128,256]{3,2,1,0:T(8,128)(2,1)} %get-tuple-element.71), channel_id=1, source_target_pairs={{0,8},{8,0},{1,9},{9,1},{2,10},{10,2},{3,11},{11,3},{4,12},{12,4},... | collective-permute-start | bytes 3145736 | tf_op jit(solution)/shard_map/L_swap/ppermute | solution.py:282
  177.2 7.0 %all-to-all-start.3 = ((bf16[16,128,128]{2,1,0:T(8,128)(2,1)}), bf16[16,128,128]{2,1,0:T(8,128)(2,1)S(1)}, u32[]{:S(2)}, u32[]{:S(2)}) async-start(bf16[16,128,128]{2,1,0:T(8,128)(2,1)} %bitcast.18), calls=%async_computation.3 | async-start | bytes 1048576 | tf_op jit(solution)/shard_map/all_to_all | solution.py:384
  187.6 1.2 copy-done.2
  188.8 1.2 copy-done.4
  190.0 2.8 %grad_second.1 = bf16[4,4,256,256]{3,2,1,0:T(8,128)(2,1)} custom-call(s32[4]{0:T(128)S(1)} %pad_add_fusion.1.pos_ref, s32[4,6]{1,0:T(4,128)S(1)} %pad_add_fusion.tab_ref, bf16[4,4,128,256]{3,2,1,0:T(8,128)(2,1)S(1)} %copy-done.2, bf16[4,4,128,256]{3,2,1,0:T(8,128)(2,1)S(1)} %copy-done.4, bf16[8,2,128,128]{3,2,1,0:T(8,128)(2,1)S(1)} %all-to-all-done.2.d_ref.refs_0_, ...), custom_call_target="tpu_custom_call" | custom-call | flops 536870912 | bytes 4194304 | tf_op jit(solution)/shard_map/grad_second/pallas_call | solution.py:257
  192.8 2.0 all-to-all-done.3
  194.8 4.5 %grad_first.1 = bf16[4,8,256,256]{3,2,1,0:T(8,128)(2,1)} custom-call(s32[4]{0:T(128)S(1)} %pad_add_fusion.1.pos_ref, s32[4,6]{1,0:T(4,128)S(1)} %pad_add_fusion.tab_ref, bf16[4,8,128,256]{3,2,1,0:T(8,128)(2,1)S(1)} %copy-done.1, bf16[4,8,128,256]{3,2,1,0:T(8,128)(2,1)} %collective-permute-done.36.po_ref, bf16[2,8,128,128]{3,2,1,0:T(8,128)(2,1)S(1)} %bitcast.40), custom_call_target="tpu_custom_call" | custom-call | flops 1073741824 | bytes 8388608 | tf_op jit(solution)/shard_map/grad_first/pallas_call | solution.py:257
  (110 shorter events, 19.2 us)
Async XLA Ops:
  0.6 46.7 %copy-start.16 = (s32[4,1]{0,1:T(1,128)S(1)}, s32[4,1]{0,1:T(1,128)}, u32[]{:S(2)}) copy-start(s32[4,1]{0,1:T(1,128)} %param.12) | copy-start | bytes 52
  0.6 46.8 %copy-start.17 = (s32[4,1]{0,1:T(1,128)S(1)}, s32[4,1]{0,1:T(1,128)}, u32[]{:S(2)}) copy-start(s32[4,1]{0,1:T(1,128)} %param.16) | copy-start | bytes 52
  0.7 26.5 %collective-permute-start.8 = (bf16[4,8,256,256]{3,2,1,0:T(8,128)(2,1)}, bf16[4,8,256,256]{3,2,1,0:T(8,128)(2,1)}, u32[]{:S(2)}, u32[]{:S(2)}) collective-permute-start(bf16[4,8,256,256]{3,2,1,0:T(8,128)(2,1)} %refs_14_.1), channel_id=1, source_target_pairs={{0,8},{8,0},{1,9},{9,1},{2,10},{10,2},{3,11},{11,3},{4,12},{12,4},... | collective-permute-start | bytes 12582920 | tf_op jit(solution)/shard_map/L_w1/ppermute | solution.py:282
  4.0 10.7 %collective-permute-start.2 = (bf16[8,20480]{1,0:T(8,128)(2,1)}, bf16[8,20480]{1,0:T(8,128)(2,1)S(1)}, u32[]{:S(2)}, u32[]{:S(2)}) collective-permute-start(bf16[8,20480]{1,0:T(8,128)(2,1)} %refs_0_.1), channel_id=1, source_target_pairs={{0,64},{64,128},{128,192},{192,0},{1,65},{65,129},{129,193},{193,1... | collective-permute-start | bytes 983048 | tf_op jit(solution)/shard_map/L_xp/ppermute | solution.py:277
  4.0 10.7 %collective-permute-start.3 = (bf16[8,20480]{1,0:T(8,128)(2,1)}, bf16[8,20480]{1,0:T(8,128)(2,1)S(1)}, u32[]{:S(2)}, u32[]{:S(2)}) collective-permute-start(bf16[8,20480]{1,0:T(8,128)(2,1)} %refs_0_.1), channel_id=1, source_target_pairs={{0,192},{64,0},{128,64},{192,128},{1,193},{65,1},{129,65},{193,129... | collective-permute-start | bytes 983048 | tf_op jit(solution)/shard_map/L_xn/ppermute | solution.py:277
  6.7 14.0 %collective-permute-start.4 = (bf16[8,20480]{1,0:T(8,128)(2,1)}, bf16[8,20480]{1,0:T(8,128)(2,1)S(1)}, u32[]{:S(2)}, u32[]{:S(2)}) collective-permute-start(bf16[8,20480]{1,0:T(8,128)(2,1)} %refs_0_.1), channel_id=1, source_target_pairs={{0,16},{16,32},{32,48},{48,0},{1,17},{17,33},{33,49},{49,1},{2,18}... | collective-permute-start | bytes 983048 | tf_op jit(solution)/shard_map/L_zp/ppermute | solution.py:277
  7.9 19.2 %collective-permute-start.5 = (bf16[8,20480]{1,0:T(8,128)(2,1)}, bf16[8,20480]{1,0:T(8,128)(2,1)S(1)}, u32[]{:S(2)}, u32[]{:S(2)}) collective-permute-start(bf16[8,20480]{1,0:T(8,128)(2,1)} %refs_0_.1), channel_id=1, source_target_pairs={{0,48},{16,0},{32,16},{48,32},{1,49},{17,1},{33,17},{49,33},{2,50}... | collective-permute-start | bytes 983048 | tf_op jit(solution)/shard_map/L_zn/ppermute | solution.py:277
  14.7 43.1 %copy-start.8 = (bf16[8,20480]{1,0:T(8,128)(2,1)}, bf16[8,20480]{1,0:T(8,128)(2,1)S(1)}, u32[]{:S(2)}) copy-start(bf16[8,20480]{1,0:T(8,128)(2,1)S(1)} %collective-permute-done.2.refs_1_) | copy-start | bytes 983044
  14.7 47.0 %copy-start.15 = (s32[4,4]{1,0:T(4,128)S(1)}, s32[4,4]{1,0:T(4,128)}, u32[]{:S(2)}) copy-start(s32[4,4]{1,0:T(4,128)} %param.15) | copy-start | bytes 196
  14.7 50.7 %copy-start = (bf16[4,4,256,256]{3,2,1,0:T(8,128)(2,1)S(1)}, bf16[4,4,256,256]{3,2,1,0:T(8,128)(2,1)}, u32[]{:S(2)}) copy-start(bf16[4,4,256,256]{3,2,1,0:T(8,128)(2,1)} %own_ref.1) | copy-start | bytes 6291460
  14.7 50.9 %copy-start.14 = (s32[128,8]{0,1:T(8,128)S(1)}, s32[128,8]{0,1:T(8,128)}, u32[]{:S(2)}) copy-start(s32[128,8]{0,1:T(8,128)} %param.11) | copy-start | bytes 12292
  14.7 12.4 %collective-permute-start.6 = (bf16[8,10240]{1,0:T(8,128)(2,1)S(1)}, bf16[8,10240]{1,0:T(8,128)(2,1)S(1)}, u32[]{:S(2)}, u32[]{:S(2)}) collective-permute-start(bf16[8,10240]{1,0:T(8,128)(2,1)S(1)} %slice.24), channel_id=1, source_target_pairs={{0,64},{64,128},{128,192},{192,0},{1,65},{65,129},{129,193},{193,1... | collective-permute-start | bytes 491528 | tf_op jit(solution)/shard_map/L_xl/ppermute | solution.py:277
  14.8 12.3 %collective-permute-start.7 = (bf16[8,10240]{1,0:T(8,128)(2,1)S(1)}, bf16[8,10240]{1,0:T(8,128)(2,1)S(1)}, u32[]{:S(2)}, u32[]{:S(2)}) collective-permute-start(bf16[8,10240]{1,0:T(8,128)(2,1)S(1)} %slice.25), channel_id=1, source_target_pairs={{0,192},{64,0},{128,64},{192,128},{1,193},{65,1},{129,65},{193,129... | collective-permute-start | bytes 491528 | tf_op jit(solution)/shard_map/L_xh/ppermute | solution.py:277
  27.2 16.6 %collective-permute-start.11 = (bf16[16,20480]{1,0:T(8,128)(2,1)S(1)}, bf16[16,20480]{1,0:T(8,128)(2,1)S(1)}, u32[]{:S(2)}, u32[]{:S(2)}) collective-permute-start(bf16[16,20480]{1,0:T(8,128)(2,1)S(1)} %pad_maximum_fusion.refs_4_), channel_id=1, source_target_pairs={{0,64},{64,128},{128,192},{192,0},{1,65},{65,129},{129,193},{193,1... | collective-permute-start | bytes 1966088 | tf_op jit(solution)/shard_map/L_tp/ppermute | solution.py:277
  28.0 15.8 %collective-permute-start.12 = (bf16[16,20480]{1,0:T(8,128)(2,1)S(1)}, bf16[16,20480]{1,0:T(8,128)(2,1)S(1)}, u32[]{:S(2)}, u32[]{:S(2)}) collective-permute-start(bf16[16,20480]{1,0:T(8,128)(2,1)S(1)} %pad_maximum_fusion.refs_4_), channel_id=1, source_target_pairs={{0,192},{64,0},{128,64},{192,128},{1,193},{65,1},{129,65},{193,129... | collective-permute-start | bytes 1966088 | tf_op jit(solution)/shard_map/L_tn/ppermute | solution.py:277
  30.0 6.5 %collective-permute-start.10 = (bf16[8,10240]{1,0:T(8,128)(2,1)S(1)}, bf16[8,10240]{1,0:T(8,128)(2,1)S(1)}, u32[]{:S(2)}, u32[]{:S(2)}) collective-permute-start(bf16[8,10240]{1,0:T(8,128)(2,1)S(1)} %slice.27), channel_id=1, source_target_pairs={{0,48},{16,0},{32,16},{48,32},{1,49},{17,1},{33,17},{49,33},{2,50}... | collective-permute-start | bytes 491528 | tf_op jit(solution)/shard_map/L_zr/ppermute | solution.py:277
  32.3 6.4 %collective-permute-start.9 = (bf16[8,10240]{1,0:T(8,128)(2,1)S(1)}, bf16[8,10240]{1,0:T(8,128)(2,1)S(1)}, u32[]{:S(2)}, u32[]{:S(2)}) collective-permute-start(bf16[8,10240]{1,0:T(8,128)(2,1)S(1)} %slice.26), channel_id=1, source_target_pairs={{0,16},{16,32},{32,48},{48,0},{1,17},{17,33},{33,49},{49,1},{2,18}... | collective-permute-start | bytes 491528 | tf_op jit(solution)/shard_map/L_zl/ppermute | solution.py:277
  33.1 33.2 %copy-start.6 = (bf16[8,20480]{1,0:T(8,128)(2,1)}, bf16[8,20480]{1,0:T(8,128)(2,1)S(1)}, u32[]{:S(2)}) copy-start(bf16[8,20480]{1,0:T(8,128)(2,1)S(1)} %pad_maximum_fusion.1.refs_3_) | copy-start | bytes 983044
  38.7 18.1 %collective-permute-start.15 = (bf16[8,20480]{1,0:T(8,128)(2,1)S(1)}, bf16[8,20480]{1,0:T(8,128)(2,1)}, u32[]{:S(2)}, u32[]{:S(2)}) collective-permute-start(bf16[8,20480]{1,0:T(8,128)(2,1)S(1)} %pad_maximum_fusion.1.refs_3_), channel_id=1, source_target_pairs={{0,16},{16,32},{32,48},{48,0},{1,17},{17,33},{33,49},{49,1},{2,18}... | collective-permute-start | bytes 983048 | tf_op jit(solution)/shard_map/L_wp/ppermute | solution.py:277
  41.2 15.6 %collective-permute-start.16 = (bf16[8,20480]{1,0:T(8,128)(2,1)S(1)}, bf16[8,20480]{1,0:T(8,128)(2,1)}, u32[]{:S(2)}, u32[]{:S(2)}) collective-permute-start(bf16[8,20480]{1,0:T(8,128)(2,1)S(1)} %pad_maximum_fusion.1.refs_3_), channel_id=1, source_target_pairs={{0,48},{16,0},{32,16},{48,32},{1,49},{17,1},{33,17},{49,33},{2,50}... | collective-permute-start | bytes 983048 | tf_op jit(solution)/shard_map/L_wn/ppermute | solution.py:277
  44.6 12.2 %collective-permute-start.13 = (bf16[8,20480]{1,0:T(8,128)(2,1)S(1)}, bf16[8,20480]{1,0:T(8,128)(2,1)}, u32[]{:S(2)}, u32[]{:S(2)}) collective-permute-start(bf16[8,20480]{1,0:T(8,128)(2,1)S(1)} %pad_maximum_fusion.2.refs_9_), channel_id=1, source_target_pairs={{0,64},{64,128},{128,192},{192,0},{1,65},{65,129},{129,193},{193,1... | collective-permute-start | bytes 983048 | tf_op jit(solution)/shard_map/L_fp/ppermute | solution.py:277
  45.5 11.3 %collective-permute-start.14 = (bf16[8,20480]{1,0:T(8,128)(2,1)S(1)}, bf16[8,20480]{1,0:T(8,128)(2,1)}, u32[]{:S(2)}, u32[]{:S(2)}) collective-permute-start(bf16[8,20480]{1,0:T(8,128)(2,1)S(1)} %pad_maximum_fusion.2.refs_9_), channel_id=1, source_target_pairs={{0,192},{64,0},{128,64},{192,128},{1,193},{65,1},{129,65},{193,129... | collective-permute-start | bytes 983048 | tf_op jit(solution)/shard_map/L_fn/ppermute | solution.py:277
  57.8 8.5 %collective-permute-start.17 = (bf16[8,10240]{1,0:T(8,128)(2,1)S(1)}, bf16[8,10240]{1,0:T(8,128)(2,1)}, u32[]{:S(2)}, u32[]{:S(2)}) collective-permute-start(bf16[8,10240]{1,0:T(8,128)(2,1)S(1)} %slice.28), channel_id=1, source_target_pairs={{0,64},{64,128},{128,192},{192,0},{1,65},{65,129},{129,193},{193,1... | collective-permute-start | bytes 491528 | tf_op jit(solution)/shard_map/L_fl/ppermute | solution.py:277
  59.0 7.3 %collective-permute-start.18 = (bf16[8,10240]{1,0:T(8,128)(2,1)S(1)}, bf16[8,10240]{1,0:T(8,128)(2,1)S(1)}, u32[]{:S(2)}, u32[]{:S(2)}) collective-permute-start(bf16[8,10240]{1,0:T(8,128)(2,1)S(1)} %slice.29), channel_id=1, source_target_pairs={{0,192},{64,0},{128,64},{192,128},{1,193},{65,1},{129,65},{193,129... | collective-permute-start | bytes 491528 | tf_op jit(solution)/shard_map/L_fh/ppermute | solution.py:277
  61.8 4.5 %collective-permute-start = (s32[4,6]{1,0:T(4,128)S(1)}, s32[4,6]{1,0:T(4,128)S(1)}, u32[]{:S(2)}, u32[]{:S(2)}) collective-permute-start(s32[4,6]{1,0:T(4,128)S(1)} %pad_add_fusion.tab_ref), channel_id=1, source_target_pairs={{0,8},{8,0},{1,9},{9,1},{2,10},{10,2},{3,11},{11,3},{4,12},{12,4},... | collective-permute-start | bytes 296 | tf_op jit(solution)/shard_map/L_swap/ppermute | solution.py:282
  65.4 38.9 %collective-permute-start.26 = (bf16[4,4,256,256]{3,2,1,0:T(8,128)(2,1)S(1)}, bf16[4,4,256,256]{3,2,1,0:T(8,128)(2,1)}, u32[]{:S(2)}, u32[]{:S(2)}) collective-permute-start(bf16[4,4,256,256]{3,2,1,0:T(8,128)(2,1)S(1)} %copy-done), channel_id=1, source_target_pairs={{0,8},{8,0},{1,9},{9,1},{2,10},{10,2},{3,11},{11,3},{4,12},{12,4},... | collective-permute-start | bytes 6291464 | tf_op jit(solution)/shard_map/L_swap/ppermute | solution.py:282
  78.0 11.4 %all-to-all-start = ((bf16[8,2,128,128]{3,2,1,0:T(8,128)(2,1)}), bf16[8,2,128,128]{3,2,1,0:T(8,128)(2,1)S(1)}, u32[]{:S(2)}, u32[]{:S(2)}) async-start(bf16[8,2,128,128]{3,2,1,0:T(8,128)(2,1)} %get-tuple-element.60), calls=%async_computation | async-start | bytes 1048576 | tf_op jit(solution)/shard_map/all_to_all | solution.py:323
  82.3 3.1 %collective-permute-start.19 = (f32[2,128]{1,0:T(2,128)S(1)}, f32[2,128]{1,0:T(2,128)S(1)}, u32[]{:S(2)}, u32[]{:S(2)}) collective-permute-start(f32[2,128]{1,0:T(2,128)S(1)} %get-tuple-element.86), channel_id=1, source_target_pairs={{0,8},{8,0},{1,9},{9,1},{2,10},{10,2},{3,11},{11,3},{4,12},{12,4},... | collective-permute-start | bytes 3080 | tf_op jit(solution)/shard_map/L_swap/ppermute | solution.py:282
  89.5 8.8 %collective-permute-start.20 = (bf16[2,128,128]{2,1,0:T(8,128)(2,1)S(1)}, bf16[2,128,128]{2,1,0:T(8,128)(2,1)S(1)}, u32[]{:S(2)}, u32[]{:S(2)}) collective-permute-start(bf16[2,128,128]{2,1,0:T(8,128)(2,1)S(1)} %tanh_convert_fusion.1), channel_id=1, source_target_pairs={{0,48},{16,0},{32,16},{48,32},{1,49},{17,1},{33,17},{49,33},{2,50}... | collective-permute-start | bytes 196616 | tf_op jit(solution)/shard_map/L_ring/ppermute | solution.py:277
  91.1 7.2 %collective-permute-start.21 = (bf16[2,128,128]{2,1,0:T(8,128)(2,1)S(1)}, bf16[2,128,128]{2,1,0:T(8,128)(2,1)S(1)}, u32[]{:S(2)}, u32[]{:S(2)}) collective-permute-start(bf16[2,128,128]{2,1,0:T(8,128)(2,1)S(1)} %tanh_convert_fusion.1), channel_id=1, source_target_pairs={{0,32},{16,48},{32,0},{48,16},{1,33},{17,49},{33,1},{49,17},{2,34}... | collective-permute-start | bytes 196616 | tf_op jit(solution)/shard_map/L_ring/ppermute | solution.py:277
  96.3 6.4 %collective-permute-start.22 = (bf16[2,128,128]{2,1,0:T(8,128)(2,1)S(1)}, bf16[2,128,128]{2,1,0:T(8,128)(2,1)S(1)}, u32[]{:S(2)}, u32[]{:S(2)}) collective-permute-start(bf16[2,128,128]{2,1,0:T(8,128)(2,1)S(1)} %tanh_convert_fusion.1), channel_id=1, source_target_pairs={{0,16},{16,32},{32,48},{48,0},{1,17},{17,33},{33,49},{49,1},{2,18}... | collective-permute-start | bytes 196616 | tf_op jit(solution)/shard_map/L_ring/ppermute | solution.py:277
  102.8 5.3 %collective-permute-start.23 = (bf16[4,2,128,128]{3,2,1,0:T(8,128)(2,1)S(1)}, bf16[4,2,128,128]{3,2,1,0:T(8,128)(2,1)S(1)}, u32[]{:S(2)}, u32[]{:S(2)}) collective-permute-start(bf16[4,2,128,128]{3,2,1,0:T(8,128)(2,1)S(1)} %pad_maximum_fusion.3.refs_0_), channel_id=1, source_target_pairs={{0,192},{64,0},{128,64},{192,128},{1,193},{65,1},{129,65},{193,129... | collective-permute-start | bytes 786440 | tf_op jit(solution)/shard_map/L_ring/ppermute | solution.py:277
  103.1 6.8 %collective-permute-start.24 = (bf16[4,2,128,128]{3,2,1,0:T(8,128)(2,1)S(1)}, bf16[4,2,128,128]{3,2,1,0:T(8,128)(2,1)S(1)}, u32[]{:S(2)}, u32[]{:S(2)}) collective-permute-start(bf16[4,2,128,128]{3,2,1,0:T(8,128)(2,1)S(1)} %pad_maximum_fusion.3.refs_0_), channel_id=1, source_target_pairs={{0,128},{64,192},{128,0},{192,64},{1,129},{65,193},{129,1},{193,65... | collective-permute-start | bytes 786440 | tf_op jit(solution)/shard_map/L_ring/ppermute | solution.py:277
  103.1 9.5 %collective-permute-start.25 = (bf16[4,2,128,128]{3,2,1,0:T(8,128)(2,1)S(1)}, bf16[4,2,128,128]{3,2,1,0:T(8,128)(2,1)S(1)}, u32[]{:S(2)}, u32[]{:S(2)}) collective-permute-start(bf16[4,2,128,128]{3,2,1,0:T(8,128)(2,1)S(1)} %pad_maximum_fusion.3.refs_0_), channel_id=1, source_target_pairs={{0,64},{64,128},{128,192},{192,0},{1,65},{65,129},{129,193},{193,1... | collective-permute-start | bytes 786440 | tf_op jit(solution)/shard_map/L_ring/ppermute | solution.py:277
  117.8 13.5 %all-to-all-start.1 = ((bf16[8,2,128,128]{3,2,1,0:T(8,128)(2,1)}), bf16[8,2,128,128]{3,2,1,0:T(8,128)(2,1)S(1)}, u32[]{:S(2)}, u32[]{:S(2)}) async-start(bf16[8,2,128,128]{3,2,1,0:T(8,128)(2,1)} %get-tuple-element.61), calls=%async_computation.1 | async-start | bytes 1048576 | tf_op jit(solution)/shard_map/all_to_all | solution.py:323
  122.5 9.6 %collective-permute-start.1 = (bf16[16,8,128]{2,1,0:T(8,128)(2,1)S(1)}, bf16[16,8,128]{2,1,0:T(8,128)(2,1)S(1)}, u32[]{:S(2)}, u32[]{:S(2)}) collective-permute-start(bf16[16,8,128]{2,1,0:T(8,128)(2,1)S(1)} %get-tuple-element.82), channel_id=1, source_target_pairs={{0,8},{8,0},{1,9},{9,1},{2,10},{10,2},{3,11},{11,3},{4,12},{12,4},... | collective-permute-start | bytes 98312 | tf_op jit(solution)/shard_map/L_swap/ppermute | solution.py:282
  133.1 12.5 %all-to-all-start.2 = ((bf16[8,2,128,128]{3,2,1,0:T(8,128)(2,1)}), bf16[8,2,128,128]{3,2,1,0:T(8,128)(2,1)S(1)}, u32[]{:S(2)}, u32[]{:S(2)}) async-start(bf16[8,2,128,128]{3,2,1,0:T(8,128)(2,1)} %broadcast_in_dim.4), calls=%async_computation.2 | async-start | bytes 1048576 | tf_op jit(solution)/shard_map/all_to_all | solution.py:319
  138.4 56.4 %collective-permute-start.36 = (bf16[4,8,128,256]{3,2,1,0:T(8,128)(2,1)}, bf16[4,8,128,256]{3,2,1,0:T(8,128)(2,1)}, u32[]{:S(2)}, u32[]{:S(2)}) collective-permute-start(bf16[4,8,128,256]{3,2,1,0:T(8,128)(2,1)} %get-tuple-element.74), channel_id=1, source_target_pairs={{0,8},{8,0},{1,9},{9,1},{2,10},{10,2},{3,11},{11,3},{4,12},{12,4},... | collective-permute-start | bytes 6291464 | tf_op jit(solution)/shard_map/L_swap/ppermute | solution.py:282
  150.0 9.3 %collective-permute-start.27 = (bf16[4,2,128,128]{3,2,1,0:T(8,128)(2,1)S(1)}, bf16[4,2,128,128]{3,2,1,0:T(8,128)(2,1)S(1)}, u32[]{:S(2)}, u32[]{:S(2)}) collective-permute-start(bf16[4,2,128,128]{3,2,1,0:T(8,128)(2,1)S(1)} %get-tuple-element.63), channel_id=1, source_target_pairs={{0,64},{64,128},{128,192},{192,0},{1,65},{65,129},{129,193},{193,1... | collective-permute-start | bytes 786440 | tf_op jit(solution)/shard_map/L_ring/ppermute | solution.py:277
  150.1 9.2 %collective-permute-start.28 = (bf16[4,2,128,128]{3,2,1,0:T(8,128)(2,1)S(1)}, bf16[4,2,128,128]{3,2,1,0:T(8,128)(2,1)S(1)}, u32[]{:S(2)}, u32[]{:S(2)}) collective-permute-start(bf16[4,2,128,128]{3,2,1,0:T(8,128)(2,1)S(1)} %get-tuple-element.64), channel_id=1, source_target_pairs={{0,128},{64,192},{128,0},{192,64},{1,129},{65,193},{129,1},{193,65... | collective-permute-start | bytes 786440 | tf_op jit(solution)/shard_map/L_ring/ppermute | solution.py:277
  151.6 8.3 %collective-permute-start.29 = (bf16[4,2,128,128]{3,2,1,0:T(8,128)(2,1)S(1)}, bf16[4,2,128,128]{3,2,1,0:T(8,128)(2,1)S(1)}, u32[]{:S(2)}, u32[]{:S(2)}) collective-permute-start(bf16[4,2,128,128]{3,2,1,0:T(8,128)(2,1)S(1)} %get-tuple-element.65), channel_id=1, source_target_pairs={{0,192},{64,0},{128,64},{192,128},{1,193},{65,1},{129,65},{193,129... | collective-permute-start | bytes 786440 | tf_op jit(solution)/shard_map/L_ring/ppermute | solution.py:277
  160.1 16.2 %collective-permute-start.30 = (bf16[2,128,128]{2,1,0:T(8,128)(2,1)S(1)}, bf16[2,128,128]{2,1,0:T(8,128)(2,1)S(1)}, u32[]{:S(2)}, u32[]{:S(2)}) collective-permute-start(bf16[2,128,128]{2,1,0:T(8,128)(2,1)S(1)} %get-tuple-element.67), channel_id=1, source_target_pairs={{0,16},{16,32},{32,48},{48,0},{1,17},{17,33},{33,49},{49,1},{2,18}... | collective-permute-start | bytes 196616 | tf_op jit(solution)/shard_map/L_ring/ppermute | solution.py:277
  161.5 14.8 %collective-permute-start.31 = (bf16[2,128,128]{2,1,0:T(8,128)(2,1)S(1)}, bf16[2,128,128]{2,1,0:T(8,128)(2,1)S(1)}, u32[]{:S(2)}, u32[]{:S(2)}) collective-permute-start(bf16[2,128,128]{2,1,0:T(8,128)(2,1)S(1)} %get-tuple-element.68), channel_id=1, source_target_pairs={{0,32},{16,48},{32,0},{48,16},{1,33},{17,49},{33,1},{49,17},{2,34}... | collective-permute-start | bytes 196616 | tf_op jit(solution)/shard_map/L_ring/ppermute | solution.py:277
  165.2 11.1 %collective-permute-start.32 = (bf16[2,128,128]{2,1,0:T(8,128)(2,1)S(1)}, bf16[2,128,128]{2,1,0:T(8,128)(2,1)S(1)}, u32[]{:S(2)}, u32[]{:S(2)}) collective-permute-start(bf16[2,128,128]{2,1,0:T(8,128)(2,1)S(1)} %get-tuple-element.69), channel_id=1, source_target_pairs={{0,48},{16,0},{32,16},{48,32},{1,49},{17,1},{33,17},{49,33},{2,50}... | collective-permute-start | bytes 196616 | tf_op jit(solution)/shard_map/L_ring/ppermute | solution.py:277
  167.4 19.2 %collective-permute-start.33 = (bf16[4,4,128,256]{3,2,1,0:T(8,128)(2,1)}, bf16[4,4,128,256]{3,2,1,0:T(8,128)(2,1)S(1)}, u32[]{:S(2)}, u32[]{:S(2)}) collective-permute-start(bf16[4,4,128,256]{3,2,1,0:T(8,128)(2,1)} %get-tuple-element.71), channel_id=1, source_target_pairs={{0,8},{8,0},{1,9},{9,1},{2,10},{10,2},{3,11},{11,3},{4,12},{12,4},... | collective-permute-start | bytes 3145736 | tf_op jit(solution)/shard_map/L_swap/ppermute | solution.py:282
  177.2 17.6 %all-to-all-start.3 = ((bf16[16,128,128]{2,1,0:T(8,128)(2,1)}), bf16[16,128,128]{2,1,0:T(8,128)(2,1)S(1)}, u32[]{:S(2)}, u32[]{:S(2)}) async-start(bf16[16,128,128]{2,1,0:T(8,128)(2,1)} %bitcast.18), calls=%async_computation.3 | async-start | bytes 1048576 | tf_op jit(solution)/shard_map/all_to_all | solution.py:384
  184.3 3.3 %collective-permute-start.34 = (bf16[8,128,128]{2,1,0:T(8,128)(2,1)S(1)}, bf16[8,128,128]{2,1,0:T(8,128)(2,1)S(1)}, u32[]{:S(2)}, u32[]{:S(2)}) collective-permute-start(bf16[8,128,128]{2,1,0:T(8,128)(2,1)S(1)} %dynamic-slice_bitcast_fusion), channel_id=1, source_target_pairs={{0,8},{8,0},{1,9},{9,1},{2,10},{10,2},{3,11},{11,3},{4,12},{12,4},... | collective-permute-start | bytes 786440 | tf_op jit(solution)/shard_map/L_swap/ppermute | solution.py:282
  184.5 1.4 collective-permute-start.35
  (13 other events, 105.8 us)

commit v4 on v3

--- a/solution.py
+++ b/solution.py
@@ -13,6 +13,7 @@
 ROWS = 4
 NX = 4
 NZ = 4
+CHUNK = 2560
 OUT = ("x", "zh", "core")
 IN = ("zl", "y")
 F32 = jnp.float32
@@ -59,6 +60,15 @@
         for src, (a, offsets, first) in zip(srcs, pieces):
             for m, (dx, dz) in enumerate(offsets):
                 row = ((x + dx) % NX * NZ + (z + dz) % NZ) * own_rows
+                for q in range(0, a.shape[1], CHUNK):
+                    pltpu.make_async_copy(
+                        src.at[pl.ds(m * own_rows, own_rows), pl.ds(q, CHUNK)],
+                        whole.at[
+                            pl.ds(pl.multiple_of(row, own_rows), own_rows),
+                            pl.ds(first + q, CHUNK),
+                        ],
+                        sems.at[len(copies)],
+                    ).start()
                 copies.append(
                     pltpu.make_async_copy(
                         src.at[pl.ds(m * own_rows, own_rows), :],
@@ -69,17 +79,18 @@
                         sems.at[len(copies)],
                     )
                 )
-                copies[-1].start()
 
         def load(who, r):
             src = (own_ref, sib_ref)[who]
             return pltpu.make_async_copy(src.at[r], weights.at[who, r], wsems.at[who, r])
 
+        load(0, 0).start()
+        for c in copies:
+            c.wait()
         for who in range(2):
             for r in range(ROWS):
-                load(who, r).start()
-        for c in copies:
-            c.wait()
+                if who + r:
+                    load(who, r).start()
         for mine in (True, False):
             who, tab, to = (0, tab_ref, p_own) if mine else (1, sib_tab_ref, p_sib)
             base = (out_at if mine else out_at ^ 1) * ROWS

time: 200 us -> 199 us (level)
  no operation moved by 1% of the time
where the time goes in v4:
time: 199 us; the launch traced here: 198 us
  starting transfers between devices  98 us (49%)
  waiting for transfers between devices  60.4 us (30%)
  Pallas kernels  26.9 us (14%)
  local copies, waits for them, and re-layouts  10.7 us (5%)
    ppermute x28, waiting for transfers between devices, ring(): return lax.ppermute(value, axis, [(i, (i + step) % n) for i in range(n)])  49.6 us
    ppermute x28, starting transfers between devices, ring(): return lax.ppermute(value, axis, [(i, (i + step) % n) for i in range(n)])  43.6 us
    ppermute x9, starting transfers between devices, swap(): return lax.ppermute(value, 'core', [(0, 1), (1, 0)])  33.1 us
    pallas_call x1, Pallas kernels, forward_first(): pl.pallas_call(body, out_shape=(jax.ShapeDtypeStruct((2 * ROWS, 2, frames...  9.9 us
    all_to_all x2, starting transfers between devices, sum_axis(): lax.all_to_all(parts, axis, 0, 0, tiled=True).astype(F32)  8.91 us
    pallas_call x2, Pallas kernels, weight_grads(): pl.pallas_call(body, out_shape=jax.ShapeDtypeStruct((ROWS, slots, BLK, BL...  7.31 us
    all_to_all x1, starting transfers between devices, shards(): lax.all_to_all(to_all.reshape(-1, *delta_first.shape[1:]), ('core', *IN),...  7.01 us
    unnamed x43, local copies, waits for them, and re-layouts  6.87 us
  transfers between devices with their start and end apart: 41, of which 20 were waited for; matrix products, arithmetic and copies ran while one was open for 2% of the time, Pallas kernels for 9%

profile of v4, /device:TPU:1, one launch (start us, length us, event | category | flops | bytes accessed | tf_op | source)
XLA Modules:
  0.0 198.4 jit_solution(867842091171346429)
XLA Ops:
  0.7 3.3 %collective-permute-start.8 = (bf16[4,8,256,256]{3,2,1,0:T(8,128)(2,1)}, bf16[4,8,256,256]{3,2,1,0:T(8,128)(2,1)}, u32[]{:S(2)}, u32[]{:S(2)}) collective-permute-start(bf16[4,8,256,256]{3,2,1,0:T(8,128)(2,1)} %refs_14_.1), channel_id=1, source_target_pairs={{0,8},{8,0},{1,9},{9,1},{2,10},{10,2},{3,11},{11,3},{4,12},{12,4},... | collective-permute-start | bytes 12582920 | tf_op jit(solution)/shard_map/L_w1/ppermute | solution.py:293
  4.0 2.7 %collective-permute-start.3 = (bf16[8,20480]{1,0:T(8,128)(2,1)}, bf16[8,20480]{1,0:T(8,128)(2,1)S(1)}, u32[]{:S(2)}, u32[]{:S(2)}) collective-permute-start(bf16[8,20480]{1,0:T(8,128)(2,1)} %refs_0_.1), channel_id=1, source_target_pairs={{0,192},{64,0},{128,64},{192,128},{1,193},{65,1},{129,65},{193,129... | collective-permute-start | bytes 983048 | tf_op jit(solution)/shard_map/L_xn/ppermute | solution.py:288
  6.7 1.3 collective-permute-start.4
  7.9 3.0 %collective-permute-start.5 = (bf16[8,20480]{1,0:T(8,128)(2,1)}, bf16[8,20480]{1,0:T(8,128)(2,1)S(1)}, u32[]{:S(2)}, u32[]{:S(2)}) collective-permute-start(bf16[8,20480]{1,0:T(8,128)(2,1)} %refs_0_.1), channel_id=1, source_target_pairs={{0,48},{16,0},{32,16},{48,32},{1,49},{17,1},{33,17},{49,33},{2,50}... | collective-permute-start | bytes 983048 | tf_op jit(solution)/shard_map/L_zn/ppermute | solution.py:288
  11.0 3.7 %collective-permute-done.2.refs_1_ = bf16[8,20480]{1,0:T(8,128)(2,1)S(1)} collective-permute-done((bf16[8,20480]{1,0:T(8,128)(2,1)}, bf16[8,20480]{1,0:T(8,128)(2,1)S(1)}, u32[]{:S(2)}, u32[]{:S(2)}) %collective-permute-start.2) | collective-permute-done | bytes 327712 | tf_op jit(solution)/shard_map/L_xp/ppermute | solution.py:288
  14.8 2.7 %collective-permute-start.7 = (bf16[8,10240]{1,0:T(8,128)(2,1)S(1)}, bf16[8,10240]{1,0:T(8,128)(2,1)S(1)}, u32[]{:S(2)}, u32[]{:S(2)}) collective-permute-start(bf16[8,10240]{1,0:T(8,128)(2,1)S(1)} %slice.25), channel_id=1, source_target_pairs={{0,192},{64,0},{128,64},{192,128},{1,193},{65,1},{129,65},{193,129... | collective-permute-start | bytes 491528 | tf_op jit(solution)/shard_map/L_xh/ppermute | solution.py:288
  17.6 3.1 %collective-permute-done.4 = bf16[8,20480]{1,0:T(8,128)(2,1)S(1)} collective-permute-done((bf16[8,20480]{1,0:T(8,128)(2,1)}, bf16[8,20480]{1,0:T(8,128)(2,1)S(1)}, u32[]{:S(2)}, u32[]{:S(2)}) %collective-permute-start.4) | collective-permute-done | bytes 327712 | tf_op jit(solution)/shard_map/L_zp/ppermute | solution.py:288
  20.7 6.4 %collective-permute-done.5 = bf16[8,20480]{1,0:T(8,128)(2,1)S(1)} collective-permute-done((bf16[8,20480]{1,0:T(8,128)(2,1)}, bf16[8,20480]{1,0:T(8,128)(2,1)S(1)}, u32[]{:S(2)}, u32[]{:S(2)}) %collective-permute-start.5) | collective-permute-done | bytes 327712 | tf_op jit(solution)/shard_map/L_zn/ppermute | solution.py:288
  28.0 1.9 collective-permute-start.12
  30.0 2.4 %collective-permute-start.10 = (bf16[8,10240]{1,0:T(8,128)(2,1)S(1)}, bf16[8,10240]{1,0:T(8,128)(2,1)S(1)}, u32[]{:S(2)}, u32[]{:S(2)}) collective-permute-start(bf16[8,10240]{1,0:T(8,128)(2,1)S(1)} %slice.27), channel_id=1, source_target_pairs={{0,48},{16,0},{32,16},{48,32},{1,49},{17,1},{33,17},{49,33},{2,50}... | collective-permute-start | bytes 491528 | tf_op jit(solution)/shard_map/L_zr/ppermute | solution.py:288
  33.1 3.4 %collective-permute-done.10 = bf16[8,10240]{1,0:T(8,128)(2,1)S(1)} collective-permute-done((bf16[8,10240]{1,0:T(8,128)(2,1)S(1)}, bf16[8,10240]{1,0:T(8,128)(2,1)S(1)}, u32[]{:S(2)}, u32[]{:S(2)}) %collective-permute-start.10) | collective-permute-done | bytes 163872 | tf_op jit(solution)/shard_map/L_zr/ppermute | solution.py:288
  36.4 2.3 %collective-permute-done.9 = bf16[8,10240]{1,0:T(8,128)(2,1)S(1)} collective-permute-done((bf16[8,10240]{1,0:T(8,128)(2,1)S(1)}, bf16[8,10240]{1,0:T(8,128)(2,1)S(1)}, u32[]{:S(2)}, u32[]{:S(2)}) %collective-permute-start.9) | collective-permute-done | bytes 163872 | tf_op jit(solution)/shard_map/L_zl/ppermute | solution.py:288
  38.7 2.5 %collective-permute-start.15 = (bf16[8,20480]{1,0:T(8,128)(2,1)S(1)}, bf16[8,20480]{1,0:T(8,128)(2,1)}, u32[]{:S(2)}, u32[]{:S(2)}) collective-permute-start(bf16[8,20480]{1,0:T(8,128)(2,1)S(1)} %pad_maximum_fusion.1.refs_3_), channel_id=1, source_target_pairs={{0,16},{16,32},{32,48},{48,0},{1,17},{17,33},{33,49},{49,1},{2,18}... | collective-permute-start | bytes 983048 | tf_op jit(solution)/shard_map/L_wp/ppermute | solution.py:288
  42.3 1.4 collective-permute-done.11.refs_5_
  45.5 1.8 collective-permute-start.14
  47.5 9.3 %collective-permute-done.15.refs_7_ = bf16[8,20480]{1,0:T(8,128)(2,1)} collective-permute-done((bf16[8,20480]{1,0:T(8,128)(2,1)S(1)}, bf16[8,20480]{1,0:T(8,128)(2,1)}, u32[]{:S(2)}, u32[]{:S(2)}) %collective-permute-start.15) | collective-permute-done | bytes 327712 | tf_op jit(solution)/shard_map/L_wp/ppermute | solution.py:288
  59.0 2.7 %collective-permute-start.18 = (bf16[8,10240]{1,0:T(8,128)(2,1)S(1)}, bf16[8,10240]{1,0:T(8,128)(2,1)S(1)}, u32[]{:S(2)}, u32[]{:S(2)}) collective-permute-start(bf16[8,10240]{1,0:T(8,128)(2,1)S(1)} %slice.29), channel_id=1, source_target_pairs={{0,192},{64,0},{128,64},{192,128},{1,193},{65,1},{129,65},{193,129... | collective-permute-start | bytes 491528 | tf_op jit(solution)/shard_map/L_fh/ppermute | solution.py:288
  61.8 3.6 %collective-permute-start = (s32[4,6]{1,0:T(4,128)S(1)}, s32[4,6]{1,0:T(4,128)S(1)}, u32[]{:S(2)}, u32[]{:S(2)}) collective-permute-start(s32[4,6]{1,0:T(4,128)S(1)} %pad_add_fusion.tab_ref), channel_id=1, source_target_pairs={{0,8},{8,0},{1,9},{9,1},{2,10},{10,2},{3,11},{11,3},{4,12},{12,4},... | collective-permute-start | bytes 296 | tf_op jit(solution)/shard_map/L_swap/ppermute | solution.py:293
  66.9 9.9 %forward_first.1 = (bf16[8,2,128,128]{3,2,1,0:T(8,128)(2,1)}, bf16[4,8,128,256]{3,2,1,0:T(8,128)(2,1)}, bf16[4,8,128,256]{3,2,1,0:T(8,128)(2,1)}) custom-call(s32[4]{0:T(128)S(1)} %pad_add_fusion.1.pos_ref, s32[128,8]{1,0:T(8,128)S(1)} %copy.16.cols_ref, s32[4,6]{1,0:T(4,128)S(1)} %pad_add_fusion.tab_ref, s32[4,6]{1,0:T(4,128)S(1)} %collective-permute-done.sib_tab_ref, ...), custom_call_target="tpu_custom_call" | custom-call | flops 2147483648 | bytes 16777216 | tf_op jit(solution)/shard_map/forward_first/pallas_call | solution.py:119
  76.8 4.2 %all-to-all-start = ((bf16[8,2,128,128]{3,2,1,0:T(8,128)(2,1)}), bf16[8,2,128,128]{3,2,1,0:T(8,128)(2,1)S(1)}, u32[]{:S(2)}, u32[]{:S(2)}) async-start(bf16[8,2,128,128]{3,2,1,0:T(8,128)(2,1)} %get-tuple-element.60), calls=%async_computation | async-start | bytes 1048576 | tf_op jit(solution)/shard_map/all_to_all | solution.py:334
  81.1 2.3 %collective-permute-start.19 = (f32[2,128]{1,0:T(2,128)S(1)}, f32[2,128]{1,0:T(2,128)S(1)}, u32[]{:S(2)}, u32[]{:S(2)}) collective-permute-start(f32[2,128]{1,0:T(2,128)S(1)} %get-tuple-element.86), channel_id=1, source_target_pairs={{0,8},{8,0},{1,9},{9,1},{2,10},{10,2},{3,11},{11,3},{4,12},{12,4},... | collective-permute-start | bytes 3080 | tf_op jit(solution)/shard_map/L_swap/ppermute | solution.py:293
  84.2 4.1 %all-to-all-done = bf16[8,2,128,128]{3,2,1,0:T(8,128)(2,1)S(1)} async-done(((bf16[8,2,128,128]{3,2,1,0:T(8,128)(2,1)}), bf16[8,2,128,128]{3,2,1,0:T(8,128)(2,1)S(1)}, u32[]{:S(2)}, u32[]{:S(2)}) %all-to-all-start) | async-done | bytes 524320 | tf_op jit(solution)/shard_map/all_to_all | solution.py:334
  88.3 1.6 collective-permute-start.20
  89.9 5.2 %collective-permute-start.21 = (bf16[2,128,128]{2,1,0:T(8,128)(2,1)S(1)}, bf16[2,128,128]{2,1,0:T(8,128)(2,1)S(1)}, u32[]{:S(2)}, u32[]{:S(2)}) collective-permute-start(bf16[2,128,128]{2,1,0:T(8,128)(2,1)S(1)} %tanh_convert_fusion.1), channel_id=1, source_target_pairs={{0,32},{16,48},{32,0},{48,16},{1,33},{17,49},{33,1},{49,17},{2,34}... | collective-permute-start | bytes 196616 | tf_op jit(solution)/shard_map/L_ring/ppermute | solution.py:288
  95.1 1.9 collective-permute-start.22
  97.1 4.5 %collective-permute-done.22 = bf16[2,128,128]{2,1,0:T(8,128)(2,1)S(1)} collective-permute-done((bf16[2,128,128]{2,1,0:T(8,128)(2,1)S(1)}, bf16[2,128,128]{2,1,0:T(8,128)(2,1)S(1)}, u32[]{:S(2)}, u32[]{:S(2)}) %collective-permute-start.22) | collective-permute-done | bytes 65568 | tf_op jit(solution)/shard_map/L_ring/ppermute | solution.py:288
  101.9 1.2 collective-permute-start.25
  103.2 3.7 %collective-permute-done.23.refs_1_ = bf16[4,2,128,128]{3,2,1,0:T(8,128)(2,1)S(1)} collective-permute-done((bf16[4,2,128,128]{3,2,1,0:T(8,128)(2,1)S(1)}, bf16[4,2,128,128]{3,2,1,0:T(8,128)(2,1)S(1)}, u32[]{:S(2)}, u32[]{:S(2)}) %collective-permute-start.23) | collective-permute-done | bytes 262176 | tf_op jit(solution)/shard_map/L_ring/ppermute | solution.py:288
  106.9 1.8 collective-permute-done.24.refs_2_
  108.8 2.7 %collective-permute-done.25.refs_3_ = bf16[4,2,128,128]{3,2,1,0:T(8,128)(2,1)S(1)} collective-permute-done((bf16[4,2,128,128]{3,2,1,0:T(8,128)(2,1)S(1)}, bf16[4,2,128,128]{3,2,1,0:T(8,128)(2,1)S(1)}, u32[]{:S(2)}, u32[]{:S(2)}) %collective-permute-start.25) | collective-permute-done | bytes 262176 | tf_op jit(solution)/shard_map/L_ring/ppermute | solution.py:288
  111.5 5.1 %forward_second.1 = (bf16[8,2,128,128]{3,2,1,0:T(8,128)(2,1)}, bf16[4,4,128,256]{3,2,1,0:T(8,128)(2,1)}, bf16[4,4,128,256]{3,2,1,0:T(8,128)(2,1)}) custom-call(s32[4]{0:T(128)S(1)} %pad_add_fusion.1.pos_ref, s32[4,6]{1,0:T(4,128)S(1)} %pad_add_fusion.tab_ref, s32[4,6]{1,0:T(4,128)S(1)} %collective-permute-done.sib_tab_ref, ...), custom_call_target="tpu_custom_call" | custom-call | flops 1073741824 | bytes 8388608 | tf_op jit(solution)/shard_map/forward_second/pallas_call | solution.py:174
  116.6 4.7 %all-to-all-start.1 = ((bf16[8,2,128,128]{3,2,1,0:T(8,128)(2,1)}), bf16[8,2,128,128]{3,2,1,0:T(8,128)(2,1)S(1)}, u32[]{:S(2)}, u32[]{:S(2)}) async-start(bf16[8,2,128,128]{3,2,1,0:T(8,128)(2,1)} %get-tuple-element.61), calls=%async_computation.1 | async-start | bytes 1048576 | tf_op jit(solution)/shard_map/all_to_all | solution.py:334
  121.3 8.8 %collective-permute-start.1 = (bf16[16,8,128]{2,1,0:T(8,128)(2,1)S(1)}, bf16[16,8,128]{2,1,0:T(8,128)(2,1)S(1)}, u32[]{:S(2)}, u32[]{:S(2)}) collective-permute-start(bf16[16,8,128]{2,1,0:T(8,128)(2,1)S(1)} %get-tuple-element.82), channel_id=1, source_target_pairs={{0,8},{8,0},{1,9},{9,1},{2,10},{10,2},{3,11},{11,3},{4,12},{12,4},... | collective-permute-start | bytes 98312 | tf_op jit(solution)/shard_map/L_swap/ppermute | solution.py:293
  131.9 5.3 %all-to-all-start.2 = ((bf16[8,2,128,128]{3,2,1,0:T(8,128)(2,1)}), bf16[8,2,128,128]{3,2,1,0:T(8,128)(2,1)S(1)}, u32[]{:S(2)}, u32[]{:S(2)}) async-start(bf16[8,2,128,128]{3,2,1,0:T(8,128)(2,1)} %broadcast_in_dim.4), calls=%async_computation.2 | async-start | bytes 1048576 | tf_op jit(solution)/shard_map/all_to_all | solution.py:330
  137.3 5.6 %collective-permute-start.36 = (bf16[4,8,128,256]{3,2,1,0:T(8,128)(2,1)}, bf16[4,8,128,256]{3,2,1,0:T(8,128)(2,1)}, u32[]{:S(2)}, u32[]{:S(2)}) collective-permute-start(bf16[4,8,128,256]{3,2,1,0:T(8,128)(2,1)} %get-tuple-element.74), channel_id=1, source_target_pairs={{0,8},{8,0},{1,9},{9,1},{2,10},{10,2},{3,11},{11,3},{4,12},{12,4},... | collective-permute-start | bytes 6291464 | tf_op jit(solution)/shard_map/L_swap/ppermute | solution.py:293
  142.8 1.6 all-to-all-done.2.d_ref.refs_0_
  144.4 4.4 %adjoint_second.1 = (bf16[4,2,128,128]{3,2,1,0:T(8,128)(2,1)S(1)}, bf16[4,2,128,128]{3,2,1,0:T(8,128)(2,1)S(1)}, bf16[4,2,128,128]{3,2,1,0:T(8,128)(2,1)S(1)}, bf16[4,2,128,128]{3,2,1,0:T(8,128)(2,1)S(1)}) custom-call(s32[4]{0:T(128)S(1)} %pad_add_fusion.1.pos_ref, s32[4,6]{1,0:T(4,128)S(1)} %pad_add_fusion.tab_ref, ...), custom_call_target="tpu_custom_call" | custom-call | flops 1073741824 | bytes 8388608 | tf_op jit(solution)/shard_map/adjoint_second/pallas_call | solution.py:215
  148.9 1.5 collective-permute-start.28
  151.6 6.6 %collective-permute-done.27.refs_1_ = bf16[4,2,128,128]{3,2,1,0:T(8,128)(2,1)S(1)} collective-permute-done((bf16[4,2,128,128]{3,2,1,0:T(8,128)(2,1)S(1)}, bf16[4,2,128,128]{3,2,1,0:T(8,128)(2,1)S(1)}, u32[]{:S(2)}, u32[]{:S(2)}) %collective-permute-start.27) | collective-permute-done | bytes 262176 | tf_op jit(solution)/shard_map/L_ring/ppermute | solution.py:288
  158.9 1.4 collective-permute-start.30
  160.3 3.7 %collective-permute-start.31 = (bf16[2,128,128]{2,1,0:T(8,128)(2,1)S(1)}, bf16[2,128,128]{2,1,0:T(8,128)(2,1)S(1)}, u32[]{:S(2)}, u32[]{:S(2)}) collective-permute-start(bf16[2,128,128]{2,1,0:T(8,128)(2,1)S(1)} %get-tuple-element.68), channel_id=1, source_target_pairs={{0,32},{16,48},{32,0},{48,16},{1,33},{17,49},{33,1},{49,17},{2,34}... | collective-permute-start | bytes 196616 | tf_op jit(solution)/shard_map/L_ring/ppermute | solution.py:288
  164.0 2.2 %collective-permute-start.32 = (bf16[2,128,128]{2,1,0:T(8,128)(2,1)S(1)}, bf16[2,128,128]{2,1,0:T(8,128)(2,1)S(1)}, u32[]{:S(2)}, u32[]{:S(2)}) collective-permute-start(bf16[2,128,128]{2,1,0:T(8,128)(2,1)S(1)} %get-tuple-element.69), channel_id=1, source_target_pairs={{0,48},{16,0},{32,16},{48,32},{1,49},{17,1},{33,17},{49,33},{2,50}... | collective-permute-start | bytes 196616 | tf_op jit(solution)/shard_map/L_ring/ppermute | solution.py:288
  166.2 8.8 %collective-permute-start.33 = (bf16[4,4,128,256]{3,2,1,0:T(8,128)(2,1)}, bf16[4,4,128,256]{3,2,1,0:T(8,128)(2,1)S(1)}, u32[]{:S(2)}, u32[]{:S(2)}) collective-permute-start(bf16[4,4,128,256]{3,2,1,0:T(8,128)(2,1)} %get-tuple-element.71), channel_id=1, source_target_pairs={{0,8},{8,0},{1,9},{9,1},{2,10},{10,2},{3,11},{11,3},{4,12},{12,4},... | collective-permute-start | bytes 3145736 | tf_op jit(solution)/shard_map/L_swap/ppermute | solution.py:293
  176.1 7.0 %all-to-all-start.3 = ((bf16[16,128,128]{2,1,0:T(8,128)(2,1)}), bf16[16,128,128]{2,1,0:T(8,128)(2,1)S(1)}, u32[]{:S(2)}, u32[]{:S(2)}) async-start(bf16[16,128,128]{2,1,0:T(8,128)(2,1)} %bitcast.18), calls=%async_computation.3 | async-start | bytes 1048576 | tf_op jit(solution)/shard_map/all_to_all | solution.py:395
  186.4 1.2 copy-done.2
  188.9 2.8 %grad_second.1 = bf16[4,4,256,256]{3,2,1,0:T(8,128)(2,1)} custom-call(s32[4]{0:T(128)S(1)} %pad_add_fusion.1.pos_ref, s32[4,6]{1,0:T(4,128)S(1)} %pad_add_fusion.tab_ref, bf16[4,4,128,256]{3,2,1,0:T(8,128)(2,1)S(1)} %copy-done.2, bf16[4,4,128,256]{3,2,1,0:T(8,128)(2,1)S(1)} %copy-done.4, bf16[8,2,128,128]{3,2,1,0:T(8,128)(2,1)S(1)} %all-to-all-done.2.d_ref.refs_0_, ...), custom_call_target="tpu_custom_call" | custom-call | flops 536870912 | bytes 4194304 | tf_op jit(solution)/shard_map/grad_second/pallas_call | solution.py:268
  191.7 2.0 %all-to-all-done.3 = bf16[16,128,128]{2,1,0:T(8,128)(2,1)S(1)} async-done(((bf16[16,128,128]{2,1,0:T(8,128)(2,1)}), bf16[16,128,128]{2,1,0:T(8,128)(2,1)S(1)}, u32[]{:S(2)}, u32[]{:S(2)}) %all-to-all-start.3) | async-done | bytes 524320 | tf_op jit(solution)/shard_map/all_to_all | solution.py:395
  193.6 4.5 %grad_first.1 = bf16[4,8,256,256]{3,2,1,0:T(8,128)(2,1)} custom-call(s32[4]{0:T(128)S(1)} %pad_add_fusion.1.pos_ref, s32[4,6]{1,0:T(4,128)S(1)} %pad_add_fusion.tab_ref, bf16[4,8,128,256]{3,2,1,0:T(8,128)(2,1)S(1)} %copy-done.1, bf16[4,8,128,256]{3,2,1,0:T(8,128)(2,1)} %collective-permute-done.36.po_ref, bf16[2,8,128,128]{3,2,1,0:T(8,128)(2,1)S(1)} %bitcast.40), custom_call_target="tpu_custom_call" | custom-call | flops 1073741824 | bytes 8388608 | tf_op jit(solution)/shard_map/grad_first/pallas_call | solution.py:268
  (110 shorter events, 19.2 us)
Async XLA Ops:
  0.6 46.7 %copy-start.16 = (s32[4,1]{0,1:T(1,128)S(1)}, s32[4,1]{0,1:T(1,128)}, u32[]{:S(2)}) copy-start(s32[4,1]{0,1:T(1,128)} %param.12) | copy-start | bytes 52
  0.6 46.8 %copy-start.17 = (s32[4,1]{0,1:T(1,128)S(1)}, s32[4,1]{0,1:T(1,128)}, u32[]{:S(2)}) copy-start(s32[4,1]{0,1:T(1,128)} %param.16) | copy-start | bytes 52
  0.7 26.5 %collective-permute-start.8 = (bf16[4,8,256,256]{3,2,1,0:T(8,128)(2,1)}, bf16[4,8,256,256]{3,2,1,0:T(8,128)(2,1)}, u32[]{:S(2)}, u32[]{:S(2)}) collective-permute-start(bf16[4,8,256,256]{3,2,1,0:T(8,128)(2,1)} %refs_14_.1), channel_id=1, source_target_pairs={{0,8},{8,0},{1,9},{9,1},{2,10},{10,2},{3,11},{11,3},{4,12},{12,4},... | collective-permute-start | bytes 12582920 | tf_op jit(solution)/shard_map/L_w1/ppermute | solution.py:293
  4.0 10.7 %collective-permute-start.2 = (bf16[8,20480]{1,0:T(8,128)(2,1)}, bf16[8,20480]{1,0:T(8,128)(2,1)S(1)}, u32[]{:S(2)}, u32[]{:S(2)}) collective-permute-start(bf16[8,20480]{1,0:T(8,128)(2,1)} %refs_0_.1), channel_id=1, source_target_pairs={{0,64},{64,128},{128,192},{192,0},{1,65},{65,129},{129,193},{193,1... | collective-permute-start | bytes 983048 | tf_op jit(solution)/shard_map/L_xp/ppermute | solution.py:288
  4.0 10.7 %collective-permute-start.3 = (bf16[8,20480]{1,0:T(8,128)(2,1)}, bf16[8,20480]{1,0:T(8,128)(2,1)S(1)}, u32[]{:S(2)}, u32[]{:S(2)}) collective-permute-start(bf16[8,20480]{1,0:T(8,128)(2,1)} %refs_0_.1), channel_id=1, source_target_pairs={{0,192},{64,0},{128,64},{192,128},{1,193},{65,1},{129,65},{193,129... | collective-permute-start | bytes 983048 | tf_op jit(solution)/shard_map/L_xn/ppermute | solution.py:288
  6.7 14.0 %collective-permute-start.4 = (bf16[8,20480]{1,0:T(8,128)(2,1)}, bf16[8,20480]{1,0:T(8,128)(2,1)S(1)}, u32[]{:S(2)}, u32[]{:S(2)}) collective-permute-start(bf16[8,20480]{1,0:T(8,128)(2,1)} %refs_0_.1), channel_id=1, source_target_pairs={{0,16},{16,32},{32,48},{48,0},{1,17},{17,33},{33,49},{49,1},{2,18}... | collective-permute-start | bytes 983048 | tf_op jit(solution)/shard_map/L_zp/ppermute | solution.py:288
  7.9 19.2 %collective-permute-start.5 = (bf16[8,20480]{1,0:T(8,128)(2,1)}, bf16[8,20480]{1,0:T(8,128)(2,1)S(1)}, u32[]{:S(2)}, u32[]{:S(2)}) collective-permute-start(bf16[8,20480]{1,0:T(8,128)(2,1)} %refs_0_.1), channel_id=1, source_target_pairs={{0,48},{16,0},{32,16},{48,32},{1,49},{17,1},{33,17},{49,33},{2,50}... | collective-permute-start | bytes 983048 | tf_op jit(solution)/shard_map/L_zn/ppermute | solution.py:288
  14.7 43.1 %copy-start.8 = (bf16[8,20480]{1,0:T(8,128)(2,1)}, bf16[8,20480]{1,0:T(8,128)(2,1)S(1)}, u32[]{:S(2)}) copy-start(bf16[8,20480]{1,0:T(8,128)(2,1)S(1)} %collective-permute-done.2.refs_1_) | copy-start | bytes 983044
  14.7 47.0 %copy-start.15 = (s32[4,4]{1,0:T(4,128)S(1)}, s32[4,4]{1,0:T(4,128)}, u32[]{:S(2)}) copy-start(s32[4,4]{1,0:T(4,128)} %param.15) | copy-start | bytes 196
  14.7 50.7 %copy-start = (bf16[4,4,256,256]{3,2,1,0:T(8,128)(2,1)S(1)}, bf16[4,4,256,256]{3,2,1,0:T(8,128)(2,1)}, u32[]{:S(2)}) copy-start(bf16[4,4,256,256]{3,2,1,0:T(8,128)(2,1)} %own_ref.1) | copy-start | bytes 6291460
  14.7 50.9 %copy-start.14 = (s32[128,8]{0,1:T(8,128)S(1)}, s32[128,8]{0,1:T(8,128)}, u32[]{:S(2)}) copy-start(s32[128,8]{0,1:T(8,128)} %param.11) | copy-start | bytes 12292
  14.7 12.4 %collective-permute-start.6 = (bf16[8,10240]{1,0:T(8,128)(2,1)S(1)}, bf16[8,10240]{1,0:T(8,128)(2,1)S(1)}, u32[]{:S(2)}, u32[]{:S(2)}) collective-permute-start(bf16[8,10240]{1,0:T(8,128)(2,1)S(1)} %slice.24), channel_id=1, source_target_pairs={{0,64},{64,128},{128,192},{192,0},{1,65},{65,129},{129,193},{193,1... | collective-permute-start | bytes 491528 | tf_op jit(solution)/shard_map/L_xl/ppermute | solution.py:288
  14.8 12.3 %collective-permute-start.7 = (bf16[8,10240]{1,0:T(8,128)(2,1)S(1)}, bf16[8,10240]{1,0:T(8,128)(2,1)S(1)}, u32[]{:S(2)}, u32[]{:S(2)}) collective-permute-start(bf16[8,10240]{1,0:T(8,128)(2,1)S(1)} %slice.25), channel_id=1, source_target_pairs={{0,192},{64,0},{128,64},{192,128},{1,193},{65,1},{129,65},{193,129... | collective-permute-start | bytes 491528 | tf_op jit(solution)/shard_map/L_xh/ppermute | solution.py:288
  27.2 16.6 %collective-permute-start.11 = (bf16[16,20480]{1,0:T(8,128)(2,1)S(1)}, bf16[16,20480]{1,0:T(8,128)(2,1)S(1)}, u32[]{:S(2)}, u32[]{:S(2)}) collective-permute-start(bf16[16,20480]{1,0:T(8,128)(2,1)S(1)} %pad_maximum_fusion.refs_4_), channel_id=1, source_target_pairs={{0,64},{64,128},{128,192},{192,0},{1,65},{65,129},{129,193},{193,1... | collective-permute-start | bytes 1966088 | tf_op jit(solution)/shard_map/L_tp/ppermute | solution.py:288
  28.0 15.8 %collective-permute-start.12 = (bf16[16,20480]{1,0:T(8,128)(2,1)S(1)}, bf16[16,20480]{1,0:T(8,128)(2,1)S(1)}, u32[]{:S(2)}, u32[]{:S(2)}) collective-permute-start(bf16[16,20480]{1,0:T(8,128)(2,1)S(1)} %pad_maximum_fusion.refs_4_), channel_id=1, source_target_pairs={{0,192},{64,0},{128,64},{192,128},{1,193},{65,1},{129,65},{193,129... | collective-permute-start | bytes 1966088 | tf_op jit(solution)/shard_map/L_tn/ppermute | solution.py:288
  30.0 6.5 %collective-permute-start.10 = (bf16[8,10240]{1,0:T(8,128)(2,1)S(1)}, bf16[8,10240]{1,0:T(8,128)(2,1)S(1)}, u32[]{:S(2)}, u32[]{:S(2)}) collective-permute-start(bf16[8,10240]{1,0:T(8,128)(2,1)S(1)} %slice.27), channel_id=1, source_target_pairs={{0,48},{16,0},{32,16},{48,32},{1,49},{17,1},{33,17},{49,33},{2,50}... | collective-permute-start | bytes 491528 | tf_op jit(solution)/shard_map/L_zr/ppermute | solution.py:288
  32.3 6.4 %collective-permute-start.9 = (bf16[8,10240]{1,0:T(8,128)(2,1)S(1)}, bf16[8,10240]{1,0:T(8,128)(2,1)S(1)}, u32[]{:S(2)}, u32[]{:S(2)}) collective-permute-start(bf16[8,10240]{1,0:T(8,128)(2,1)S(1)} %slice.26), channel_id=1, source_target_pairs={{0,16},{16,32},{32,48},{48,0},{1,17},{17,33},{33,49},{49,1},{2,18}... | collective-permute-start | bytes 491528 | tf_op jit(solution)/shard_map/L_zl/ppermute | solution.py:288
  33.1 33.2 %copy-start.6 = (bf16[8,20480]{1,0:T(8,128)(2,1)}, bf16[8,20480]{1,0:T(8,128)(2,1)S(1)}, u32[]{:S(2)}) copy-start(bf16[8,20480]{1,0:T(8,128)(2,1)S(1)} %pad_maximum_fusion.1.refs_3_) | copy-start | bytes 983044
  38.7 18.1 %collective-permute-start.15 = (bf16[8,20480]{1,0:T(8,128)(2,1)S(1)}, bf16[8,20480]{1,0:T(8,128)(2,1)}, u32[]{:S(2)}, u32[]{:S(2)}) collective-permute-start(bf16[8,20480]{1,0:T(8,128)(2,1)S(1)} %pad_maximum_fusion.1.refs_3_), channel_id=1, source_target_pairs={{0,16},{16,32},{32,48},{48,0},{1,17},{17,33},{33,49},{49,1},{2,18}... | collective-permute-start | bytes 983048 | tf_op jit(solution)/shard_map/L_wp/ppermute | solution.py:288
  41.2 15.6 %collective-permute-start.16 = (bf16[8,20480]{1,0:T(8,128)(2,1)S(1)}, bf16[8,20480]{1,0:T(8,128)(2,1)}, u32[]{:S(2)}, u32[]{:S(2)}) collective-permute-start(bf16[8,20480]{1,0:T(8,128)(2,1)S(1)} %pad_maximum_fusion.1.refs_3_), channel_id=1, source_target_pairs={{0,48},{16,0},{32,16},{48,32},{1,49},{17,1},{33,17},{49,33},{2,50}... | collective-permute-start | bytes 983048 | tf_op jit(solution)/shard_map/L_wn/ppermute | solution.py:288
  44.6 12.2 %collective-permute-start.13 = (bf16[8,20480]{1,0:T(8,128)(2,1)S(1)}, bf16[8,20480]{1,0:T(8,128)(2,1)}, u32[]{:S(2)}, u32[]{:S(2)}) collective-permute-start(bf16[8,20480]{1,0:T(8,128)(2,1)S(1)} %pad_maximum_fusion.2.refs_9_), channel_id=1, source_target_pairs={{0,64},{64,128},{128,192},{192,0},{1,65},{65,129},{129,193},{193,1... | collective-permute-start | bytes 983048 | tf_op jit(solution)/shard_map/L_fp/ppermute | solution.py:288
  45.5 11.3 %collective-permute-start.14 = (bf16[8,20480]{1,0:T(8,128)(2,1)S(1)}, bf16[8,20480]{1,0:T(8,128)(2,1)}, u32[]{:S(2)}, u32[]{:S(2)}) collective-permute-start(bf16[8,20480]{1,0:T(8,128)(2,1)S(1)} %pad_maximum_fusion.2.refs_9_), channel_id=1, source_target_pairs={{0,192},{64,0},{128,64},{192,128},{1,193},{65,1},{129,65},{193,129... | collective-permute-start | bytes 983048 | tf_op jit(solution)/shard_map/L_fn/ppermute | solution.py:288
  57.8 8.5 %collective-permute-start.17 = (bf16[8,10240]{1,0:T(8,128)(2,1)S(1)}, bf16[8,10240]{1,0:T(8,128)(2,1)}, u32[]{:S(2)}, u32[]{:S(2)}) collective-permute-start(bf16[8,10240]{1,0:T(8,128)(2,1)S(1)} %slice.28), channel_id=1, source_target_pairs={{0,64},{64,128},{128,192},{192,0},{1,65},{65,129},{129,193},{193,1... | collective-permute-start | bytes 491528 | tf_op jit(solution)/shard_map/L_fl/ppermute | solution.py:288
  59.0 7.3 %collective-permute-start.18 = (bf16[8,10240]{1,0:T(8,128)(2,1)S(1)}, bf16[8,10240]{1,0:T(8,128)(2,1)S(1)}, u32[]{:S(2)}, u32[]{:S(2)}) collective-permute-start(bf16[8,10240]{1,0:T(8,128)(2,1)S(1)} %slice.29), channel_id=1, source_target_pairs={{0,192},{64,0},{128,64},{192,128},{1,193},{65,1},{129,65},{193,129... | collective-permute-start | bytes 491528 | tf_op jit(solution)/shard_map/L_fh/ppermute | solution.py:288
  61.8 4.5 %collective-permute-start = (s32[4,6]{1,0:T(4,128)S(1)}, s32[4,6]{1,0:T(4,128)S(1)}, u32[]{:S(2)}, u32[]{:S(2)}) collective-permute-start(s32[4,6]{1,0:T(4,128)S(1)} %pad_add_fusion.tab_ref), channel_id=1, source_target_pairs={{0,8},{8,0},{1,9},{9,1},{2,10},{10,2},{3,11},{11,3},{4,12},{12,4},... | collective-permute-start | bytes 296 | tf_op jit(solution)/shard_map/L_swap/ppermute | solution.py:293
  65.4 37.7 %collective-permute-start.26 = (bf16[4,4,256,256]{3,2,1,0:T(8,128)(2,1)S(1)}, bf16[4,4,256,256]{3,2,1,0:T(8,128)(2,1)}, u32[]{:S(2)}, u32[]{:S(2)}) collective-permute-start(bf16[4,4,256,256]{3,2,1,0:T(8,128)(2,1)S(1)} %copy-done), channel_id=1, source_target_pairs={{0,8},{8,0},{1,9},{9,1},{2,10},{10,2},{3,11},{11,3},{4,12},{12,4},... | collective-permute-start | bytes 6291464 | tf_op jit(solution)/shard_map/L_swap/ppermute | solution.py:293
  76.8 11.4 %all-to-all-start = ((bf16[8,2,128,128]{3,2,1,0:T(8,128)(2,1)}), bf16[8,2,128,128]{3,2,1,0:T(8,128)(2,1)S(1)}, u32[]{:S(2)}, u32[]{:S(2)}) async-start(bf16[8,2,128,128]{3,2,1,0:T(8,128)(2,1)} %get-tuple-element.60), calls=%async_computation | async-start | bytes 1048576 | tf_op jit(solution)/shard_map/all_to_all | solution.py:334
  81.1 3.1 %collective-permute-start.19 = (f32[2,128]{1,0:T(2,128)S(1)}, f32[2,128]{1,0:T(2,128)S(1)}, u32[]{:S(2)}, u32[]{:S(2)}) collective-permute-start(f32[2,128]{1,0:T(2,128)S(1)} %get-tuple-element.86), channel_id=1, source_target_pairs={{0,8},{8,0},{1,9},{9,1},{2,10},{10,2},{3,11},{11,3},{4,12},{12,4},... | collective-permute-start | bytes 3080 | tf_op jit(solution)/shard_map/L_swap/ppermute | solution.py:293
  88.3 8.8 %collective-permute-start.20 = (bf16[2,128,128]{2,1,0:T(8,128)(2,1)S(1)}, bf16[2,128,128]{2,1,0:T(8,128)(2,1)S(1)}, u32[]{:S(2)}, u32[]{:S(2)}) collective-permute-start(bf16[2,128,128]{2,1,0:T(8,128)(2,1)S(1)} %tanh_convert_fusion.1), channel_id=1, source_target_pairs={{0,48},{16,0},{32,16},{48,32},{1,49},{17,1},{33,17},{49,33},{2,50}... | collective-permute-start | bytes 196616 | tf_op jit(solution)/shard_map/L_ring/ppermute | solution.py:288
  89.9 7.2 %collective-permute-start.21 = (bf16[2,128,128]{2,1,0:T(8,128)(2,1)S(1)}, bf16[2,128,128]{2,1,0:T(8,128)(2,1)S(1)}, u32[]{:S(2)}, u32[]{:S(2)}) collective-permute-start(bf16[2,128,128]{2,1,0:T(8,128)(2,1)S(1)} %tanh_convert_fusion.1), channel_id=1, source_target_pairs={{0,32},{16,48},{32,0},{48,16},{1,33},{17,49},{33,1},{49,17},{2,34}... | collective-permute-start | bytes 196616 | tf_op jit(solution)/shard_map/L_ring/ppermute | solution.py:288
  95.1 6.4 %collective-permute-start.22 = (bf16[2,128,128]{2,1,0:T(8,128)(2,1)S(1)}, bf16[2,128,128]{2,1,0:T(8,128)(2,1)S(1)}, u32[]{:S(2)}, u32[]{:S(2)}) collective-permute-start(bf16[2,128,128]{2,1,0:T(8,128)(2,1)S(1)} %tanh_convert_fusion.1), channel_id=1, source_target_pairs={{0,16},{16,32},{32,48},{48,0},{1,17},{17,33},{33,49},{49,1},{2,18}... | collective-permute-start | bytes 196616 | tf_op jit(solution)/shard_map/L_ring/ppermute | solution.py:288
  101.6 5.3 %collective-permute-start.23 = (bf16[4,2,128,128]{3,2,1,0:T(8,128)(2,1)S(1)}, bf16[4,2,128,128]{3,2,1,0:T(8,128)(2,1)S(1)}, u32[]{:S(2)}, u32[]{:S(2)}) collective-permute-start(bf16[4,2,128,128]{3,2,1,0:T(8,128)(2,1)S(1)} %pad_maximum_fusion.3.refs_0_), channel_id=1, source_target_pairs={{0,192},{64,0},{128,64},{192,128},{1,193},{65,1},{129,65},{193,129... | collective-permute-start | bytes 786440 | tf_op jit(solution)/shard_map/L_ring/ppermute | solution.py:288
  101.9 6.8 %collective-permute-start.24 = (bf16[4,2,128,128]{3,2,1,0:T(8,128)(2,1)S(1)}, bf16[4,2,128,128]{3,2,1,0:T(8,128)(2,1)S(1)}, u32[]{:S(2)}, u32[]{:S(2)}) collective-permute-start(bf16[4,2,128,128]{3,2,1,0:T(8,128)(2,1)S(1)} %pad_maximum_fusion.3.refs_0_), channel_id=1, source_target_pairs={{0,128},{64,192},{128,0},{192,64},{1,129},{65,193},{129,1},{193,65... | collective-permute-start | bytes 786440 | tf_op jit(solution)/shard_map/L_ring/ppermute | solution.py:288
  101.9 9.5 %collective-permute-start.25 = (bf16[4,2,128,128]{3,2,1,0:T(8,128)(2,1)S(1)}, bf16[4,2,128,128]{3,2,1,0:T(8,128)(2,1)S(1)}, u32[]{:S(2)}, u32[]{:S(2)}) collective-permute-start(bf16[4,2,128,128]{3,2,1,0:T(8,128)(2,1)S(1)} %pad_maximum_fusion.3.refs_0_), channel_id=1, source_target_pairs={{0,64},{64,128},{128,192},{192,0},{1,65},{65,129},{129,193},{193,1... | collective-permute-start | bytes 786440 | tf_op jit(solution)/shard_map/L_ring/ppermute | solution.py:288
  116.6 13.5 %all-to-all-start.1 = ((bf16[8,2,128,128]{3,2,1,0:T(8,128)(2,1)}), bf16[8,2,128,128]{3,2,1,0:T(8,128)(2,1)S(1)}, u32[]{:S(2)}, u32[]{:S(2)}) async-start(bf16[8,2,128,128]{3,2,1,0:T(8,128)(2,1)} %get-tuple-element.61), calls=%async_computation.1 | async-start | bytes 1048576 | tf_op jit(solution)/shard_map/all_to_all | solution.py:334
  121.3 9.6 %collective-permute-start.1 = (bf16[16,8,128]{2,1,0:T(8,128)(2,1)S(1)}, bf16[16,8,128]{2,1,0:T(8,128)(2,1)S(1)}, u32[]{:S(2)}, u32[]{:S(2)}) collective-permute-start(bf16[16,8,128]{2,1,0:T(8,128)(2,1)S(1)} %get-tuple-element.82), channel_id=1, source_target_pairs={{0,8},{8,0},{1,9},{9,1},{2,10},{10,2},{3,11},{11,3},{4,12},{12,4},... | collective-permute-start | bytes 98312 | tf_op jit(solution)/shard_map/L_swap/ppermute | solution.py:293
  131.9 12.5 %all-to-all-start.2 = ((bf16[8,2,128,128]{3,2,1,0:T(8,128)(2,1)}), bf16[8,2,128,128]{3,2,1,0:T(8,128)(2,1)S(1)}, u32[]{:S(2)}, u32[]{:S(2)}) async-start(bf16[8,2,128,128]{3,2,1,0:T(8,128)(2,1)} %broadcast_in_dim.4), calls=%async_computation.2 | async-start | bytes 1048576 | tf_op jit(solution)/shard_map/all_to_all | solution.py:330
  137.3 56.4 %collective-permute-start.36 = (bf16[4,8,128,256]{3,2,1,0:T(8,128)(2,1)}, bf16[4,8,128,256]{3,2,1,0:T(8,128)(2,1)}, u32[]{:S(2)}, u32[]{:S(2)}) collective-permute-start(bf16[4,8,128,256]{3,2,1,0:T(8,128)(2,1)} %get-tuple-element.74), channel_id=1, source_target_pairs={{0,8},{8,0},{1,9},{9,1},{2,10},{10,2},{3,11},{11,3},{4,12},{12,4},... | collective-permute-start | bytes 6291464 | tf_op jit(solution)/shard_map/L_swap/ppermute | solution.py:293
  148.8 9.3 %collective-permute-start.27 = (bf16[4,2,128,128]{3,2,1,0:T(8,128)(2,1)S(1)}, bf16[4,2,128,128]{3,2,1,0:T(8,128)(2,1)S(1)}, u32[]{:S(2)}, u32[]{:S(2)}) collective-permute-start(bf16[4,2,128,128]{3,2,1,0:T(8,128)(2,1)S(1)} %get-tuple-element.63), channel_id=1, source_target_pairs={{0,64},{64,128},{128,192},{192,0},{1,65},{65,129},{129,193},{193,1... | collective-permute-start | bytes 786440 | tf_op jit(solution)/shard_map/L_ring/ppermute | solution.py:288
  148.9 9.2 %collective-permute-start.28 = (bf16[4,2,128,128]{3,2,1,0:T(8,128)(2,1)S(1)}, bf16[4,2,128,128]{3,2,1,0:T(8,128)(2,1)S(1)}, u32[]{:S(2)}, u32[]{:S(2)}) collective-permute-start(bf16[4,2,128,128]{3,2,1,0:T(8,128)(2,1)S(1)} %get-tuple-element.64), channel_id=1, source_target_pairs={{0,128},{64,192},{128,0},{192,64},{1,129},{65,193},{129,1},{193,65... | collective-permute-start | bytes 786440 | tf_op jit(solution)/shard_map/L_ring/ppermute | solution.py:288
  150.4 8.4 %collective-permute-start.29 = (bf16[4,2,128,128]{3,2,1,0:T(8,128)(2,1)S(1)}, bf16[4,2,128,128]{3,2,1,0:T(8,128)(2,1)S(1)}, u32[]{:S(2)}, u32[]{:S(2)}) collective-permute-start(bf16[4,2,128,128]{3,2,1,0:T(8,128)(2,1)S(1)} %get-tuple-element.65), channel_id=1, source_target_pairs={{0,192},{64,0},{128,64},{192,128},{1,193},{65,1},{129,65},{193,129... | collective-permute-start | bytes 786440 | tf_op jit(solution)/shard_map/L_ring/ppermute | solution.py:288
  158.9 16.2 %collective-permute-start.30 = (bf16[2,128,128]{2,1,0:T(8,128)(2,1)S(1)}, bf16[2,128,128]{2,1,0:T(8,128)(2,1)S(1)}, u32[]{:S(2)}, u32[]{:S(2)}) collective-permute-start(bf16[2,128,128]{2,1,0:T(8,128)(2,1)S(1)} %get-tuple-element.67), channel_id=1, source_target_pairs={{0,16},{16,32},{32,48},{48,0},{1,17},{17,33},{33,49},{49,1},{2,18}... | collective-permute-start | bytes 196616 | tf_op jit(solution)/shard_map/L_ring/ppermute | solution.py:288
  160.3 14.8 %collective-permute-start.31 = (bf16[2,128,128]{2,1,0:T(8,128)(2,1)S(1)}, bf16[2,128,128]{2,1,0:T(8,128)(2,1)S(1)}, u32[]{:S(2)}, u32[]{:S(2)}) collective-permute-start(bf16[2,128,128]{2,1,0:T(8,128)(2,1)S(1)} %get-tuple-element.68), channel_id=1, source_target_pairs={{0,32},{16,48},{32,0},{48,16},{1,33},{17,49},{33,1},{49,17},{2,34}... | collective-permute-start | bytes 196616 | tf_op jit(solution)/shard_map/L_ring/ppermute | solution.py:288
  164.0 11.1 %collective-permute-start.32 = (bf16[2,128,128]{2,1,0:T(8,128)(2,1)S(1)}, bf16[2,128,128]{2,1,0:T(8,128)(2,1)S(1)}, u32[]{:S(2)}, u32[]{:S(2)}) collective-permute-start(bf16[2,128,128]{2,1,0:T(8,128)(2,1)S(1)} %get-tuple-element.69), channel_id=1, source_target_pairs={{0,48},{16,0},{32,16},{48,32},{1,49},{17,1},{33,17},{49,33},{2,50}... | collective-permute-start | bytes 196616 | tf_op jit(solution)/shard_map/L_ring/ppermute | solution.py:288
  166.2 19.2 %collective-permute-start.33 = (bf16[4,4,128,256]{3,2,1,0:T(8,128)(2,1)}, bf16[4,4,128,256]{3,2,1,0:T(8,128)(2,1)S(1)}, u32[]{:S(2)}, u32[]{:S(2)}) collective-permute-start(bf16[4,4,128,256]{3,2,1,0:T(8,128)(2,1)} %get-tuple-element.71), channel_id=1, source_target_pairs={{0,8},{8,0},{1,9},{9,1},{2,10},{10,2},{3,11},{11,3},{4,12},{12,4},... | collective-permute-start | bytes 3145736 | tf_op jit(solution)/shard_map/L_swap/ppermute | solution.py:293
  176.1 17.6 %all-to-all-start.3 = ((bf16[16,128,128]{2,1,0:T(8,128)(2,1)}), bf16[16,128,128]{2,1,0:T(8,128)(2,1)S(1)}, u32[]{:S(2)}, u32[]{:S(2)}) async-start(bf16[16,128,128]{2,1,0:T(8,128)(2,1)} %bitcast.18), calls=%async_computation.3 | async-start | bytes 1048576 | tf_op jit(solution)/shard_map/all_to_all | solution.py:395
  183.1 3.3 %collective-permute-start.34 = (bf16[8,128,128]{2,1,0:T(8,128)(2,1)S(1)}, bf16[8,128,128]{2,1,0:T(8,128)(2,1)S(1)}, u32[]{:S(2)}, u32[]{:S(2)}) collective-permute-start(bf16[8,128,128]{2,1,0:T(8,128)(2,1)S(1)} %dynamic-slice_bitcast_fusion), channel_id=1, source_target_pairs={{0,8},{8,0},{1,9},{9,1},{2,10},{10,2},{3,11},{11,3},{4,12},{12,4},... | collective-permute-start | bytes 786440 | tf_op jit(solution)/shard_map/L_swap/ppermute | solution.py:293
  183.4 1.4 collective-permute-start.35
  (13 other events, 103.4 us)

commit v5 on v4

--- a/solution.py
+++ b/solution.py
@@ -288,6 +288,13 @@
         return lax.ppermute(value, axis, [(i, (i + step) % n) for i in range(n)])
 
 
+def shares_of(values, axis, sign):
+    far = ring(values[2], axis, 2, "far")
+    one, three = ring(values[1], axis, sign, "one"), ring(values[3], axis, -sign, "three")
+    far, one, three = together(far, one, three)
+    return [values[0], one, far, three]
+
+
 def swap(value, label="swap"):
     with jax.named_scope("L_" + label):
         return lax.ppermute(value, "core", [(0, 1), (1, 0)])
@@ -373,8 +380,8 @@
     )
     summed_first = sum_axis(partial_first, IN)
     hidden_first = jnp.tanh(summed_first + biases[:, 0][:, None, :]).astype(BF16)
-    along_z = jnp.stack([hidden_first] + [ring(hidden_first, "zh", -k) for k in range(1, NZ)])
-    hidden = [along_z] + [ring(along_z, "x", -k) for k in range(1, NX)]
+    along_z = jnp.stack(shares_of([hidden_first] * NZ, "zh", -1))
+    hidden = shares_of([along_z] * NX, "x", -1)
 
     partial_second, panels_second, lent_second = forward_second(
         pos, table, sib_table, hidden, weight_second, sibling_second
@@ -386,8 +393,8 @@
     rows_second = gather_axis(delta_second, IN)
 
     back = adjoint_second(pos, table, sib_table, rows_second, weight_second, sibling_second)
-    along_x = add_shares([back[0]] + [ring(back[k], "x", k) for k in range(1, NX)])
-    shares = [along_x[0]] + [ring(along_x[k], "zh", k) for k in range(1, NZ)]
+    along_x = add_shares(shares_of(back, "x", 1))
+    shares = shares_of(along_x, "zh", 1)
     back_first = sum(s.astype(F32) for s in shares)
     hid32 = hidden_first.astype(F32)
     delta_first = (back_first * (1.0 - hid32 * hid32)).astype(BF16)

time: 199 us -> 195 us (0.980)
  waiting for transfers between devices: 60.4 us -> 58 us
    ppermute x9, starting transfers between devices: 33.1 us -> 29.8 us  [swap(): return lax.ppermute(value, 'core', [(0, 1), (1, 0)])]
    ppermute x28, waiting for transfers between devices: 49.6 us -> 46.7 us  [ring(): return lax.ppermute(value, axis, [(i, (i + step) % n) for i in range(n)])]
  transfers between devices with their start and end apart: 41 -> 41, of which waited for: 20 -> 21; matrix products, arithmetic and copies ran while one was open for 2% -> 2% of each run, Pallas kernels for 9% -> 9%
where the time goes in v5:
time: 195 us; the launch traced here: 194 us
  starting transfers between devices  96.1 us (49%)
  waiting for transfers between devices  58 us (30%)
  Pallas kernels  26.9 us (14%)
  local copies, waits for them, and re-layouts  10.7 us (5%)
    ppermute x28, waiting for transfers between devices, ring(): return lax.ppermute(value, axis, [(i, (i + step) % n) for i in range(n)])  46.7 us
    ppermute x28, starting transfers between devices, ring(): return lax.ppermute(value, axis, [(i, (i + step) % n) for i in range(n)])  45.2 us
    ppermute x9, starting transfers between devices, swap(): return lax.ppermute(value, 'core', [(0, 1), (1, 0)])  29.8 us
    all_to_all x2, starting transfers between devices, sum_axis(): lax.all_to_all(parts, axis, 0, 0, tiled=True).astype(F32)  10.2 us
    pallas_call x1, Pallas kernels, forward_first(): pl.pallas_call(body, out_shape=(jax.ShapeDtypeStruct((2 * ROWS, 2, frames...  9.91 us
    pallas_call x2, Pallas kernels, weight_grads(): pl.pallas_call(body, out_shape=jax.ShapeDtypeStruct((ROWS, slots, BLK, BL...  7.32 us
    unnamed x43, local copies, waits for them, and re-layouts  6.87 us
    all_to_all x1, starting transfers between devices, shards(): lax.all_to_all(to_all.reshape(-1, *delta_first.shape[1:]), ('core', *IN),...  6.06 us
  transfers between devices with their start and end apart: 41, of which 21 were waited for; matrix products, arithmetic and copies ran while one was open for 2% of the time, Pallas kernels for 9%

profile of v5, /device:TPU:1, one launch (start us, length us, event | category | flops | bytes accessed | tf_op | source)
XLA Modules:
  0.0 194.1 jit_solution(5798672945636626724)
XLA Ops:
  0.7 3.3 %collective-permute-start.8 = (bf16[4,8,256,256]{3,2,1,0:T(8,128)(2,1)}, bf16[4,8,256,256]{3,2,1,0:T(8,128)(2,1)}, u32[]{:S(2)}, u32[]{:S(2)}) collective-permute-start(bf16[4,8,256,256]{3,2,1,0:T(8,128)(2,1)} %refs_14_.1), channel_id=1, source_target_pairs={{0,8},{8,0},{1,9},{9,1},{2,10},{10,2},{3,11},{11,3},{4,12},{12,4},... | collective-permute-start | bytes 12582920 | tf_op jit(solution)/shard_map/L_w1/ppermute | solution.py:300
  4.0 2.7 %collective-permute-start.3 = (bf16[8,20480]{1,0:T(8,128)(2,1)}, bf16[8,20480]{1,0:T(8,128)(2,1)S(1)}, u32[]{:S(2)}, u32[]{:S(2)}) collective-permute-start(bf16[8,20480]{1,0:T(8,128)(2,1)} %refs_0_.1), channel_id=1, source_target_pairs={{0,192},{64,0},{128,64},{192,128},{1,193},{65,1},{129,65},{193,129... | collective-permute-start | bytes 983048 | tf_op jit(solution)/shard_map/L_xn/ppermute | solution.py:288
  6.7 1.3 collective-permute-start.4
  7.9 3.0 %collective-permute-start.5 = (bf16[8,20480]{1,0:T(8,128)(2,1)}, bf16[8,20480]{1,0:T(8,128)(2,1)S(1)}, u32[]{:S(2)}, u32[]{:S(2)}) collective-permute-start(bf16[8,20480]{1,0:T(8,128)(2,1)} %refs_0_.1), channel_id=1, source_target_pairs={{0,48},{16,0},{32,16},{48,32},{1,49},{17,1},{33,17},{49,33},{2,50}... | collective-permute-start | bytes 983048 | tf_op jit(solution)/shard_map/L_zn/ppermute | solution.py:288
  11.0 3.7 %collective-permute-done.2.refs_1_ = bf16[8,20480]{1,0:T(8,128)(2,1)S(1)} collective-permute-done((bf16[8,20480]{1,0:T(8,128)(2,1)}, bf16[8,20480]{1,0:T(8,128)(2,1)S(1)}, u32[]{:S(2)}, u32[]{:S(2)}) %collective-permute-start.2) | collective-permute-done | bytes 327712 | tf_op jit(solution)/shard_map/L_xp/ppermute | solution.py:288
  14.8 2.7 %collective-permute-start.7 = (bf16[8,10240]{1,0:T(8,128)(2,1)S(1)}, bf16[8,10240]{1,0:T(8,128)(2,1)S(1)}, u32[]{:S(2)}, u32[]{:S(2)}) collective-permute-start(bf16[8,10240]{1,0:T(8,128)(2,1)S(1)} %slice.25), channel_id=1, source_target_pairs={{0,192},{64,0},{128,64},{192,128},{1,193},{65,1},{129,65},{193,129... | collective-permute-start | bytes 491528 | tf_op jit(solution)/shard_map/L_xh/ppermute | solution.py:288
  17.6 3.1 %collective-permute-done.4 = bf16[8,20480]{1,0:T(8,128)(2,1)S(1)} collective-permute-done((bf16[8,20480]{1,0:T(8,128)(2,1)}, bf16[8,20480]{1,0:T(8,128)(2,1)S(1)}, u32[]{:S(2)}, u32[]{:S(2)}) %collective-permute-start.4) | collective-permute-done | bytes 327712 | tf_op jit(solution)/shard_map/L_zp/ppermute | solution.py:288
  20.7 6.4 %collective-permute-done.5 = bf16[8,20480]{1,0:T(8,128)(2,1)S(1)} collective-permute-done((bf16[8,20480]{1,0:T(8,128)(2,1)}, bf16[8,20480]{1,0:T(8,128)(2,1)S(1)}, u32[]{:S(2)}, u32[]{:S(2)}) %collective-permute-start.5) | collective-permute-done | bytes 327712 | tf_op jit(solution)/shard_map/L_zn/ppermute | solution.py:288
  28.0 1.9 %collective-permute-start.12 = (bf16[16,20480]{1,0:T(8,128)(2,1)S(1)}, bf16[16,20480]{1,0:T(8,128)(2,1)S(1)}, u32[]{:S(2)}, u32[]{:S(2)}) collective-permute-start(bf16[16,20480]{1,0:T(8,128)(2,1)S(1)} %pad_maximum_fusion.refs_4_), channel_id=1, source_target_pairs={{0,192},{64,0},{128,64},{192,128},{1,193},{65,1},{129,65},{193,129... | collective-permute-start | bytes 1966088 | tf_op jit(solution)/shard_map/L_tn/ppermute | solution.py:288
  30.0 2.4 %collective-permute-start.10 = (bf16[8,10240]{1,0:T(8,128)(2,1)S(1)}, bf16[8,10240]{1,0:T(8,128)(2,1)S(1)}, u32[]{:S(2)}, u32[]{:S(2)}) collective-permute-start(bf16[8,10240]{1,0:T(8,128)(2,1)S(1)} %slice.27), channel_id=1, source_target_pairs={{0,48},{16,0},{32,16},{48,32},{1,49},{17,1},{33,17},{49,33},{2,50}... | collective-permute-start | bytes 491528 | tf_op jit(solution)/shard_map/L_zr/ppermute | solution.py:288
  33.1 3.4 %collective-permute-done.10 = bf16[8,10240]{1,0:T(8,128)(2,1)S(1)} collective-permute-done((bf16[8,10240]{1,0:T(8,128)(2,1)S(1)}, bf16[8,10240]{1,0:T(8,128)(2,1)S(1)}, u32[]{:S(2)}, u32[]{:S(2)}) %collective-permute-start.10) | collective-permute-done | bytes 163872 | tf_op jit(solution)/shard_map/L_zr/ppermute | solution.py:288
  36.4 2.3 %collective-permute-done.9 = bf16[8,10240]{1,0:T(8,128)(2,1)S(1)} collective-permute-done((bf16[8,10240]{1,0:T(8,128)(2,1)S(1)}, bf16[8,10240]{1,0:T(8,128)(2,1)S(1)}, u32[]{:S(2)}, u32[]{:S(2)}) %collective-permute-start.9) | collective-permute-done | bytes 163872 | tf_op jit(solution)/shard_map/L_zl/ppermute | solution.py:288
  38.7 2.5 %collective-permute-start.15 = (bf16[8,20480]{1,0:T(8,128)(2,1)S(1)}, bf16[8,20480]{1,0:T(8,128)(2,1)}, u32[]{:S(2)}, u32[]{:S(2)}) collective-permute-start(bf16[8,20480]{1,0:T(8,128)(2,1)S(1)} %pad_maximum_fusion.1.refs_3_), channel_id=1, source_target_pairs={{0,16},{16,32},{32,48},{48,0},{1,17},{17,33},{33,49},{49,1},{2,18}... | collective-permute-start | bytes 983048 | tf_op jit(solution)/shard_map/L_wp/ppermute | solution.py:288
  42.3 1.4 collective-permute-done.11.refs_5_
  45.5 1.8 collective-permute-start.14
  47.5 9.3 %collective-permute-done.15.refs_7_ = bf16[8,20480]{1,0:T(8,128)(2,1)} collective-permute-done((bf16[8,20480]{1,0:T(8,128)(2,1)S(1)}, bf16[8,20480]{1,0:T(8,128)(2,1)}, u32[]{:S(2)}, u32[]{:S(2)}) %collective-permute-start.15) | collective-permute-done | bytes 327712 | tf_op jit(solution)/shard_map/L_wp/ppermute | solution.py:288
  59.0 2.7 %collective-permute-start.18 = (bf16[8,10240]{1,0:T(8,128)(2,1)S(1)}, bf16[8,10240]{1,0:T(8,128)(2,1)S(1)}, u32[]{:S(2)}, u32[]{:S(2)}) collective-permute-start(bf16[8,10240]{1,0:T(8,128)(2,1)S(1)} %slice.29), channel_id=1, source_target_pairs={{0,192},{64,0},{128,64},{192,128},{1,193},{65,1},{129,65},{193,129... | collective-permute-start | bytes 491528 | tf_op jit(solution)/shard_map/L_fh/ppermute | solution.py:288
  61.8 3.6 %collective-permute-start = (s32[4,6]{1,0:T(4,128)S(1)}, s32[4,6]{1,0:T(4,128)S(1)}, u32[]{:S(2)}, u32[]{:S(2)}) collective-permute-start(s32[4,6]{1,0:T(4,128)S(1)} %pad_add_fusion.tab_ref), channel_id=1, source_target_pairs={{0,8},{8,0},{1,9},{9,1},{2,10},{10,2},{3,11},{11,3},{4,12},{12,4},... | collective-permute-start | bytes 296 | tf_op jit(solution)/shard_map/L_swap/ppermute | solution.py:300
  66.9 9.9 %forward_first.1 = (bf16[8,2,128,128]{3,2,1,0:T(8,128)(2,1)}, bf16[4,8,128,256]{3,2,1,0:T(8,128)(2,1)}, bf16[4,8,128,256]{3,2,1,0:T(8,128)(2,1)}) custom-call(s32[4]{0:T(128)S(1)} %pad_add_fusion.1.pos_ref, s32[128,8]{1,0:T(8,128)S(1)} %copy.16.cols_ref, s32[4,6]{1,0:T(4,128)S(1)} %pad_add_fusion.tab_ref, s32[4,6]{1,0:T(4,128)S(1)} %collective-permute-done.sib_tab_ref, ...), custom_call_target="tpu_custom_call" | custom-call | flops 2147483648 | bytes 16777216 | tf_op jit(solution)/shard_map/forward_first/pallas_call | solution.py:119
  76.8 4.2 %all-to-all-start = ((bf16[8,2,128,128]{3,2,1,0:T(8,128)(2,1)}), bf16[8,2,128,128]{3,2,1,0:T(8,128)(2,1)S(1)}, u32[]{:S(2)}, u32[]{:S(2)}) async-start(bf16[8,2,128,128]{3,2,1,0:T(8,128)(2,1)} %get-tuple-element.72), calls=%async_computation | async-start | bytes 1048576 | tf_op jit(solution)/shard_map/all_to_all | solution.py:341
  81.1 2.3 %collective-permute-start.19 = (f32[2,128]{1,0:T(2,128)S(1)}, f32[2,128]{1,0:T(2,128)S(1)}, u32[]{:S(2)}, u32[]{:S(2)}) collective-permute-start(f32[2,128]{1,0:T(2,128)S(1)} %get-tuple-element.110), channel_id=1, source_target_pairs={{0,8},{8,0},{1,9},{9,1},{2,10},{10,2},{3,11},{11,3},{4,12},{12,4},... | collective-permute-start | bytes 3080 | tf_op jit(solution)/shard_map/L_swap/ppermute | solution.py:300
  84.2 4.0 %all-to-all-done = bf16[8,2,128,128]{3,2,1,0:T(8,128)(2,1)S(1)} async-done(((bf16[8,2,128,128]{3,2,1,0:T(8,128)(2,1)}), bf16[8,2,128,128]{3,2,1,0:T(8,128)(2,1)S(1)}, u32[]{:S(2)}, u32[]{:S(2)}) %all-to-all-start) | async-done | bytes 524320 | tf_op jit(solution)/shard_map/all_to_all | solution.py:341
  88.3 6.4 %collective-permute-start.20 = (bf16[2,128,128]{2,1,0:T(8,128)(2,1)S(1)}, bf16[2,128,128]{2,1,0:T(8,128)(2,1)S(1)}, u32[]{:S(2)}, u32[]{:S(2)}) collective-permute-start(bf16[2,128,128]{2,1,0:T(8,128)(2,1)S(1)} %tanh_convert_fusion.1), channel_id=1, source_target_pairs={{0,32},{16,48},{32,0},{48,16},{1,33},{17,49},{33,1},{49,17},{2,34}... | collective-permute-start | bytes 196616 | tf_op jit(solution)/shard_map/L_far/ppermute | solution.py:288
  95.1 1.9 collective-permute-start.22
  97.1 2.0 %collective-permute-done.21 = bf16[2,128,128]{2,1,0:T(8,128)(2,1)S(1)} collective-permute-done((bf16[2,128,128]{2,1,0:T(8,128)(2,1)S(1)}, bf16[2,128,128]{2,1,0:T(8,128)(2,1)S(1)}, u32[]{:S(2)}, u32[]{:S(2)}) %collective-permute-start.21) | collective-permute-done | bytes 65568 | tf_op jit(solution)/shard_map/L_one/ppermute | solution.py:288
  99.1 2.4 %collective-permute-done.22 = bf16[2,128,128]{2,1,0:T(8,128)(2,1)S(1)} collective-permute-done((bf16[2,128,128]{2,1,0:T(8,128)(2,1)S(1)}, bf16[2,128,128]{2,1,0:T(8,128)(2,1)S(1)}, u32[]{:S(2)}, u32[]{:S(2)}) %collective-permute-start.22) | collective-permute-done | bytes 65568 | tf_op jit(solution)/shard_map/L_three/ppermute | solution.py:288
  103.2 5.3 %collective-permute-done.23.refs_2_ = bf16[4,2,128,128]{3,2,1,0:T(8,128)(2,1)S(1)} collective-permute-done((bf16[4,2,128,128]{3,2,1,0:T(8,128)(2,1)S(1)}, bf16[4,2,128,128]{3,2,1,0:T(8,128)(2,1)S(1)}, u32[]{:S(2)}, u32[]{:S(2)}) %collective-permute-start.23) | collective-permute-done | bytes 262176 | tf_op jit(solution)/shard_map/L_far/ppermute | solution.py:288
  109.3 1.9 collective-permute-done.25.refs_3_
  111.2 5.1 %forward_second.1 = (bf16[8,2,128,128]{3,2,1,0:T(8,128)(2,1)}, bf16[4,4,128,256]{3,2,1,0:T(8,128)(2,1)}, bf16[4,4,128,256]{3,2,1,0:T(8,128)(2,1)}) custom-call(s32[4]{0:T(128)S(1)} %pad_add_fusion.1.pos_ref, s32[4,6]{1,0:T(4,128)S(1)} %pad_add_fusion.tab_ref, s32[4,6]{1,0:T(4,128)S(1)} %collective-permute-done.sib_tab_ref, ...), custom_call_target="tpu_custom_call" | custom-call | flops 1073741824 | bytes 8388608 | tf_op jit(solution)/shard_map/forward_second/pallas_call | solution.py:174
  116.3 6.0 %all-to-all-start.1 = ((bf16[8,2,128,128]{3,2,1,0:T(8,128)(2,1)}), bf16[8,2,128,128]{3,2,1,0:T(8,128)(2,1)S(1)}, u32[]{:S(2)}, u32[]{:S(2)}) async-start(bf16[8,2,128,128]{3,2,1,0:T(8,128)(2,1)} %get-tuple-element.79), calls=%async_computation.1 | async-start | bytes 1048576 | tf_op jit(solution)/shard_map/all_to_all | solution.py:341
  122.4 5.8 %collective-permute-start.1 = (bf16[16,8,128]{2,1,0:T(8,128)(2,1)S(1)}, bf16[16,8,128]{2,1,0:T(8,128)(2,1)S(1)}, u32[]{:S(2)}, u32[]{:S(2)}) collective-permute-start(bf16[16,8,128]{2,1,0:T(8,128)(2,1)S(1)} %get-tuple-element.106), channel_id=1, source_target_pairs={{0,8},{8,0},{1,9},{9,1},{2,10},{10,2},{3,11},{11,3},{4,12},{12,4},... | collective-permute-start | bytes 98312 | tf_op jit(solution)/shard_map/L_swap/ppermute | solution.py:300
  128.2 1.3 all-to-all-done.1
  130.6 4.8 %all-to-all-start.2 = ((bf16[8,2,128,128]{3,2,1,0:T(8,128)(2,1)}), bf16[8,2,128,128]{3,2,1,0:T(8,128)(2,1)S(1)}, u32[]{:S(2)}, u32[]{:S(2)}) async-start(bf16[8,2,128,128]{3,2,1,0:T(8,128)(2,1)} %broadcast_in_dim.4), calls=%async_computation.2 | async-start | bytes 1048576 | tf_op jit(solution)/shard_map/all_to_all | solution.py:337
  135.3 5.6 %collective-permute-start.36 = (bf16[4,8,128,256]{3,2,1,0:T(8,128)(2,1)}, bf16[4,8,128,256]{3,2,1,0:T(8,128)(2,1)}, u32[]{:S(2)}, u32[]{:S(2)}) collective-permute-start(bf16[4,8,128,256]{3,2,1,0:T(8,128)(2,1)} %get-tuple-element.98), channel_id=1, source_target_pairs={{0,8},{8,0},{1,9},{9,1},{2,10},{10,2},{3,11},{11,3},{4,12},{12,4},... | collective-permute-start | bytes 6291464 | tf_op jit(solution)/shard_map/L_swap/ppermute | solution.py:300
  140.9 1.6 all-to-all-done.2.d_ref.refs_0_
  142.4 4.4 %adjoint_second.1 = (bf16[4,2,128,128]{3,2,1,0:T(8,128)(2,1)S(1)}, bf16[4,2,128,128]{3,2,1,0:T(8,128)(2,1)S(1)}, bf16[4,2,128,128]{3,2,1,0:T(8,128)(2,1)S(1)}, bf16[4,2,128,128]{3,2,1,0:T(8,128)(2,1)S(1)}) custom-call(s32[4]{0:T(128)S(1)} %pad_add_fusion.1.pos_ref, s32[4,6]{1,0:T(4,128)S(1)} %pad_add_fusion.tab_ref, ...), custom_call_target="tpu_custom_call" | custom-call | flops 1073741824 | bytes 8388608 | tf_op jit(solution)/shard_map/adjoint_second/pallas_call | solution.py:215
  146.9 2.3 %collective-permute-start.27 = (bf16[4,2,128,128]{3,2,1,0:T(8,128)(2,1)S(1)}, bf16[4,2,128,128]{3,2,1,0:T(8,128)(2,1)S(1)}, u32[]{:S(2)}, u32[]{:S(2)}) collective-permute-start(bf16[4,2,128,128]{3,2,1,0:T(8,128)(2,1)S(1)} %get-tuple-element.81), channel_id=1, source_target_pairs={{0,128},{64,192},{128,0},{192,64},{1,129},{65,193},{129,1},{193,65... | collective-permute-start | bytes 786440 | tf_op jit(solution)/shard_map/L_far/ppermute | solution.py:288
  149.4 2.4 %collective-permute-start.29 = (bf16[4,2,128,128]{3,2,1,0:T(8,128)(2,1)S(1)}, bf16[4,2,128,128]{3,2,1,0:T(8,128)(2,1)S(1)}, u32[]{:S(2)}, u32[]{:S(2)}) collective-permute-start(bf16[4,2,128,128]{3,2,1,0:T(8,128)(2,1)S(1)} %get-tuple-element.83), channel_id=1, source_target_pairs={{0,192},{64,0},{128,64},{192,128},{1,193},{65,1},{129,65},{193,129... | collective-permute-start | bytes 786440 | tf_op jit(solution)/shard_map/L_three/ppermute | solution.py:288
  151.8 1.9 collective-permute-done.27.refs_2_
  153.8 2.7 %collective-permute-done.28.refs_1_ = bf16[4,2,128,128]{3,2,1,0:T(8,128)(2,1)S(1)} collective-permute-done((bf16[4,2,128,128]{3,2,1,0:T(8,128)(2,1)S(1)}, bf16[4,2,128,128]{3,2,1,0:T(8,128)(2,1)S(1)}, u32[]{:S(2)}, u32[]{:S(2)}) %collective-permute-start.28) | collective-permute-done | bytes 262176 | tf_op jit(solution)/shard_map/L_one/ppermute | solution.py:288
  156.6 3.0 %collective-permute-start.30 = (bf16[2,128,128]{2,1,0:T(8,128)(2,1)S(1)}, bf16[2,128,128]{2,1,0:T(8,128)(2,1)S(1)}, u32[]{:S(2)}, u32[]{:S(2)}) collective-permute-start(bf16[2,128,128]{2,1,0:T(8,128)(2,1)S(1)} %get-tuple-element.88), channel_id=1, source_target_pairs={{0,32},{16,48},{32,0},{48,16},{1,33},{17,49},{33,1},{49,17},{2,34}... | collective-permute-start | bytes 196616 | tf_op jit(solution)/shard_map/L_far/ppermute | solution.py:288
  159.6 3.6 %collective-permute-start.32 = (bf16[2,128,128]{2,1,0:T(8,128)(2,1)S(1)}, bf16[2,128,128]{2,1,0:T(8,128)(2,1)S(1)}, u32[]{:S(2)}, u32[]{:S(2)}) collective-permute-start(bf16[2,128,128]{2,1,0:T(8,128)(2,1)S(1)} %get-tuple-element.90), channel_id=1, source_target_pairs={{0,48},{16,0},{32,16},{48,32},{1,49},{17,1},{33,17},{49,33},{2,50}... | collective-permute-start | bytes 196616 | tf_op jit(solution)/shard_map/L_three/ppermute | solution.py:288
  163.2 8.6 %collective-permute-start.33 = (bf16[4,4,128,256]{3,2,1,0:T(8,128)(2,1)}, bf16[4,4,128,256]{3,2,1,0:T(8,128)(2,1)S(1)}, u32[]{:S(2)}, u32[]{:S(2)}) collective-permute-start(bf16[4,4,128,256]{3,2,1,0:T(8,128)(2,1)} %get-tuple-element.95), channel_id=1, source_target_pairs={{0,8},{8,0},{1,9},{9,1},{2,10},{10,2},{3,11},{11,3},{4,12},{12,4},... | collective-permute-start | bytes 3145736 | tf_op jit(solution)/shard_map/L_swap/ppermute | solution.py:300
  172.8 6.1 %all-to-all-start.3 = ((bf16[16,128,128]{2,1,0:T(8,128)(2,1)}), bf16[16,128,128]{2,1,0:T(8,128)(2,1)S(1)}, u32[]{:S(2)}, u32[]{:S(2)}) async-start(bf16[16,128,128]{2,1,0:T(8,128)(2,1)} %bitcast.18), calls=%async_computation.3 | async-start | bytes 1048576 | tf_op jit(solution)/shard_map/all_to_all | solution.py:402
  182.2 1.2 copy-done.2
  184.6 2.8 %grad_second.1 = bf16[4,4,256,256]{3,2,1,0:T(8,128)(2,1)} custom-call(s32[4]{0:T(128)S(1)} %pad_add_fusion.1.pos_ref, s32[4,6]{1,0:T(4,128)S(1)} %pad_add_fusion.tab_ref, bf16[4,4,128,256]{3,2,1,0:T(8,128)(2,1)S(1)} %copy-done.2, bf16[4,4,128,256]{3,2,1,0:T(8,128)(2,1)S(1)} %copy-done.4, bf16[8,2,128,128]{3,2,1,0:T(8,128)(2,1)S(1)} %all-to-all-done.2.d_ref.refs_0_, ...), custom_call_target="tpu_custom_call" | custom-call | flops 536870912 | bytes 4194304 | tf_op jit(solution)/shard_map/grad_second/pallas_call | solution.py:268
  187.4 2.0 %all-to-all-done.3 = bf16[16,128,128]{2,1,0:T(8,128)(2,1)S(1)} async-done(((bf16[16,128,128]{2,1,0:T(8,128)(2,1)}), bf16[16,128,128]{2,1,0:T(8,128)(2,1)S(1)}, u32[]{:S(2)}, u32[]{:S(2)}) %all-to-all-start.3) | async-done | bytes 524320 | tf_op jit(solution)/shard_map/all_to_all | solution.py:402
  189.4 4.5 %grad_first.1 = bf16[4,8,256,256]{3,2,1,0:T(8,128)(2,1)} custom-call(s32[4]{0:T(128)S(1)} %pad_add_fusion.1.pos_ref, s32[4,6]{1,0:T(4,128)S(1)} %pad_add_fusion.tab_ref, bf16[4,8,128,256]{3,2,1,0:T(8,128)(2,1)S(1)} %copy-done.1, bf16[4,8,128,256]{3,2,1,0:T(8,128)(2,1)} %collective-permute-done.36.po_ref, bf16[2,8,128,128]{3,2,1,0:T(8,128)(2,1)S(1)} %bitcast.40), custom_call_target="tpu_custom_call" | custom-call | flops 1073741824 | bytes 8388608 | tf_op jit(solution)/shard_map/grad_first/pallas_call | solution.py:268
  (110 shorter events, 19.4 us)
Async XLA Ops:
  0.6 46.7 %copy-start.16 = (s32[4,1]{0,1:T(1,128)S(1)}, s32[4,1]{0,1:T(1,128)}, u32[]{:S(2)}) copy-start(s32[4,1]{0,1:T(1,128)} %param.12) | copy-start | bytes 52
  0.6 46.8 %copy-start.17 = (s32[4,1]{0,1:T(1,128)S(1)}, s32[4,1]{0,1:T(1,128)}, u32[]{:S(2)}) copy-start(s32[4,1]{0,1:T(1,128)} %param.16) | copy-start | bytes 52
  0.7 26.5 %collective-permute-start.8 = (bf16[4,8,256,256]{3,2,1,0:T(8,128)(2,1)}, bf16[4,8,256,256]{3,2,1,0:T(8,128)(2,1)}, u32[]{:S(2)}, u32[]{:S(2)}) collective-permute-start(bf16[4,8,256,256]{3,2,1,0:T(8,128)(2,1)} %refs_14_.1), channel_id=1, source_target_pairs={{0,8},{8,0},{1,9},{9,1},{2,10},{10,2},{3,11},{11,3},{4,12},{12,4},... | collective-permute-start | bytes 12582920 | tf_op jit(solution)/shard_map/L_w1/ppermute | solution.py:300
  4.0 10.7 %collective-permute-start.2 = (bf16[8,20480]{1,0:T(8,128)(2,1)}, bf16[8,20480]{1,0:T(8,128)(2,1)S(1)}, u32[]{:S(2)}, u32[]{:S(2)}) collective-permute-start(bf16[8,20480]{1,0:T(8,128)(2,1)} %refs_0_.1), channel_id=1, source_target_pairs={{0,64},{64,128},{128,192},{192,0},{1,65},{65,129},{129,193},{193,1... | collective-permute-start | bytes 983048 | tf_op jit(solution)/shard_map/L_xp/ppermute | solution.py:288
  4.0 10.7 %collective-permute-start.3 = (bf16[8,20480]{1,0:T(8,128)(2,1)}, bf16[8,20480]{1,0:T(8,128)(2,1)S(1)}, u32[]{:S(2)}, u32[]{:S(2)}) collective-permute-start(bf16[8,20480]{1,0:T(8,128)(2,1)} %refs_0_.1), channel_id=1, source_target_pairs={{0,192},{64,0},{128,64},{192,128},{1,193},{65,1},{129,65},{193,129... | collective-permute-start | bytes 983048 | tf_op jit(solution)/shard_map/L_xn/ppermute | solution.py:288
  6.7 14.0 %collective-permute-start.4 = (bf16[8,20480]{1,0:T(8,128)(2,1)}, bf16[8,20480]{1,0:T(8,128)(2,1)S(1)}, u32[]{:S(2)}, u32[]{:S(2)}) collective-permute-start(bf16[8,20480]{1,0:T(8,128)(2,1)} %refs_0_.1), channel_id=1, source_target_pairs={{0,16},{16,32},{32,48},{48,0},{1,17},{17,33},{33,49},{49,1},{2,18}... | collective-permute-start | bytes 983048 | tf_op jit(solution)/shard_map/L_zp/ppermute | solution.py:288
  7.9 19.2 %collective-permute-start.5 = (bf16[8,20480]{1,0:T(8,128)(2,1)}, bf16[8,20480]{1,0:T(8,128)(2,1)S(1)}, u32[]{:S(2)}, u32[]{:S(2)}) collective-permute-start(bf16[8,20480]{1,0:T(8,128)(2,1)} %refs_0_.1), channel_id=1, source_target_pairs={{0,48},{16,0},{32,16},{48,32},{1,49},{17,1},{33,17},{49,33},{2,50}... | collective-permute-start | bytes 983048 | tf_op jit(solution)/shard_map/L_zn/ppermute | solution.py:288
  14.7 43.1 %copy-start.8 = (bf16[8,20480]{1,0:T(8,128)(2,1)}, bf16[8,20480]{1,0:T(8,128)(2,1)S(1)}, u32[]{:S(2)}) copy-start(bf16[8,20480]{1,0:T(8,128)(2,1)S(1)} %collective-permute-done.2.refs_1_) | copy-start | bytes 983044
  14.7 47.0 %copy-start.15 = (s32[4,4]{1,0:T(4,128)S(1)}, s32[4,4]{1,0:T(4,128)}, u32[]{:S(2)}) copy-start(s32[4,4]{1,0:T(4,128)} %param.15) | copy-start | bytes 196
  14.7 50.7 %copy-start = (bf16[4,4,256,256]{3,2,1,0:T(8,128)(2,1)S(1)}, bf16[4,4,256,256]{3,2,1,0:T(8,128)(2,1)}, u32[]{:S(2)}) copy-start(bf16[4,4,256,256]{3,2,1,0:T(8,128)(2,1)} %own_ref.1) | copy-start | bytes 6291460
  14.7 50.9 %copy-start.14 = (s32[128,8]{0,1:T(8,128)S(1)}, s32[128,8]{0,1:T(8,128)}, u32[]{:S(2)}) copy-start(s32[128,8]{0,1:T(8,128)} %param.11) | copy-start | bytes 12292
  14.7 12.4 %collective-permute-start.6 = (bf16[8,10240]{1,0:T(8,128)(2,1)S(1)}, bf16[8,10240]{1,0:T(8,128)(2,1)S(1)}, u32[]{:S(2)}, u32[]{:S(2)}) collective-permute-start(bf16[8,10240]{1,0:T(8,128)(2,1)S(1)} %slice.24), channel_id=1, source_target_pairs={{0,64},{64,128},{128,192},{192,0},{1,65},{65,129},{129,193},{193,1... | collective-permute-start | bytes 491528 | tf_op jit(solution)/shard_map/L_xl/ppermute | solution.py:288
  14.8 12.3 %collective-permute-start.7 = (bf16[8,10240]{1,0:T(8,128)(2,1)S(1)}, bf16[8,10240]{1,0:T(8,128)(2,1)S(1)}, u32[]{:S(2)}, u32[]{:S(2)}) collective-permute-start(bf16[8,10240]{1,0:T(8,128)(2,1)S(1)} %slice.25), channel_id=1, source_target_pairs={{0,192},{64,0},{128,64},{192,128},{1,193},{65,1},{129,65},{193,129... | collective-permute-start | bytes 491528 | tf_op jit(solution)/shard_map/L_xh/ppermute | solution.py:288
  27.2 16.6 %collective-permute-start.11 = (bf16[16,20480]{1,0:T(8,128)(2,1)S(1)}, bf16[16,20480]{1,0:T(8,128)(2,1)S(1)}, u32[]{:S(2)}, u32[]{:S(2)}) collective-permute-start(bf16[16,20480]{1,0:T(8,128)(2,1)S(1)} %pad_maximum_fusion.refs_4_), channel_id=1, source_target_pairs={{0,64},{64,128},{128,192},{192,0},{1,65},{65,129},{129,193},{193,1... | collective-permute-start | bytes 1966088 | tf_op jit(solution)/shard_map/L_tp/ppermute | solution.py:288
  28.0 15.8 %collective-permute-start.12 = (bf16[16,20480]{1,0:T(8,128)(2,1)S(1)}, bf16[16,20480]{1,0:T(8,128)(2,1)S(1)}, u32[]{:S(2)}, u32[]{:S(2)}) collective-permute-start(bf16[16,20480]{1,0:T(8,128)(2,1)S(1)} %pad_maximum_fusion.refs_4_), channel_id=1, source_target_pairs={{0,192},{64,0},{128,64},{192,128},{1,193},{65,1},{129,65},{193,129... | collective-permute-start | bytes 1966088 | tf_op jit(solution)/shard_map/L_tn/ppermute | solution.py:288
  30.0 6.5 %collective-permute-start.10 = (bf16[8,10240]{1,0:T(8,128)(2,1)S(1)}, bf16[8,10240]{1,0:T(8,128)(2,1)S(1)}, u32[]{:S(2)}, u32[]{:S(2)}) collective-permute-start(bf16[8,10240]{1,0:T(8,128)(2,1)S(1)} %slice.27), channel_id=1, source_target_pairs={{0,48},{16,0},{32,16},{48,32},{1,49},{17,1},{33,17},{49,33},{2,50}... | collective-permute-start | bytes 491528 | tf_op jit(solution)/shard_map/L_zr/ppermute | solution.py:288
  32.3 6.4 %collective-permute-start.9 = (bf16[8,10240]{1,0:T(8,128)(2,1)S(1)}, bf16[8,10240]{1,0:T(8,128)(2,1)S(1)}, u32[]{:S(2)}, u32[]{:S(2)}) collective-permute-start(bf16[8,10240]{1,0:T(8,128)(2,1)S(1)} %slice.26), channel_id=1, source_target_pairs={{0,16},{16,32},{32,48},{48,0},{1,17},{17,33},{33,49},{49,1},{2,18}... | collective-permute-start | bytes 491528 | tf_op jit(solution)/shard_map/L_zl/ppermute | solution.py:288
  33.1 33.2 %copy-start.6 = (bf16[8,20480]{1,0:T(8,128)(2,1)}, bf16[8,20480]{1,0:T(8,128)(2,1)S(1)}, u32[]{:S(2)}) copy-start(bf16[8,20480]{1,0:T(8,128)(2,1)S(1)} %pad_maximum_fusion.1.refs_3_) | copy-start | bytes 983044
  38.7 18.1 %collective-permute-start.15 = (bf16[8,20480]{1,0:T(8,128)(2,1)S(1)}, bf16[8,20480]{1,0:T(8,128)(2,1)}, u32[]{:S(2)}, u32[]{:S(2)}) collective-permute-start(bf16[8,20480]{1,0:T(8,128)(2,1)S(1)} %pad_maximum_fusion.1.refs_3_), channel_id=1, source_target_pairs={{0,16},{16,32},{32,48},{48,0},{1,17},{17,33},{33,49},{49,1},{2,18}... | collective-permute-start | bytes 983048 | tf_op jit(solution)/shard_map/L_wp/ppermute | solution.py:288
  41.2 15.6 %collective-permute-start.16 = (bf16[8,20480]{1,0:T(8,128)(2,1)S(1)}, bf16[8,20480]{1,0:T(8,128)(2,1)}, u32[]{:S(2)}, u32[]{:S(2)}) collective-permute-start(bf16[8,20480]{1,0:T(8,128)(2,1)S(1)} %pad_maximum_fusion.1.refs_3_), channel_id=1, source_target_pairs={{0,48},{16,0},{32,16},{48,32},{1,49},{17,1},{33,17},{49,33},{2,50}... | collective-permute-start | bytes 983048 | tf_op jit(solution)/shard_map/L_wn/ppermute | solution.py:288
  44.6 12.2 %collective-permute-start.13 = (bf16[8,20480]{1,0:T(8,128)(2,1)S(1)}, bf16[8,20480]{1,0:T(8,128)(2,1)}, u32[]{:S(2)}, u32[]{:S(2)}) collective-permute-start(bf16[8,20480]{1,0:T(8,128)(2,1)S(1)} %pad_maximum_fusion.2.refs_9_), channel_id=1, source_target_pairs={{0,64},{64,128},{128,192},{192,0},{1,65},{65,129},{129,193},{193,1... | collective-permute-start | bytes 983048 | tf_op jit(solution)/shard_map/L_fp/ppermute | solution.py:288
  45.5 11.3 %collective-permute-start.14 = (bf16[8,20480]{1,0:T(8,128)(2,1)S(1)}, bf16[8,20480]{1,0:T(8,128)(2,1)}, u32[]{:S(2)}, u32[]{:S(2)}) collective-permute-start(bf16[8,20480]{1,0:T(8,128)(2,1)S(1)} %pad_maximum_fusion.2.refs_9_), channel_id=1, source_target_pairs={{0,192},{64,0},{128,64},{192,128},{1,193},{65,1},{129,65},{193,129... | collective-permute-start | bytes 983048 | tf_op jit(solution)/shard_map/L_fn/ppermute | solution.py:288
  57.8 8.5 %collective-permute-start.17 = (bf16[8,10240]{1,0:T(8,128)(2,1)S(1)}, bf16[8,10240]{1,0:T(8,128)(2,1)}, u32[]{:S(2)}, u32[]{:S(2)}) collective-permute-start(bf16[8,10240]{1,0:T(8,128)(2,1)S(1)} %slice.28), channel_id=1, source_target_pairs={{0,64},{64,128},{128,192},{192,0},{1,65},{65,129},{129,193},{193,1... | collective-permute-start | bytes 491528 | tf_op jit(solution)/shard_map/L_fl/ppermute | solution.py:288
  59.0 7.3 %collective-permute-start.18 = (bf16[8,10240]{1,0:T(8,128)(2,1)S(1)}, bf16[8,10240]{1,0:T(8,128)(2,1)S(1)}, u32[]{:S(2)}, u32[]{:S(2)}) collective-permute-start(bf16[8,10240]{1,0:T(8,128)(2,1)S(1)} %slice.29), channel_id=1, source_target_pairs={{0,192},{64,0},{128,64},{192,128},{1,193},{65,1},{129,65},{193,129... | collective-permute-start | bytes 491528 | tf_op jit(solution)/shard_map/L_fh/ppermute | solution.py:288
  61.8 4.5 %collective-permute-start = (s32[4,6]{1,0:T(4,128)S(1)}, s32[4,6]{1,0:T(4,128)S(1)}, u32[]{:S(2)}, u32[]{:S(2)}) collective-permute-start(s32[4,6]{1,0:T(4,128)S(1)} %pad_add_fusion.tab_ref), channel_id=1, source_target_pairs={{0,8},{8,0},{1,9},{9,1},{2,10},{10,2},{3,11},{11,3},{4,12},{12,4},... | collective-permute-start | bytes 296 | tf_op jit(solution)/shard_map/L_swap/ppermute | solution.py:300
  65.4 45.8 %collective-permute-start.26 = (bf16[4,4,256,256]{3,2,1,0:T(8,128)(2,1)S(1)}, bf16[4,4,256,256]{3,2,1,0:T(8,128)(2,1)}, u32[]{:S(2)}, u32[]{:S(2)}) collective-permute-start(bf16[4,4,256,256]{3,2,1,0:T(8,128)(2,1)S(1)} %copy-done), channel_id=1, source_target_pairs={{0,8},{8,0},{1,9},{9,1},{2,10},{10,2},{3,11},{11,3},{4,12},{12,4},... | collective-permute-start | bytes 6291464 | tf_op jit(solution)/shard_map/L_swap/ppermute | solution.py:300
  76.8 11.4 %all-to-all-start = ((bf16[8,2,128,128]{3,2,1,0:T(8,128)(2,1)}), bf16[8,2,128,128]{3,2,1,0:T(8,128)(2,1)S(1)}, u32[]{:S(2)}, u32[]{:S(2)}) async-start(bf16[8,2,128,128]{3,2,1,0:T(8,128)(2,1)} %get-tuple-element.72), calls=%async_computation | async-start | bytes 1048576 | tf_op jit(solution)/shard_map/all_to_all | solution.py:341
  81.1 3.1 %collective-permute-start.19 = (f32[2,128]{1,0:T(2,128)S(1)}, f32[2,128]{1,0:T(2,128)S(1)}, u32[]{:S(2)}, u32[]{:S(2)}) collective-permute-start(f32[2,128]{1,0:T(2,128)S(1)} %get-tuple-element.110), channel_id=1, source_target_pairs={{0,8},{8,0},{1,9},{9,1},{2,10},{10,2},{3,11},{11,3},{4,12},{12,4},... | collective-permute-start | bytes 3080 | tf_op jit(solution)/shard_map/L_swap/ppermute | solution.py:300
  88.3 8.8 %collective-permute-start.20 = (bf16[2,128,128]{2,1,0:T(8,128)(2,1)S(1)}, bf16[2,128,128]{2,1,0:T(8,128)(2,1)S(1)}, u32[]{:S(2)}, u32[]{:S(2)}) collective-permute-start(bf16[2,128,128]{2,1,0:T(8,128)(2,1)S(1)} %tanh_convert_fusion.1), channel_id=1, source_target_pairs={{0,32},{16,48},{32,0},{48,16},{1,33},{17,49},{33,1},{49,17},{2,34}... | collective-permute-start | bytes 196616 | tf_op jit(solution)/shard_map/L_far/ppermute | solution.py:288
  94.7 4.4 %collective-permute-start.21 = (bf16[2,128,128]{2,1,0:T(8,128)(2,1)S(1)}, bf16[2,128,128]{2,1,0:T(8,128)(2,1)S(1)}, u32[]{:S(2)}, u32[]{:S(2)}) collective-permute-start(bf16[2,128,128]{2,1,0:T(8,128)(2,1)S(1)} %tanh_convert_fusion.1), channel_id=1, source_target_pairs={{0,48},{16,0},{32,16},{48,32},{1,49},{17,1},{33,17},{49,33},{2,50}... | collective-permute-start | bytes 196616 | tf_op jit(solution)/shard_map/L_one/ppermute | solution.py:288
  95.1 6.4 %collective-permute-start.22 = (bf16[2,128,128]{2,1,0:T(8,128)(2,1)S(1)}, bf16[2,128,128]{2,1,0:T(8,128)(2,1)S(1)}, u32[]{:S(2)}, u32[]{:S(2)}) collective-permute-start(bf16[2,128,128]{2,1,0:T(8,128)(2,1)S(1)} %tanh_convert_fusion.1), channel_id=1, source_target_pairs={{0,16},{16,32},{32,48},{48,0},{1,17},{17,33},{33,49},{49,1},{2,18}... | collective-permute-start | bytes 196616 | tf_op jit(solution)/shard_map/L_three/ppermute | solution.py:288
  101.6 6.9 %collective-permute-start.23 = (bf16[4,2,128,128]{3,2,1,0:T(8,128)(2,1)S(1)}, bf16[4,2,128,128]{3,2,1,0:T(8,128)(2,1)S(1)}, u32[]{:S(2)}, u32[]{:S(2)}) collective-permute-start(bf16[4,2,128,128]{3,2,1,0:T(8,128)(2,1)S(1)} %pad_maximum_fusion.3.refs_0_), channel_id=1, source_target_pairs={{0,128},{64,192},{128,0},{192,64},{1,129},{65,193},{129,1},{193,65... | collective-permute-start | bytes 786440 | tf_op jit(solution)/shard_map/L_far/ppermute | solution.py:288
  101.7 7.7 %collective-permute-start.24 = (bf16[4,2,128,128]{3,2,1,0:T(8,128)(2,1)S(1)}, bf16[4,2,128,128]{3,2,1,0:T(8,128)(2,1)S(1)}, u32[]{:S(2)}, u32[]{:S(2)}) collective-permute-start(bf16[4,2,128,128]{3,2,1,0:T(8,128)(2,1)S(1)} %pad_maximum_fusion.3.refs_0_), channel_id=1, source_target_pairs={{0,192},{64,0},{128,64},{192,128},{1,193},{65,1},{129,65},{193,129... | collective-permute-start | bytes 786440 | tf_op jit(solution)/shard_map/L_one/ppermute | solution.py:288
  102.2 8.9 %collective-permute-start.25 = (bf16[4,2,128,128]{3,2,1,0:T(8,128)(2,1)S(1)}, bf16[4,2,128,128]{3,2,1,0:T(8,128)(2,1)S(1)}, u32[]{:S(2)}, u32[]{:S(2)}) collective-permute-start(bf16[4,2,128,128]{3,2,1,0:T(8,128)(2,1)S(1)} %pad_maximum_fusion.3.refs_0_), channel_id=1, source_target_pairs={{0,64},{64,128},{128,192},{192,0},{1,65},{65,129},{129,193},{193,1... | collective-permute-start | bytes 786440 | tf_op jit(solution)/shard_map/L_three/ppermute | solution.py:288
  116.3 13.2 %all-to-all-start.1 = ((bf16[8,2,128,128]{3,2,1,0:T(8,128)(2,1)}), bf16[8,2,128,128]{3,2,1,0:T(8,128)(2,1)S(1)}, u32[]{:S(2)}, u32[]{:S(2)}) async-start(bf16[8,2,128,128]{3,2,1,0:T(8,128)(2,1)} %get-tuple-element.79), calls=%async_computation.1 | async-start | bytes 1048576 | tf_op jit(solution)/shard_map/all_to_all | solution.py:341
  122.4 7.2 %collective-permute-start.1 = (bf16[16,8,128]{2,1,0:T(8,128)(2,1)S(1)}, bf16[16,8,128]{2,1,0:T(8,128)(2,1)S(1)}, u32[]{:S(2)}, u32[]{:S(2)}) collective-permute-start(bf16[16,8,128]{2,1,0:T(8,128)(2,1)S(1)} %get-tuple-element.106), channel_id=1, source_target_pairs={{0,8},{8,0},{1,9},{9,1},{2,10},{10,2},{3,11},{11,3},{4,12},{12,4},... | collective-permute-start | bytes 98312 | tf_op jit(solution)/shard_map/L_swap/ppermute | solution.py:300
  130.6 11.9 %all-to-all-start.2 = ((bf16[8,2,128,128]{3,2,1,0:T(8,128)(2,1)}), bf16[8,2,128,128]{3,2,1,0:T(8,128)(2,1)S(1)}, u32[]{:S(2)}, u32[]{:S(2)}) async-start(bf16[8,2,128,128]{3,2,1,0:T(8,128)(2,1)} %broadcast_in_dim.4), calls=%async_computation.2 | async-start | bytes 1048576 | tf_op jit(solution)/shard_map/all_to_all | solution.py:337
  135.3 54.1 %collective-permute-start.36 = (bf16[4,8,128,256]{3,2,1,0:T(8,128)(2,1)}, bf16[4,8,128,256]{3,2,1,0:T(8,128)(2,1)}, u32[]{:S(2)}, u32[]{:S(2)}) collective-permute-start(bf16[4,8,128,256]{3,2,1,0:T(8,128)(2,1)} %get-tuple-element.98), channel_id=1, source_target_pairs={{0,8},{8,0},{1,9},{9,1},{2,10},{10,2},{3,11},{11,3},{4,12},{12,4},... | collective-permute-start | bytes 6291464 | tf_op jit(solution)/shard_map/L_swap/ppermute | solution.py:300
  146.9 6.9 %collective-permute-start.27 = (bf16[4,2,128,128]{3,2,1,0:T(8,128)(2,1)S(1)}, bf16[4,2,128,128]{3,2,1,0:T(8,128)(2,1)S(1)}, u32[]{:S(2)}, u32[]{:S(2)}) collective-permute-start(bf16[4,2,128,128]{3,2,1,0:T(8,128)(2,1)S(1)} %get-tuple-element.81), channel_id=1, source_target_pairs={{0,128},{64,192},{128,0},{192,64},{1,129},{65,193},{129,1},{193,65... | collective-permute-start | bytes 786440 | tf_op jit(solution)/shard_map/L_far/ppermute | solution.py:288
  149.1 7.3 %collective-permute-start.28 = (bf16[4,2,128,128]{3,2,1,0:T(8,128)(2,1)S(1)}, bf16[4,2,128,128]{3,2,1,0:T(8,128)(2,1)S(1)}, u32[]{:S(2)}, u32[]{:S(2)}) collective-permute-start(bf16[4,2,128,128]{3,2,1,0:T(8,128)(2,1)S(1)} %get-tuple-element.82), channel_id=1, source_target_pairs={{0,64},{64,128},{128,192},{192,0},{1,65},{65,129},{129,193},{193,1... | collective-permute-start | bytes 786440 | tf_op jit(solution)/shard_map/L_one/ppermute | solution.py:288
  149.4 7.0 %collective-permute-start.29 = (bf16[4,2,128,128]{3,2,1,0:T(8,128)(2,1)S(1)}, bf16[4,2,128,128]{3,2,1,0:T(8,128)(2,1)S(1)}, u32[]{:S(2)}, u32[]{:S(2)}) collective-permute-start(bf16[4,2,128,128]{3,2,1,0:T(8,128)(2,1)S(1)} %get-tuple-element.83), channel_id=1, source_target_pairs={{0,192},{64,0},{128,64},{192,128},{1,193},{65,1},{129,65},{193,129... | collective-permute-start | bytes 786440 | tf_op jit(solution)/shard_map/L_three/ppermute | solution.py:288
  156.6 15.1 %collective-permute-start.30 = (bf16[2,128,128]{2,1,0:T(8,128)(2,1)S(1)}, bf16[2,128,128]{2,1,0:T(8,128)(2,1)S(1)}, u32[]{:S(2)}, u32[]{:S(2)}) collective-permute-start(bf16[2,128,128]{2,1,0:T(8,128)(2,1)S(1)} %get-tuple-element.88), channel_id=1, source_target_pairs={{0,32},{16,48},{32,0},{48,16},{1,33},{17,49},{33,1},{49,17},{2,34}... | collective-permute-start | bytes 196616 | tf_op jit(solution)/shard_map/L_far/ppermute | solution.py:288
  159.6 12.1 %collective-permute-start.31 = (bf16[2,128,128]{2,1,0:T(8,128)(2,1)S(1)}, bf16[2,128,128]{2,1,0:T(8,128)(2,1)S(1)}, u32[]{:S(2)}, u32[]{:S(2)}) collective-permute-start(bf16[2,128,128]{2,1,0:T(8,128)(2,1)S(1)} %get-tuple-element.89), channel_id=1, source_target_pairs={{0,16},{16,32},{32,48},{48,0},{1,17},{17,33},{33,49},{49,1},{2,18}... | collective-permute-start | bytes 196616 | tf_op jit(solution)/shard_map/L_one/ppermute | solution.py:288
  159.6 12.1 %collective-permute-start.32 = (bf16[2,128,128]{2,1,0:T(8,128)(2,1)S(1)}, bf16[2,128,128]{2,1,0:T(8,128)(2,1)S(1)}, u32[]{:S(2)}, u32[]{:S(2)}) collective-permute-start(bf16[2,128,128]{2,1,0:T(8,128)(2,1)S(1)} %get-tuple-element.90), channel_id=1, source_target_pairs={{0,48},{16,0},{32,16},{48,32},{1,49},{17,1},{33,17},{49,33},{2,50}... | collective-permute-start | bytes 196616 | tf_op jit(solution)/shard_map/L_three/ppermute | solution.py:288
  163.2 18.0 %collective-permute-start.33 = (bf16[4,4,128,256]{3,2,1,0:T(8,128)(2,1)}, bf16[4,4,128,256]{3,2,1,0:T(8,128)(2,1)S(1)}, u32[]{:S(2)}, u32[]{:S(2)}) collective-permute-start(bf16[4,4,128,256]{3,2,1,0:T(8,128)(2,1)} %get-tuple-element.95), channel_id=1, source_target_pairs={{0,8},{8,0},{1,9},{9,1},{2,10},{10,2},{3,11},{11,3},{4,12},{12,4},... | collective-permute-start | bytes 3145736 | tf_op jit(solution)/shard_map/L_swap/ppermute | solution.py:300
  172.8 16.6 %all-to-all-start.3 = ((bf16[16,128,128]{2,1,0:T(8,128)(2,1)}), bf16[16,128,128]{2,1,0:T(8,128)(2,1)S(1)}, u32[]{:S(2)}, u32[]{:S(2)}) async-start(bf16[16,128,128]{2,1,0:T(8,128)(2,1)} %bitcast.18), calls=%async_computation.3 | async-start | bytes 1048576 | tf_op jit(solution)/shard_map/all_to_all | solution.py:402
  178.9 3.3 %collective-permute-start.34 = (bf16[8,128,128]{2,1,0:T(8,128)(2,1)S(1)}, bf16[8,128,128]{2,1,0:T(8,128)(2,1)S(1)}, u32[]{:S(2)}, u32[]{:S(2)}) collective-permute-start(bf16[8,128,128]{2,1,0:T(8,128)(2,1)S(1)} %dynamic-slice_bitcast_fusion), channel_id=1, source_target_pairs={{0,8},{8,0},{1,9},{9,1},{2,10},{10,2},{3,11},{11,3},{4,12},{12,4},... | collective-permute-start | bytes 786440 | tf_op jit(solution)/shard_map/L_swap/ppermute | solution.py:300
  179.1 1.4 collective-permute-start.35
  (13 other events, 104.5 us)
